TPU v7x, 128 devices: a whole 4x4x4 slice. The times are simulated.
128 devices in a mesh: strike: 8 (over z, x_hi), normal: 16 (over x_lo, y, core).
Axes of the slice: x: 4 (x_hi: 2, x_lo: 2; x = x_hi * 2 + x_lo), y: 4, z: 4, core: 2. Of those that a mesh axis runs over, the one named last changes fastest.
Arguments:
- velocity: float32 [3, 256, 256, 384], P(None, 'strike', 'normal'), may hold values from -6 to 6
- stress: float32 [6, 256, 256, 384], P(None, 'strike', 'normal'), may hold values from -6 to 6
- modulus: float32 [256, 256, 384], P('strike', 'normal'), may hold values from 0.5 to 2
- buoyancy: float32 [256, 256, 384], P('strike', 'normal'), may hold values from 0.5 to 1.5
- fault_state: float32 [256, 384], P(('strike', 'normal')), may hold values from -0.3 to 0.3
- fault_mask: int32 [256, 384], P(('strike', 'normal')), may hold values 0 or 1
- region_ids: int32 [256, 384], P(('strike', 'normal')), may hold values from 0 to 3
- friction_table: float32 [4, 4], replicated, may hold values from 0.2 to 2
Outputs:
- velocity_out: float32 [3, 256, 256, 384], P(None, 'strike', 'normal')
- stress_out: float32 [6, 256, 256, 384], P(None, 'strike', 'normal')
- slip_rate: float32 [256, 384], P(('strike', 'normal'))
- state_out: float32 [256, 384], P(('strike', 'normal'))
Inputs may be any that keep to these rules, and one draw needn't show every extreme that they name: `region_ids`: region ids index the columns of friction_table.
All inputs are finite; a program needn't handle non-finite values. No bound on the sum of `fault_mask` on one device may be relied on, other than what follows from the above.
Results may differ from a plain program's by a relative error of at most 0.0003.
Values sent between devices are 32-bit elements; how exact they have to be, the bound alone decides.
No kernel may reach another device: no remote copies, remote signals or barrier semaphores. Data moves between devices by JAX's collectives and lax.ppermute only.
A program may use at most 128 MiB of HBM per device.

v0:
```python
import functools

import jax
import jax.numpy as jnp
from jax import lax
from jax.experimental import pallas as pl
from jax.experimental.pallas import tpu as pltpu
from jax.sharding import PartitionSpec as P

STEPS = 2
NEWTON = 4

C1 = 9.0 / 8.0
C2 = -1.0 / 24.0
DT = 0.1
ETA = 1.0

F32 = jnp.float32
SXX, SYY, SZZ, SXY, SXZ, SYZ = range(6)


def shift_up(x, axis):
    count = lax.axis_size(axis)
    return lax.ppermute(x, axis, [(i, (i + 1) % count) for i in range(count)])


def shift_down(x, axis):
    count = lax.axis_size(axis)
    return lax.ppermute(x, axis, [((i + 1) % count, i) for i in range(count)])


def swap_odd(x, axis):
    count = lax.axis_size(axis)
    pairs = []
    for i in range(1, count, 2):
        j = (i + 1) % count
        pairs += [(i, j), (j, i)]
    return lax.ppermute(x, axis, pairs)


VMEM = pl.BlockSpec(memory_space=pltpu.VMEM)
SMEM = pl.BlockSpec(memory_space=pltpu.SMEM)
ANY = pl.BlockSpec(memory_space=pl.ANY)


def call(body, ins, outs, args, scratch=(), aliases=None, cost=None, name=None):
    shapes = [
        pltpu.VMEM(shape, F32) if spec is VMEM else jax.ShapeDtypeStruct(shape, F32)
        for shape, spec in outs
    ]
    return pl.pallas_call(
        body,
        out_shape=shapes,
        in_specs=ins,
        out_specs=[spec for _, spec in outs],
        scratch_shapes=list(scratch),
        input_output_aliases=aliases or {},
        compiler_params=pltpu.CompilerParams(vmem_limit_bytes=16 << 20),
        cost_estimate=cost,
        name=name,
    )(*args)


LANES = 128


def masked(shape, offset, value):
    i = lax.broadcasted_iota(jnp.int32, shape, 0)
    n = shape[0]
    keep = i >= -offset if offset < 0 else i < n - offset
    return jnp.where(keep, jnp.asarray(value, F32), 0.0)


class Coefs:
    def __init__(self, ny):
        self.ny = ny
        self.t = {}
        for offset, value in ((-1, C1), (1, C2), (-2, C2), (1, C1), (2, C2), (-1, C2)):
            self.t[offset, value] = masked((ny, LANES), offset, value)
        self.lane = lax.broadcasted_iota(jnp.int32, (ny, LANES), 1)

    def y(self, f, offset, value):
        return pltpu.roll(f, (-offset) % self.ny, 0) * self.t[offset, value]

    def y_minus(self, fs):
        return [
            C1 * f - self.y(f, -1, C1) + self.y(f, 1, C2) - self.y(f, -2, C2) for f in fs
        ]

    def y_plus(self, fs):
        return [
            self.y(f, 1, C1) - C1 * f + self.y(f, 2, C2) - self.y(f, -1, C2) for f in fs
        ]

    def z(self, fs, offset):
        rolls = [pltpu.roll(f, (-offset) % LANES, 1) for f in fs]
        keep = self.lane < LANES - offset if offset > 0 else self.lane >= -offset
        out = []
        for k, r in enumerate(rolls):
            j = k + 1 if offset > 0 else k - 1
            out.append(jnp.where(keep, r, rolls[j] if 0 <= j < len(fs) else 0.0))
        return out

    def z_minus(self, fs):
        return [
            C1 * (f - b) + C2 * (c - d)
            for f, b, c, d in zip(fs, self.z(fs, -1), self.z(fs, 1), self.z(fs, -2))
        ]

    def z_plus(self, fs):
        return [
            C1 * (b - f) + C2 * (c - d)
            for f, b, c, d in zip(fs, self.z(fs, 1), self.z(fs, 2), self.z(fs, -1))
        ]


def add(*lists):
    return [functools.reduce(lambda p, q: p + q, parts) for parts in zip(*lists)]


def tile(k):
    return slice(k * LANES, (k + 1) * LANES)


def to_tiles(source, target, sems):
    return [
        pltpu.make_async_copy(source.at[:, tile(k)], target.at[k], sems.at[k])
        for k in range(target.shape[0])
    ]


def from_tiles(source, target, sems):
    return [
        pltpu.make_async_copy(source.at[k], target.at[:, tile(k)], sems.at[k])
        for k in range(source.shape[0])
    ]


def run(copies):
    for c in copies:
        c.start()
    for c in copies:
        c.wait()


MINUS = ((0, C1), (-1, -C1), (1, C2), (-2, -C2))
PLUS = ((1, C1), (0, -C1), (2, C2), (-1, -C2))


def slab(ref, comp, at):
    if comp is None:
        return [ref[k, at, :] for k in range(ref.shape[0])]
    return [ref[comp, k, at, :] for k in range(ref.shape[1])]


def x_terms(ref, comp, x, nx, ny, static, pairs):
    total = None
    for offset, coef in pairs:
        if static and not 0 <= x + offset < nx:
            continue
        start = (x + offset) * ny
        if not static:
            start = pl.multiple_of(start, 8)
        term = [coef * f for f in slab(ref, comp, pl.ds(start, ny))]
        total = term if total is None else add(total, term)
    return total


def over_x(nx, body):
    for x in (0, 1, nx - 2, nx - 1):
        body(x, True)

    def step(x, carry):
        body(x, False)
        return carry

    lax.fori_loop(2, nx - 2, step, 0)


def velocity_body(nx, ny, first, s, v_in, b_in, v, *refs):
    tiles = s.shape[1]
    if first:
        bd, sem = refs
        copies = to_tiles(b_in, bd, sem.at[3])
        for c in range(3):
            copies += to_tiles(v_in.at[c], v.at[c], sem.at[c])
        run(copies)
    cf = Coefs(ny)

    def body(x, static):
        start = x * ny if static else pl.multiple_of(x * ny, 8)
        at = pl.ds(start, ny)
        xt = functools.partial(x_terms, s, x=x, nx=nx, ny=ny, static=static)
        sxy, sxz, syz = slab(s, SXY, at), slab(s, SXZ, at), slab(s, SYZ, at)
        a = (
            add(xt(SXX, pairs=PLUS), cf.y_minus(sxy), cf.z_minus(sxz)),
            add(xt(SXY, pairs=MINUS), cf.y_plus(slab(s, SYY, at)), cf.z_minus(syz)),
            add(xt(SXZ, pairs=MINUS), cf.y_minus(syz), cf.z_plus(slab(s, SZZ, at))),
        )
        src = v if first else v_in
        for k in range(tiles):
            if first:
                w = DT * bd[k, at, :]
                bd[k, at, :] = w
            else:
                w = b_in[k, at, :]
            for c in range(3):
                v[c, k, at, :] = src[c, k, at, :] + w * a[c][k]

    over_x(nx, body)


def stress_body(nx, ny, first, last, *refs):
    refs = list(refs)
    v, s_in, m_in = refs[:3]
    refs = refs[3:]
    s = refs.pop(0)
    md = refs.pop(0) if first else m_in
    v_out = refs.pop(0) if last else None
    sem = refs.pop(0) if first or last else None
    tiles = s.shape[1]
    if first:
        run(to_tiles(m_in, md, sem.at[0]))
    if last:
        out = []
        for c in range(3):
            out += from_tiles(v.at[c], v_out.at[c], sem.at[c])
        for c in out:
            c.start()
    cf = Coefs(ny)

    def body(x, static):
        start = x * ny if static else pl.multiple_of(x * ny, 8)
        at = pl.ds(start, ny)
        xt = functools.partial(x_terms, v, x=x, nx=nx, ny=ny, static=static)
        vx, vy, vz = slab(v, 0, at), slab(v, 1, at), slab(v, 2, at)
        exx = xt(0, pairs=MINUS)
        eyy = cf.y_minus(vy)
        ezz = cf.z_minus(vz)
        exy = add(xt(1, pairs=PLUS), cf.y_plus(vx))
        exz = add(xt(2, pairs=PLUS), cf.z_plus(vx))
        eyz = add(cf.z_plus(vy), cf.y_plus(vz))
        tr = add(exx, eyy, ezz)
        for k in range(tiles):
            w = md[k, at, :]
            if first:
                w = DT * w
                md[k, at, :] = w
            s[SXX, k, at, :] = s_in[SXX, k, at, :] + w * (tr[k] + 2.0 * exx[k])
            s[SYY, k, at, :] = s_in[SYY, k, at, :] + w * (tr[k] + 2.0 * eyy[k])
            s[SZZ, k, at, :] = s_in[SZZ, k, at, :] + w * (tr[k] + 2.0 * ezz[k])
            s[SXY, k, at, :] = s_in[SXY, k, at, :] + w * exy[k]
            s[SXZ, k, at, :] = s_in[SXZ, k, at, :] + w * exz[k]
            s[SYZ, k, at, :] = s_in[SYZ, k, at, :] + w * eyz[k]

    over_x(nx, body)
    if last:
        for c in out:
            c.wait()


class Edges:
    def __init__(self, nx, ny):
        self.nx, self.ny = nx, ny

    def x(self, i):
        return pl.ds(i * self.ny, self.ny)

    def y(self, i):
        return pl.ds(i, self.nx, stride=self.ny)


def minus_edges(n, low, high):
    return (
        (0, -C1 * low[1] - C2 * low[0]),
        (1, -C2 * low[1]),
        (n - 1, C2 * high[0]),
    )


def plus_edges(n, low, high):
    return (
        (0, -C2 * low[0]),
        (n - 1, C1 * high[0] + C2 * high[1]),
        (n - 2, C2 * high[0]),
    )


def sides():
    out = []
    for axis in ("strike", "normal"):
        i = lax.axis_index(axis)
        last = lax.axis_size(axis) - 1
        out += [jnp.where(i > 0, 1.0, 0.0).astype(F32), jnp.where(i < last, 1.0, 0.0).astype(F32)]
    return out


def add_rows(ref, comp, w, at, factor, value):
    ref[comp, :, at, :] = ref[comp, :, at, :] + w[:, at, :] * (factor * value if factor != 1.0 else value)


def pack_stress_x(s, e, up, down):
    nx = e.nx
    for k, (c, i) in enumerate(
        ((SXX, nx - 1), (SXY, nx - 2), (SXY, nx - 1), (SXZ, nx - 2), (SXZ, nx - 1))
    ):
        up[k] = s[c, :, e.x(i), :]
    for k, (c, i) in enumerate(((SXX, 0), (SXX, 1), (SXY, 0), (SXZ, 0))):
        down[k] = s[c, :, e.x(i), :]


def pack_stress_y(s, e, up, down):
    ny = e.ny
    for k, (c, i) in enumerate(
        ((SYY, ny - 1), (SXY, ny - 2), (SXY, ny - 1), (SYZ, ny - 2), (SYZ, ny - 1))
    ):
        up[k] = s[c, :, e.y(i), :]
    for k, (c, i) in enumerate(((SYY, 0), (SYY, 1), (SXY, 0), (SYZ, 0))):
        down[k] = s[c, :, e.y(i), :]


def load_body(nx, ny, stress, s, xu, xd, yu, yd, sem):
    e = Edges(nx, ny)
    order = (SXX, SXY, SXZ, SYY, SYZ, SZZ)
    copies = {c: to_tiles(stress.at[c], s.at[c], sem.at[c]) for c in order}

    def wait(*comps):
        for c in comps:
            for copy in copies[c]:
                copy.wait()

    for c in order:
        for copy in copies[c]:
            copy.start()
    wait(SXX, SXY, SXZ)
    pack_stress_x(s, e, xu, xd)
    wait(SYY, SYZ)
    pack_stress_y(s, e, yu, yd)
    wait(SZZ)


def velocity_edges_body(nx, ny, v_in, w, s, xl, xh, yl, yh, v, yu, yd, mine, traction):
    del v_in
    e = Edges(nx, ny)
    fxl, fxh, fyl, fyh = sides()
    a = [xl[k] * fxl for k in range(5)]
    b = [xh[k] * fxh for k in range(4)]
    for comp, terms in (
        (0, plus_edges(nx, a[0:1], b[0:2])),
        (1, minus_edges(nx, a[1:3], b[2:3])),
        (2, minus_edges(nx, a[3:5], b[3:4])),
    ):
        for i, value in terms:
            add_rows(v, comp, w, e.x(i), 1.0, value)
    a = [yl[k] * fyl for k in range(5)]
    b = [yh[k] * fyh for k in range(4)]
    for comp, terms in (
        (1, plus_edges(ny, a[0:1], b[0:2])),
        (0, minus_edges(ny, a[1:3], b[2:3])),
        (2, minus_edges(ny, a[3:5], b[3:4])),
    ):
        for i, value in terms:
            add_rows(v, comp, w, e.y(i), 1.0, value)
    odd = lax.rem(lax.axis_index("normal"), 2) == 1
    mine[...] = jnp.where(odd, v[0, :, e.y(ny - 1), :], v[0, :, e.y(0), :])
    traction[...] = jnp.where(odd, s[SXY, :, e.y(ny - 1), :], yl[2])
    for k, (c, i) in enumerate(((1, ny - 2), (1, ny - 1), (0, ny - 1), (2, ny - 1))):
        yu[k] = v[c, :, e.y(i), :]
    for k, (c, i) in enumerate(((1, 0), (0, 0), (0, 1), (2, 0), (2, 1))):
        yd[k] = v[c, :, e.y(i), :]


def inverse_sinh(values):
    magnitude = jnp.abs(values)
    root = jnp.sqrt(1.0 + magnitude * magnitude)
    result = jnp.log1p(magnitude + magnitude * magnitude / (1.0 + root))
    return jnp.where(values < 0.0, -result, result)


def fault_body(nx, ny, last, *refs):
    mine, other, traction, par, st_in, v_in, v, xu, xd, st, minus_o, plus_o, trac_o = refs[:13]
    del v_in
    e = Edges(nx, ny)
    position = lax.axis_index("normal")
    members = lax.axis_size("normal")
    odd = lax.rem(position, 2) == 1
    on_minus = position == members // 2 - 1
    on_plus = position == members // 2
    m, o = mine[...], other[...]
    minus = jnp.where(odd, m, o)
    plus = jnp.where(odd, o, m)
    mask, a, b, inv_len, sigma = (par[k] for k in range(5))
    state = st_in[...]
    locked = traction[...] + ETA * (plus - minus)
    c = 0.5 * jnp.exp(state / a)
    weight = sigma * a
    rate = jnp.zeros_like(locked)
    for _ in range(NEWTON):
        arg = c * rate
        residue = locked - ETA * rate - weight * inverse_sinh(arg)
        slope = ETA + weight * c / jnp.sqrt(1.0 + arg * arg)
        rate = rate + residue / slope
    rate = rate * mask
    state = state + DT * inv_len * (jnp.exp(-state / b) - jnp.abs(rate))
    st[...] = state
    trac_o[...] = locked - ETA * rate
    middle = 0.5 * (minus + plus)
    minus = middle - 0.5 * rate
    plus = middle + 0.5 * rate
    minus_o[...] = minus
    plus_o[...] = plus
    v[0, :, e.y(ny - 1), :] = jnp.where(on_minus, minus, v[0, :, e.y(ny - 1), :])
    v[0, :, e.y(0), :] = jnp.where(on_plus, plus, v[0, :, e.y(0), :])
    for k, (comp, i) in enumerate(((0, nx - 2), (0, nx - 1), (1, nx - 1), (2, nx - 1))):
        xu[k] = v[comp, :, e.x(i), :]
    for k, (comp, i) in enumerate(((0, 0), (1, 0), (1, 1), (2, 0), (2, 1))):
        xd[k] = v[comp, :, e.x(i), :]
    if last:
        back, tmp = refs[13:]
        tmp[0] = rate
        tmp[1] = state
        count = nx // back.shape[0]
        for k in range(back.shape[0]):
            for q in range(2):
                for z in range(tmp.shape[1]):
                    back[k, q * count : (q + 1) * count, tile(z)] = tmp[
                        q, z, k * count : (k + 1) * count, :
                    ]
        pad = back.shape[1] - 2 * count
        if pad:
            back[:, 2 * count :, :] = jnp.zeros((back.shape[0], pad, back.shape[2]), F32)


def stress_edges_body(nx, ny, last, rows, *refs):
    s_in, w, xl, xh, yl, yh, minus, plus, traction = refs[:9]
    del s_in
    e = Edges(nx, ny)
    fxl, fxh, fyl, fyh = sides()
    position = lax.axis_index("normal")
    members = lax.axis_size("normal")
    on_minus = position == members // 2 - 1
    on_plus = position == members // 2
    if last:
        recv, s, out, slip, state, sem = refs[9:]
    else:
        s, xu, xd, yu, yd = refs[9:]
    a = [xl[k] * fxl for k in range(4)]
    b = [xh[k] * fxh for k in range(5)]
    for i, value in minus_edges(nx, a[0:2], b[0:1]):
        add_rows(s, SXX, w, e.x(i), 3.0, value)
        add_rows(s, SYY, w, e.x(i), 1.0, value)
        add_rows(s, SZZ, w, e.x(i), 1.0, value)
    for i, value in plus_edges(nx, a[2:3], b[1:3]):
        add_rows(s, SXY, w, e.x(i), 1.0, value)
    for i, value in plus_edges(nx, a[3:4], b[3:5]):
        add_rows(s, SXZ, w, e.x(i), 1.0, value)
    a = [yl[k] * fyl for k in range(4)]
    b = [yh[k] * fyh for k in range(5)]
    a[2] = jnp.where(on_plus, minus[...], a[2])
    b[1] = jnp.where(on_minus, plus[...], b[1])
    for i, value in minus_edges(ny, a[0:2], b[0:1]):
        add_rows(s, SXX, w, e.y(i), 1.0, value)
        add_rows(s, SYY, w, e.y(i), 3.0, value)
        add_rows(s, SZZ, w, e.y(i), 1.0, value)
    for i, value in plus_edges(ny, a[2:3], b[1:3]):
        add_rows(s, SXY, w, e.y(i), 1.0, value)
    for i, value in plus_edges(ny, a[3:4], b[3:5]):
        add_rows(s, SYZ, w, e.y(i), 1.0, value)
    s[SXY, :, e.y(ny - 1), :] = jnp.where(on_minus, traction[...], s[SXY, :, e.y(ny - 1), :])
    if last:
        copies = []
        for c in range(6):
            copies += from_tiles(s.at[c], out.at[c], sem.at[c])
        for copy in copies:
            copy.start()
        slip[...] = recv[members // 2, 0:rows, :]
        state[...] = recv[members // 2, rows : 2 * rows, :]
        for copy in copies:
            copy.wait()
    else:
        pack_stress_x(s, e, xu, xd)
        pack_stress_y(s, e, yu, yd)


def own_body(state, mask, ids, out):
    rows = state.shape[0]
    block = jnp.concatenate((state[...], mask[...].astype(F32), ids[...].astype(F32)), 0)
    pad = out.shape[1] - 3 * rows
    if pad:
        block = jnp.concatenate((block, jnp.zeros((pad, block.shape[1]), F32)), 0)
    for k in range(out.shape[0]):
        out[k] = block


def parameters_body(rows, recv, table, st, par, tmp):
    for k in range(recv.shape[0]):
        at = slice(k * rows, (k + 1) * rows)
        for z in range(st.shape[0]):
            st[z, at, :] = recv[k, 0:rows, tile(z)]
            par[0, z, at, :] = recv[k, rows : 2 * rows, tile(z)]
            tmp[z, at, :] = recv[k, 2 * rows : 3 * rows, tile(z)]
    ids = tmp[...]
    for j in range(4):
        p = jnp.zeros_like(ids)
        for r in range(table.shape[1]):
            p = jnp.where(ids == float(r), table[j, r], p)
        par[1 + j] = p


def local(velocity, stress, modulus, buoyancy, fault_state, fault_mask, region_ids, friction_table):
    members = lax.axis_size("normal")
    _, nx, ny, nz = velocity.shape
    rows = fault_state.shape[0]
    flat, nt = nx * ny, nz // LANES
    vel_in = velocity.reshape(3, flat, nz)
    str_in = stress.reshape(6, flat, nz)
    mod_in = modulus.reshape(flat, nz)
    buo_in = buoyancy.reshape(flat, nz)
    dma = lambda n: pltpu.SemaphoreType.DMA((n, nt))
    stage_cost = pl.CostEstimate(flops=4_000_000_000, bytes_accessed=16_000_000, transcendentals=0)
    side_cost = pl.CostEstimate(flops=1_000_000, bytes_accessed=1_000_000, transcendentals=0)

    depth = -(-3 * rows // 8) * 8
    (spread,) = call(
        own_body, [VMEM] * 3, [((members, depth, nz), VMEM)],
        (fault_state, fault_mask, region_ids), cost=side_cost, name="own",
    )
    s, xu, xd, yu, yd = call(
        functools.partial(load_body, nx, ny), [ANY],
        [((6, nt, flat, LANES), VMEM), ((5, nt, ny, LANES), VMEM), ((4, nt, ny, LANES), VMEM),
         ((5, nt, nx, LANES), VMEM), ((4, nt, nx, LANES), VMEM)],
        (str_in,), scratch=[dma(6)], cost=side_cost, name="load",
    )
    recv = lax.all_to_all(spread, "normal", 0, 0, tiled=True)
    state, par = call(
        functools.partial(parameters_body, rows), [VMEM, SMEM],
        [((nt, nx, LANES), VMEM), ((5, nt, nx, LANES), VMEM)], (recv, friction_table),
        scratch=[pltpu.VMEM((nt, nx, LANES), F32)], cost=side_cost, name="parameters",
    )
    v = w = m = None
    for step in range(STEPS):
        first, last = step == 0, step == STEPS - 1
        xl, xh = shift_up(xu, "strike"), shift_down(xd, "strike")
        yl, yh = shift_up(yu, "normal"), shift_down(yd, "normal")
        if first:
            v, w = call(
                functools.partial(velocity_body, nx, ny, True), [VMEM, ANY, ANY],
                [((3, nt, flat, LANES), VMEM), ((nt, flat, LANES), VMEM)], (s, vel_in, buo_in),
                scratch=[dma(4)], cost=stage_cost, name="velocity_first",
            )
        else:
            (v,) = call(
                functools.partial(velocity_body, nx, ny, False),
                [VMEM] * 3, [((3, nt, flat, LANES), VMEM)], (s, v, w),
                aliases={1: 0}, cost=stage_cost, name="velocity",
            )
        v, yu, yd, mine, traction = call(
            functools.partial(velocity_edges_body, nx, ny), [VMEM] * 7,
            [((3, nt, flat, LANES), VMEM), ((4, nt, nx, LANES), VMEM), ((5, nt, nx, LANES), VMEM),
             ((nt, nx, LANES), VMEM), ((nt, nx, LANES), VMEM)],
            (v, w, s, xl, xh, yl, yh), aliases={0: 0}, cost=side_cost, name="velocity_edges",
        )
        other = swap_odd(mine, "normal")
        yl, yh = shift_up(yu, "normal"), shift_down(yd, "normal")
        back_depth = -(-2 * rows // 8) * 8
        outs = [((3, nt, flat, LANES), VMEM), ((4, nt, ny, LANES), VMEM), ((5, nt, ny, LANES), VMEM)]
        outs += [((nt, nx, LANES), VMEM)] * 4
        if last:
            outs.append(((members, back_depth, nz), VMEM))
        got = call(
            functools.partial(fault_body, nx, ny, last), [VMEM] * 6, outs,
            (mine, other, traction, par, state, v),
            scratch=[pltpu.VMEM((2, nt, nx, LANES), F32)] if last else [],
            aliases={5: 0}, cost=side_cost, name="fault",
        )
        v, xu, xd, state, minus, plus, trac_new = got[:7]
        xl, xh = shift_up(xu, "strike"), shift_down(xd, "strike")
        outs = [((6, nt, flat, LANES), VMEM)]
        if first:
            outs.append(((nt, flat, LANES), VMEM))
        if last:
            outs.append(((3, flat, nz), ANY))
        got_s = call(
            functools.partial(stress_body, nx, ny, first, last),
            [VMEM, VMEM, ANY if first else VMEM], outs, (v, s, mod_in if first else m),
            scratch=[dma(3)] if first or last else [], aliases={1: 0}, cost=stage_cost,
            name="stress",
        )
        s = got_s[0]
        if first:
            m = got_s[1]
        edge_in = (s, m, xl, xh, yl, yh, minus, plus, trac_new)
        if last:
            v_out = got_s[-1]
            recv = lax.all_to_all(got[7], "normal", 0, 0, tiled=True)
            _, s_out, slip, state_out = call(
                functools.partial(stress_edges_body, nx, ny, True, rows), [VMEM] * 10,
                [((6, nt, flat, LANES), VMEM), ((6, flat, nz), ANY), ((rows, nz), ANY_VMEM), ((rows, nz), ANY_VMEM)],
                edge_in + (recv,), scratch=[dma(6)], aliases={0: 0}, cost=side_cost,
                name="stress_edges_last",
            )
        else:
            s, xu, xd, yu, yd = call(
                functools.partial(stress_edges_body, nx, ny, False, rows), [VMEM] * 9,
                [((6, nt, flat, LANES), VMEM), ((5, nt, ny, LANES), VMEM), ((4, nt, ny, LANES), VMEM),
                 ((5, nt, nx, LANES), VMEM), ((4, nt, nx, LANES), VMEM)],
                edge_in, aliases={0: 0}, cost=side_cost, name="stress_edges",
            )
    return (
        v_out.reshape(3, nx, ny, nz),
        s_out.reshape(6, nx, ny, nz),
        slip,
        state_out,
    )


ANY_VMEM = pl.BlockSpec(memory_space=pltpu.MemorySpace.VMEM)


def solution(mesh):
    block = P(None, "strike", "normal", None)
    part = P("strike", "normal", None)
    row = P(("strike", "normal"), None)
    return jax.shard_map(
        local,
        mesh=mesh,
        in_specs=(block, block, part, part, row, row, row, P()),
        out_specs=(block, block, row, row),
        check_vma=False,
    )
```

profile of v0, /device:TPU:1, one launch (start us, length us, event | category | flops | bytes accessed | tf_op | source)
XLA Modules:
  0.0 108.7 jit_solution(15344129524750097466)
XLA Ops:
  3.4 6.9 %all-to-all-start = ((f32[16,8,384]{2,1,0:T(8,128)}), f32[16,8,384]{2,1,0:T(8,128)S(1)}, u32[]{:S(2)}, u32[]{:S(2)}) async-start(f32[16,8,384]{2,1,0:T(8,128)} %own.1), calls=%async_computation | async-start | bytes 393216 | tf_op jit(solution)/shard_map/all_to_all | solution.py:534
  10.3 2.3 %copy-done.6 = f32[6,32,16,384]{3,2,1,0:T(8,128)S(1)} copy-done((f32[6,32,16,384]{3,2,1,0:T(8,128)S(1)}, f32[6,32,16,384]{3,2,1,0:T(8,128)}, u32[]{:S(2)}) %copy-start.6) | copy-done | bytes 4718616
  13.3 6.0 %collective-permute-start.1 = (f32[4,3,16,128]{3,2,1,0:T(8,128)S(1)}, f32[4,3,16,128]{3,2,1,0:T(8,128)S(1)}, u32[]{:S(2)}, u32[]{:S(2)}) collective-permute-start(f32[4,3,16,128]{3,2,1,0:T(8,128)S(1)} %get-tuple-element.53), channel_id=1, source_target_pairs={{16,0},{32,16},{48,32},{64,48},{80,64},{96,80},{112,96},{0,112},{1... | collective-permute-start | bytes 294920 | tf_op jit(solution)/shard_map/ppermute | solution.py:29
  19.7 1.5 %collective-permute-start.2 = (f32[5,3,32,128]{3,2,1,0:T(8,128)S(1)}, f32[5,3,32,128]{3,2,1,0:T(8,128)S(1)}, u32[]{:S(2)}, u32[]{:S(2)}) collective-permute-start(f32[5,3,32,128]{3,2,1,0:T(8,128)S(1)} %get-tuple-element.54), channel_id=1, source_target_pairs={{0,1},{1,2},{2,3},{3,4},{4,5},{5,6},{6,7},{7,8},{8,9},{9,10},{10,1... | collective-permute-start | bytes 737288 | tf_op jit(solution)/shard_map/ppermute | solution.py:24
  21.3 4.4 %velocity_first.1 = (f32[3,3,512,128]{3,2,1,0:T(8,128)S(1)}, f32[3,512,128]{2,1,0:T(8,128)S(1)}) custom-call(f32[6,3,512,128]{3,2,1,0:T(8,128)S(1)} %get-tuple-element.49.s.refs_1_, f32[3,512,384]{2,1,0:T(8,128)S(1)} %bitcast.7, f32[512,384]{1,0:T(8,128)S(1)} %bitcast.8), custom_call_target="tpu_custom_call" | custom-call | flops 4000000000 | bytes 16000000 | tf_op jit(solution)/shard_map/velocity_first/pallas_call | solution.py:51
  25.7 1.8 %collective-permute-done.xl = f32[5,3,16,128]{3,2,1,0:T(8,128)S(1)} collective-permute-done((f32[5,3,16,128]{3,2,1,0:T(8,128)S(1)}, f32[5,3,16,128]{3,2,1,0:T(8,128)S(1)}, u32[]{:S(2)}, u32[]{:S(2)}) %collective-permute-start) | collective-permute-done | bytes 122912 | tf_op jit(solution)/shard_map/ppermute | solution.py:24
  27.5 1.4 %velocity_edges.2 = (f32[3,3,512,128]{3,2,1,0:T(8,128)S(1)}, f32[4,3,32,128]{3,2,1,0:T(8,128)}, f32[5,3,32,128]{3,2,1,0:T(8,128)S(1)}, f32[3,32,128]{2,1,0:T(8,128)S(1)}, f32[3,32,128]{2,1,0:T(8,128)S(1)}) custom-call(f32[3,3,512,128]{3,2,1,0:T(8,128)S(1)} %get-tuple-element.50.v_in, ...), custom_call_target="tpu_custom_call", output_to_operand_aliasing={{0}: (0, {})} | custom-call | flops 1000000 | bytes 1000000 | tf_op jit(solution)/shard_map/velocity_edges/pallas_call | solution.py:51
  29.0 2.4 %collective-permute-start.4 = (f32[3,32,128]{2,1,0:T(8,128)S(1)}, f32[3,32,128]{2,1,0:T(8,128)S(1)}, u32[]{:S(2)}, u32[]{:S(2)}) collective-permute-start(f32[3,32,128]{2,1,0:T(8,128)S(1)} %get-tuple-element.56.refs_0_), channel_id=1, source_target_pairs={{1,2},{2,1},{3,4},{4,3},{5,6},{6,5},{7,8},{8,7},{9,10},{10,9},{11,... | collective-permute-start | bytes 147464 | tf_op jit(solution)/shard_map/ppermute | solution.py:38
  32.2 1.5 %collective-permute-start.8 = (f32[5,3,32,128]{3,2,1,0:T(8,128)S(1)}, f32[5,3,32,128]{3,2,1,0:T(8,128)S(1)}, u32[]{:S(2)}, u32[]{:S(2)}) collective-permute-start(f32[5,3,32,128]{3,2,1,0:T(8,128)S(1)} %get-tuple-element.67), channel_id=1, source_target_pairs={{1,0},{2,1},{3,2},{4,3},{5,4},{6,5},{7,6},{8,7},{9,8},{10,9},{11,1... | collective-permute-start | bytes 737288 | tf_op jit(solution)/shard_map/ppermute | solution.py:29
  34.9 4.8 %collective-permute-start.6 = (f32[5,3,16,128]{3,2,1,0:T(8,128)S(1)}, f32[5,3,16,128]{3,2,1,0:T(8,128)S(1)}, u32[]{:S(2)}, u32[]{:S(2)}) collective-permute-start(f32[5,3,16,128]{3,2,1,0:T(8,128)S(1)} %get-tuple-element.65), channel_id=1, source_target_pairs={{16,0},{32,16},{48,32},{64,48},{80,64},{96,80},{112,96},{0,112},{1... | collective-permute-start | bytes 368648 | tf_op jit(solution)/shard_map/ppermute | solution.py:29
  39.6 2.3 %copy-done.1 = f32[6,3,512,128]{3,2,1,0:T(8,128)S(1)} copy-done((f32[6,3,512,128]{3,2,1,0:T(8,128)S(1)}, f32[6,3,512,128]{3,2,1,0:T(8,128)}, u32[]{:S(2)}) %copy-start.1) | copy-done | bytes 4718616
  43.1 5.2 %stress.2 = (f32[6,3,512,128]{3,2,1,0:T(8,128)S(1)}, f32[3,512,128]{2,1,0:T(8,128)S(1)}) custom-call(f32[3,3,512,128]{3,2,1,0:T(8,128)S(1)} %get-tuple-element.61.refs_0_.v_in, f32[6,3,512,128]{3,2,1,0:T(8,128)S(1)} %copy-done.1, f32[512,384]{1,0:T(8,128)S(1)} %bitcast.9), custom_call_target="tpu_custom_call", output_to_operand_aliasing={{0}: (1, {})} | custom-call | flops 4000000000 | bytes 16000000 | tf_op jit(solution)/shard_map/stress/pallas_call | solution.py:51
  49.5 3.0 %collective-permute-start.10 = (f32[4,3,16,128]{3,2,1,0:T(8,128)S(1)}, f32[4,3,16,128]{3,2,1,0:T(8,128)S(1)}, u32[]{:S(2)}, u32[]{:S(2)}) collective-permute-start(f32[4,3,16,128]{3,2,1,0:T(8,128)S(1)} %get-tuple-element.73), channel_id=1, source_target_pairs={{16,0},{32,16},{48,32},{64,48},{80,64},{96,80},{112,96},{0,112},{1... | collective-permute-start | bytes 294920 | tf_op jit(solution)/shard_map/ppermute | solution.py:29
  52.5 5.4 %collective-permute-start.12 = (f32[4,3,32,128]{3,2,1,0:T(8,128)S(1)}, f32[4,3,32,128]{3,2,1,0:T(8,128)S(1)}, u32[]{:S(2)}, u32[]{:S(2)}) collective-permute-start(f32[4,3,32,128]{3,2,1,0:T(8,128)S(1)} %get-tuple-element.75), channel_id=1, source_target_pairs={{1,0},{2,1},{3,2},{4,3},{5,4},{6,5},{7,6},{8,7},{9,8},{10,9},{11,1... | collective-permute-start | bytes 589832 | tf_op jit(solution)/shard_map/ppermute | solution.py:29
  57.9 4.1 %velocity.1.v_in = f32[3,3,512,128]{3,2,1,0:T(8,128)S(1)} custom-call(f32[6,3,512,128]{3,2,1,0:T(8,128)S(1)} %get-tuple-element.71.s.refs_1_, f32[3,3,512,128]{3,2,1,0:T(8,128)S(1)} %get-tuple-element.61.refs_0_.v_in, f32[3,512,128]{2,1,0:T(8,128)S(1)} %copy-done.8), custom_call_target="tpu_custom_call", output_to_operand_aliasing={{}: (1, {})} | custom-call | flops 4000000000 | bytes 16000000 | tf_op jit(solution)/shard_map/velocity/pallas_call | solution.py:51
  62.1 1.5 %velocity_edges.3 = (f32[3,3,512,128]{3,2,1,0:T(8,128)S(1)}, f32[4,3,32,128]{3,2,1,0:T(8,128)}, f32[5,3,32,128]{3,2,1,0:T(8,128)}, f32[3,32,128]{2,1,0:T(8,128)S(1)}, f32[3,32,128]{2,1,0:T(8,128)S(1)}) custom-call(f32[3,3,512,128]{3,2,1,0:T(8,128)S(1)} %velocity.1.v_in, f32[3,512,128]{2,1,0:T(8,128)S(1)} %copy-done.8, ...), custom_call_target="tpu_custom_call", output_to_operand_aliasing={{0}: (0, {})} | custom-call | flops 1000000 | bytes 1000000 | tf_op jit(solution)/shard_map/velocity_edges/pallas_call | solution.py:51
  65.4 3.1 %collective-permute-start.17 = (f32[5,3,32,128]{3,2,1,0:T(8,128)}, f32[5,3,32,128]{3,2,1,0:T(8,128)}, u32[]{:S(2)}, u32[]{:S(2)}) collective-permute-start(f32[5,3,32,128]{3,2,1,0:T(8,128)} %get-tuple-element.86), channel_id=1, source_target_pairs={{1,0},{2,1},{3,2},{4,3},{5,4},{6,5},{7,6},{8,7},{9,8},{10,9},{11,1... | collective-permute-start | bytes 737288 | tf_op jit(solution)/shard_map/ppermute | solution.py:29
  73.4 7.9 %all-to-all-start.1 = ((f32[16,8,384]{2,1,0:T(8,128)}), f32[16,8,384]{2,1,0:T(8,128)S(1)}, u32[]{:S(2)}, u32[]{:S(2)}) async-start(f32[16,8,384]{2,1,0:T(8,128)} %copy-done.9), calls=%async_computation.1 | async-start | bytes 393216 | tf_op jit(solution)/shard_map/all_to_all | solution.py:595
  81.6 4.7 %collective-permute-start.15 = (f32[5,3,16,128]{3,2,1,0:T(8,128)}, f32[5,3,16,128]{3,2,1,0:T(8,128)S(1)}, u32[]{:S(2)}, u32[]{:S(2)}) collective-permute-start(f32[5,3,16,128]{3,2,1,0:T(8,128)} %copy-done.27), channel_id=1, source_target_pairs={{16,0},{32,16},{48,32},{64,48},{80,64},{96,80},{112,96},{0,112},{1... | collective-permute-start | bytes 368648 | tf_op jit(solution)/shard_map/ppermute | solution.py:29
  86.3 2.3 %copy-done.3 = f32[6,3,512,128]{3,2,1,0:T(8,128)S(1)} copy-done((f32[6,3,512,128]{3,2,1,0:T(8,128)S(1)}, f32[6,3,512,128]{3,2,1,0:T(8,128)}, u32[]{:S(2)}) %copy-start.3) | copy-done | bytes 4718616
  88.7 5.2 %stress.3 = (f32[6,3,512,128]{3,2,1,0:T(8,128)S(1)}, f32[3,512,384]{2,1,0:T(8,128)}) custom-call(f32[3,3,512,128]{3,2,1,0:T(8,128)S(1)} %get-tuple-element.80.refs_0_, f32[6,3,512,128]{3,2,1,0:T(8,128)S(1)} %copy-done.3, f32[3,512,128]{2,1,0:T(8,128)S(1)} %get-tuple-element.63.refs_1_.refs_2_), custom_call_target="tpu_custom_call", output_to_operand_aliasing={{0}: (1, {})} | custom-call | flops 4000000000 | bytes 16000000 | tf_op jit(solution)/shard_map/stress/pallas_call | solution.py:51
  93.8 2.2 %copy-done.4 = f32[6,3,512,128]{3,2,1,0:T(8,128)} copy-done((f32[6,3,512,128]{3,2,1,0:T(8,128)}, f32[6,3,512,128]{3,2,1,0:T(8,128)S(1)}, u32[]{:S(2)}) %copy-start.4) | copy-done | bytes 4718616
  97.3 2.3 %copy-done.5 = f32[6,3,512,128]{3,2,1,0:T(8,128)S(1)} copy-done((f32[6,3,512,128]{3,2,1,0:T(8,128)S(1)}, f32[6,3,512,128]{3,2,1,0:T(8,128)}, u32[]{:S(2)}) %copy-start.5) | copy-done | bytes 4718616
  103.9 4.7 %stress_edges_last.1 = (f32[6,3,512,128]{3,2,1,0:T(8,128)S(1)}, f32[6,512,384]{2,1,0:T(8,128)}, f32[2,384]{1,0:T(2,128)}, f32[2,384]{1,0:T(2,128)}) custom-call(f32[6,3,512,128]{3,2,1,0:T(8,128)S(1)} %copy-done.5, f32[3,512,128]{2,1,0:T(8,128)S(1)} %get-tuple-element.63.refs_1_.refs_2_, ...), custom_call_target="tpu_custom_call", output_to_operand_aliasing={{0}: (0, {})} | custom-call | flops 1000000 | bytes 1000000 | tf_op jit(solution)/shard_map/stress_edges_last/pallas_call | solution.py:51
  (87 shorter events, 20.5 us)
Async XLA Ops:
  3.4 28.0 %all-to-all-start = ((f32[16,8,384]{2,1,0:T(8,128)}), f32[16,8,384]{2,1,0:T(8,128)S(1)}, u32[]{:S(2)}, u32[]{:S(2)}) async-start(f32[16,8,384]{2,1,0:T(8,128)} %own.1), calls=%async_computation | async-start | bytes 393216 | tf_op jit(solution)/shard_map/all_to_all | solution.py:534
  12.6 8.6 %copy-start.25 = (f32[32,16,384]{2,1,0:T(8,128)S(1)}, f32[32,16,384]{2,1,0:T(8,128)}, u32[]{:S(2)}) copy-start(f32[32,16,384]{2,1,0:T(8,128)} %param.11) | copy-start | bytes 2359300
  13.3 14.2 %copy-start = (f32[6,3,512,128]{3,2,1,0:T(8,128)}, f32[6,3,512,128]{3,2,1,0:T(8,128)S(1)}, u32[]{:S(2)}) copy-start(f32[6,3,512,128]{3,2,1,0:T(8,128)S(1)} %get-tuple-element.49.s.refs_1_) | copy-start | bytes 14155780
  13.3 12.4 %collective-permute-start.1 = (f32[4,3,16,128]{3,2,1,0:T(8,128)S(1)}, f32[4,3,16,128]{3,2,1,0:T(8,128)S(1)}, u32[]{:S(2)}, u32[]{:S(2)}) collective-permute-start(f32[4,3,16,128]{3,2,1,0:T(8,128)S(1)} %get-tuple-element.53), channel_id=1, source_target_pairs={{16,0},{32,16},{48,32},{64,48},{80,64},{96,80},{112,96},{0,112},{1... | collective-permute-start | bytes 294920 | tf_op jit(solution)/shard_map/ppermute | solution.py:29
  19.4 8.2 %collective-permute-start = (f32[5,3,16,128]{3,2,1,0:T(8,128)S(1)}, f32[5,3,16,128]{3,2,1,0:T(8,128)S(1)}, u32[]{:S(2)}, u32[]{:S(2)}) collective-permute-start(f32[5,3,16,128]{3,2,1,0:T(8,128)S(1)} %get-tuple-element.52), channel_id=1, source_target_pairs={{0,16},{16,32},{32,48},{48,64},{64,80},{80,96},{96,112},{112,0},{1... | collective-permute-start | bytes 368648 | tf_op jit(solution)/shard_map/ppermute | solution.py:24
  19.4 8.2 %collective-permute-start.3 = (f32[4,3,32,128]{3,2,1,0:T(8,128)S(1)}, f32[4,3,32,128]{3,2,1,0:T(8,128)S(1)}, u32[]{:S(2)}, u32[]{:S(2)}) collective-permute-start(f32[4,3,32,128]{3,2,1,0:T(8,128)S(1)} %get-tuple-element.55), channel_id=1, source_target_pairs={{1,0},{2,1},{3,2},{4,3},{5,4},{6,5},{7,6},{8,7},{9,8},{10,9},{11,1... | collective-permute-start | bytes 589832 | tf_op jit(solution)/shard_map/ppermute | solution.py:29
  19.7 7.8 %collective-permute-start.2 = (f32[5,3,32,128]{3,2,1,0:T(8,128)S(1)}, f32[5,3,32,128]{3,2,1,0:T(8,128)S(1)}, u32[]{:S(2)}, u32[]{:S(2)}) collective-permute-start(f32[5,3,32,128]{3,2,1,0:T(8,128)S(1)} %get-tuple-element.54), channel_id=1, source_target_pairs={{0,1},{1,2},{2,3},{3,4},{4,5},{5,6},{6,7},{7,8},{8,9},{9,10},{10,1... | collective-permute-start | bytes 737288 | tf_op jit(solution)/shard_map/ppermute | solution.py:24
  29.0 4.7 %collective-permute-start.4 = (f32[3,32,128]{2,1,0:T(8,128)S(1)}, f32[3,32,128]{2,1,0:T(8,128)S(1)}, u32[]{:S(2)}, u32[]{:S(2)}) collective-permute-start(f32[3,32,128]{2,1,0:T(8,128)S(1)} %get-tuple-element.56.refs_0_), channel_id=1, source_target_pairs={{1,2},{2,1},{3,4},{4,3},{5,6},{6,5},{7,8},{8,7},{9,10},{10,9},{11,... | collective-permute-start | bytes 147464 | tf_op jit(solution)/shard_map/ppermute | solution.py:38
  32.1 16.2 %collective-permute-start.7 = (f32[4,3,32,128]{3,2,1,0:T(8,128)}, f32[4,3,32,128]{3,2,1,0:T(8,128)S(1)}, u32[]{:S(2)}, u32[]{:S(2)}) collective-permute-start(f32[4,3,32,128]{3,2,1,0:T(8,128)} %get-tuple-element.66), channel_id=1, source_target_pairs={{0,1},{1,2},{2,3},{3,4},{4,5},{5,6},{6,7},{7,8},{8,9},{9,10},{10,1... | collective-permute-start | bytes 589832 | tf_op jit(solution)/shard_map/ppermute | solution.py:24
  32.2 16.2 %collective-permute-start.8 = (f32[5,3,32,128]{3,2,1,0:T(8,128)S(1)}, f32[5,3,32,128]{3,2,1,0:T(8,128)S(1)}, u32[]{:S(2)}, u32[]{:S(2)}) collective-permute-start(f32[5,3,32,128]{3,2,1,0:T(8,128)S(1)} %get-tuple-element.67), channel_id=1, source_target_pairs={{1,0},{2,1},{3,2},{4,3},{5,4},{6,5},{7,6},{8,7},{9,8},{10,9},{11,1... | collective-permute-start | bytes 737288 | tf_op jit(solution)/shard_map/ppermute | solution.py:29
  34.2 14.1 %collective-permute-start.5 = (f32[4,3,16,128]{3,2,1,0:T(8,128)S(1)}, f32[4,3,16,128]{3,2,1,0:T(8,128)S(1)}, u32[]{:S(2)}, u32[]{:S(2)}) collective-permute-start(f32[4,3,16,128]{3,2,1,0:T(8,128)S(1)} %get-tuple-element.64), channel_id=1, source_target_pairs={{0,16},{16,32},{32,48},{48,64},{64,80},{80,96},{96,112},{112,0},{1... | collective-permute-start | bytes 294920 | tf_op jit(solution)/shard_map/ppermute | solution.py:24
  34.9 13.5 %collective-permute-start.6 = (f32[5,3,16,128]{3,2,1,0:T(8,128)S(1)}, f32[5,3,16,128]{3,2,1,0:T(8,128)S(1)}, u32[]{:S(2)}, u32[]{:S(2)}) collective-permute-start(f32[5,3,16,128]{3,2,1,0:T(8,128)S(1)} %get-tuple-element.65), channel_id=1, source_target_pairs={{16,0},{32,16},{48,32},{64,48},{80,64},{96,80},{112,96},{0,112},{1... | collective-permute-start | bytes 368648 | tf_op jit(solution)/shard_map/ppermute | solution.py:29
  48.4 9.6 %copy-start.8 = (f32[3,512,128]{2,1,0:T(8,128)S(1)}, f32[3,512,128]{2,1,0:T(8,128)}, u32[]{:S(2)}) copy-start(f32[3,512,128]{2,1,0:T(8,128)} %copy-done.7) | copy-start | bytes 2359300
  49.4 12.7 %copy-start.2 = (f32[6,3,512,128]{3,2,1,0:T(8,128)}, f32[6,3,512,128]{3,2,1,0:T(8,128)S(1)}, u32[]{:S(2)}) copy-start(f32[6,3,512,128]{3,2,1,0:T(8,128)S(1)} %get-tuple-element.71.s.refs_1_) | copy-start | bytes 14155780
  49.5 12.6 %collective-permute-start.10 = (f32[4,3,16,128]{3,2,1,0:T(8,128)S(1)}, f32[4,3,16,128]{3,2,1,0:T(8,128)S(1)}, u32[]{:S(2)}, u32[]{:S(2)}) collective-permute-start(f32[4,3,16,128]{3,2,1,0:T(8,128)S(1)} %get-tuple-element.73), channel_id=1, source_target_pairs={{16,0},{32,16},{48,32},{64,48},{80,64},{96,80},{112,96},{0,112},{1... | collective-permute-start | bytes 294920 | tf_op jit(solution)/shard_map/ppermute | solution.py:29
  52.4 9.7 %collective-permute-start.9 = (f32[5,3,16,128]{3,2,1,0:T(8,128)S(1)}, f32[5,3,16,128]{3,2,1,0:T(8,128)S(1)}, u32[]{:S(2)}, u32[]{:S(2)}) collective-permute-start(f32[5,3,16,128]{3,2,1,0:T(8,128)S(1)} %get-tuple-element.72), channel_id=1, source_target_pairs={{0,16},{16,32},{32,48},{48,64},{64,80},{80,96},{96,112},{112,0},{1... | collective-permute-start | bytes 368648 | tf_op jit(solution)/shard_map/ppermute | solution.py:24
  52.5 9.6 %collective-permute-start.12 = (f32[4,3,32,128]{3,2,1,0:T(8,128)S(1)}, f32[4,3,32,128]{3,2,1,0:T(8,128)S(1)}, u32[]{:S(2)}, u32[]{:S(2)}) collective-permute-start(f32[4,3,32,128]{3,2,1,0:T(8,128)S(1)} %get-tuple-element.75), channel_id=1, source_target_pairs={{1,0},{2,1},{3,2},{4,3},{5,4},{6,5},{7,6},{8,7},{9,8},{10,9},{11,1... | collective-permute-start | bytes 589832 | tf_op jit(solution)/shard_map/ppermute | solution.py:29
  57.9 4.2 %collective-permute-start.11 = (f32[5,3,32,128]{3,2,1,0:T(8,128)S(1)}, f32[5,3,32,128]{3,2,1,0:T(8,128)S(1)}, u32[]{:S(2)}, u32[]{:S(2)}) collective-permute-start(f32[5,3,32,128]{3,2,1,0:T(8,128)S(1)} %get-tuple-element.74), channel_id=1, source_target_pairs={{0,1},{1,2},{2,3},{3,4},{4,5},{5,6},{6,7},{7,8},{8,9},{9,10},{10,1... | collective-permute-start | bytes 737288 | tf_op jit(solution)/shard_map/ppermute | solution.py:24
  63.7 4.8 %collective-permute-start.13 = (f32[3,32,128]{2,1,0:T(8,128)S(1)}, f32[3,32,128]{2,1,0:T(8,128)S(1)}, u32[]{:S(2)}, u32[]{:S(2)}) collective-permute-start(f32[3,32,128]{2,1,0:T(8,128)S(1)} %get-tuple-element.76.refs_0_), channel_id=1, source_target_pairs={{1,2},{2,1},{3,4},{4,3},{5,6},{6,5},{7,8},{8,7},{9,10},{10,9},{11,... | collective-permute-start | bytes 147464 | tf_op jit(solution)/shard_map/ppermute | solution.py:38
  65.1 32.2 %collective-permute-start.16 = (f32[4,3,32,128]{3,2,1,0:T(8,128)}, f32[4,3,32,128]{3,2,1,0:T(8,128)S(1)}, u32[]{:S(2)}, u32[]{:S(2)}) collective-permute-start(f32[4,3,32,128]{3,2,1,0:T(8,128)} %get-tuple-element.85), channel_id=1, source_target_pairs={{0,1},{1,2},{2,3},{3,4},{4,5},{5,6},{6,7},{7,8},{8,9},{9,10},{10,1... | collective-permute-start | bytes 589832 | tf_op jit(solution)/shard_map/ppermute | solution.py:24
  65.4 31.9 %collective-permute-start.17 = (f32[5,3,32,128]{3,2,1,0:T(8,128)}, f32[5,3,32,128]{3,2,1,0:T(8,128)}, u32[]{:S(2)}, u32[]{:S(2)}) collective-permute-start(f32[5,3,32,128]{3,2,1,0:T(8,128)} %get-tuple-element.86), channel_id=1, source_target_pairs={{1,0},{2,1},{3,2},{4,3},{5,4},{6,5},{7,6},{8,7},{9,8},{10,9},{11,1... | collective-permute-start | bytes 737288 | tf_op jit(solution)/shard_map/ppermute | solution.py:29
  73.4 23.9 %all-to-all-start.1 = ((f32[16,8,384]{2,1,0:T(8,128)}), f32[16,8,384]{2,1,0:T(8,128)S(1)}, u32[]{:S(2)}, u32[]{:S(2)}) async-start(f32[16,8,384]{2,1,0:T(8,128)} %copy-done.9), calls=%async_computation.1 | async-start | bytes 393216 | tf_op jit(solution)/shard_map/all_to_all | solution.py:595
  81.2 14.8 %collective-permute-start.14 = (f32[4,3,16,128]{3,2,1,0:T(8,128)}, f32[4,3,16,128]{3,2,1,0:T(8,128)S(1)}, u32[]{:S(2)}, u32[]{:S(2)}) collective-permute-start(f32[4,3,16,128]{3,2,1,0:T(8,128)} %copy-done.28), channel_id=1, source_target_pairs={{0,16},{16,32},{32,48},{48,64},{64,80},{80,96},{96,112},{112,0},{1... | collective-permute-start | bytes 294920 | tf_op jit(solution)/shard_map/ppermute | solution.py:24
  81.6 15.1 %collective-permute-start.15 = (f32[5,3,16,128]{3,2,1,0:T(8,128)}, f32[5,3,16,128]{3,2,1,0:T(8,128)S(1)}, u32[]{:S(2)}, u32[]{:S(2)}) collective-permute-start(f32[5,3,16,128]{3,2,1,0:T(8,128)} %copy-done.27), channel_id=1, source_target_pairs={{16,0},{32,16},{48,32},{64,48},{80,64},{96,80},{112,96},{0,112},{1... | collective-permute-start | bytes 368648 | tf_op jit(solution)/shard_map/ppermute | solution.py:29
  (25 other events, 39.8 us)
where the time goes:
time: 110 us; the launch traced here: 109 us
  starting transfers between devices  50.5 us (46%)
  Pallas kernels  31.3 us (28%)
  local copies, waits for them, and re-layouts  24 us (22%)
  waiting for transfers between devices  1.85 us (2%)
    pallas_call x13, Pallas kernels, call(): pl.pallas_call(body, out_shape=shapes, in_specs=ins, out_specs=[spec for...  31.3 us
    ppermute x8, starting transfers between devices, shift_down(): return lax.ppermute(x, axis, [((i + 1) % count, i) for i in range(count)])  28.9 us
    unnamed x58, local copies, waits for them, and re-layouts  24 us
    all_to_all x1, starting transfers between devices, local(): recv = lax.all_to_all(got[7], 'normal', 0, 0, tiled=True)  7.86 us
    all_to_all x1, starting transfers between devices, local(): recv = lax.all_to_all(spread, 'normal', 0, 0, tiled=True)  6.91 us
    ppermute x2, starting transfers between devices, swap_odd(): return lax.ppermute(x, axis, pairs)  3.86 us
    ppermute x8, starting transfers between devices, shift_up(): return lax.ppermute(x, axis, [(i, (i + 1) % count) for i in range(count)])  3.01 us
  transfers between devices with their start and end apart: 20, of which 1 were waited for; matrix products, arithmetic and copies ran while one was open for 0% of the time, Pallas kernels for 21%

commit v1 on v0

--- a/solution.py
+++ b/solution.py
@@ -38,9 +38,14 @@
     return lax.ppermute(x, axis, pairs)
 
 
+def swap(x, bit):
+    count = lax.axis_size("normal")
+    return lax.ppermute(x, "normal", [(i, i ^ bit) for i in range(count)])
+
+
 VMEM = pl.BlockSpec(memory_space=pltpu.VMEM)
 SMEM = pl.BlockSpec(memory_space=pltpu.SMEM)
-ANY = pl.BlockSpec(memory_space=pl.ANY)
+HBM = pl.BlockSpec(memory_space=pltpu.HBM)
 
 
 def call(body, ins, outs, args, scratch=(), aliases=None, cost=None, name=None):
@@ -177,14 +182,20 @@
     lax.fori_loop(2, nx - 2, step, 0)
 
 
-def velocity_body(nx, ny, first, s, v_in, b_in, v, *refs):
+def velocity_body(nx, ny, first, s, v_in, b_in, *refs):
     tiles = s.shape[1]
     if first:
-        bd, sem = refs
+        m_in, v, bd, md, sem = refs
         copies = to_tiles(b_in, bd, sem.at[3])
         for c in range(3):
             copies += to_tiles(v_in.at[c], v.at[c], sem.at[c])
-        run(copies)
+        late = to_tiles(m_in, md, sem.at[4])
+        for c in copies + late:
+            c.start()
+        for c in copies:
+            c.wait()
+    else:
+        (v,) = refs
     cf = Coefs(ny)
 
     def body(x, static):
@@ -208,25 +219,29 @@
                 v[c, k, at, :] = src[c, k, at, :] + w * a[c][k]
 
     over_x(nx, body)
-
-
-def stress_body(nx, ny, first, last, *refs):
-    refs = list(refs)
-    v, s_in, m_in = refs[:3]
-    refs = refs[3:]
-    s = refs.pop(0)
-    md = refs.pop(0) if first else m_in
-    v_out = refs.pop(0) if last else None
-    sem = refs.pop(0) if first or last else None
-    tiles = s.shape[1]
     if first:
-        run(to_tiles(m_in, md, sem.at[0]))
+        for c in late:
+            c.wait()
+
+
+def stress_body(nx, ny, first, last, v, s_in, m_in, *refs):
     if last:
+        yl, yh, minus, plus, traction, s, v_out, s_out, sem = refs
+        md = m_in
         out = []
         for c in range(3):
             out += from_tiles(v.at[c], v_out.at[c], sem.at[c])
         for c in out:
             c.start()
+        e = Edges(nx, ny)
+        stress_y_terms(s, md, e, ny, yl, yh, minus, plus)
+        s_in = s
+    elif first:
+        s, md = refs
+    else:
+        (s,) = refs
+        md = m_in
+    tiles = s.shape[1]
     cf = Coefs(ny)
 
     def body(x, static):
@@ -242,10 +257,11 @@
         eyz = add(cf.z_plus(vy), cf.y_plus(vz))
         tr = add(exx, eyy, ezz)
         for k in range(tiles):
-            w = md[k, at, :]
             if first:
-                w = DT * w
+                w = DT * m_in[k, at, :]
                 md[k, at, :] = w
+            else:
+                w = md[k, at, :]
             s[SXX, k, at, :] = s_in[SXX, k, at, :] + w * (tr[k] + 2.0 * exx[k])
             s[SYY, k, at, :] = s_in[SYY, k, at, :] + w * (tr[k] + 2.0 * eyy[k])
             s[SZZ, k, at, :] = s_in[SZZ, k, at, :] + w * (tr[k] + 2.0 * ezz[k])
@@ -253,10 +269,35 @@
             s[SXZ, k, at, :] = s_in[SXZ, k, at, :] + w * exz[k]
             s[SYZ, k, at, :] = s_in[SYZ, k, at, :] + w * eyz[k]
 
-    over_x(nx, body)
-    if last:
-        for c in out:
-            c.wait()
+    if not last:
+        over_x(nx, body)
+        return
+
+    for x in (0, 1, nx - 2, nx - 1):
+        body(x, True)
+    on_minus, _ = fault_side()
+
+    def step(x, carry):
+        body(x, False)
+        return carry
+
+    begin, width = 2, -(-(nx - 4) // 4)
+    for stop in range(begin + width, nx - 2 + width, width):
+        stop = min(stop, nx - 2)
+        lax.fori_loop(begin, stop, step, 0)
+        at = pl.ds(begin * ny + ny - 1, stop - begin, stride=ny)
+        s[SXY, :, at, :] = jnp.where(on_minus, traction[:, begin:stop, :], s[SXY, :, at, :])
+        span = pl.ds(begin * ny, (stop - begin) * ny)
+        for c in range(6):
+            for k in range(tiles):
+                copy = pltpu.make_async_copy(
+                    s.at[c, k, span], s_out.at[c, span, tile(k)], sem.at[3 + c, k]
+                )
+                copy.start()
+                out.append(copy)
+        begin = stop
+    for c in out:
+        c.wait()
 
 
 class Edges:
@@ -293,6 +334,43 @@
         last = lax.axis_size(axis) - 1
         out += [jnp.where(i > 0, 1.0, 0.0).astype(F32), jnp.where(i < last, 1.0, 0.0).astype(F32)]
     return out
+
+
+def fault_side():
+    position = lax.axis_index("normal")
+    half = lax.axis_size("normal") // 2
+    return position == half - 1, position == half
+
+
+def stress_x_terms(s, w, e, nx, xl, xh):
+    low, high = sides()[:2]
+    a = [xl[k] * low for k in range(4)]
+    b = [xh[k] * high for k in range(5)]
+    for i, value in minus_edges(nx, a[0:2], b[0:1]):
+        add_rows(s, SXX, w, e.x(i), 3.0, value)
+        add_rows(s, SYY, w, e.x(i), 1.0, value)
+        add_rows(s, SZZ, w, e.x(i), 1.0, value)
+    for i, value in plus_edges(nx, a[2:3], b[1:3]):
+        add_rows(s, SXY, w, e.x(i), 1.0, value)
+    for i, value in plus_edges(nx, a[3:4], b[3:5]):
+        add_rows(s, SXZ, w, e.x(i), 1.0, value)
+
+
+def stress_y_terms(s, w, e, ny, yl, yh, minus, plus):
+    low, high = sides()[2:]
+    on_minus, on_plus = fault_side()
+    a = [yl[k] * low for k in range(4)]
+    b = [yh[k] * high for k in range(5)]
+    a[2] = jnp.where(on_plus, minus[...], a[2])
+    b[1] = jnp.where(on_minus, plus[...], b[1])
+    for i, value in minus_edges(ny, a[0:2], b[0:1]):
+        add_rows(s, SXX, w, e.y(i), 1.0, value)
+        add_rows(s, SYY, w, e.y(i), 3.0, value)
+        add_rows(s, SZZ, w, e.y(i), 1.0, value)
+    for i, value in plus_edges(ny, a[2:3], b[1:3]):
+        add_rows(s, SXY, w, e.y(i), 1.0, value)
+    for i, value in plus_edges(ny, a[3:4], b[3:5]):
+        add_rows(s, SYZ, w, e.y(i), 1.0, value)
 
 
 def add_rows(ref, comp, w, at, factor, value):
@@ -384,8 +462,7 @@
     position = lax.axis_index("normal")
     members = lax.axis_size("normal")
     odd = lax.rem(position, 2) == 1
-    on_minus = position == members // 2 - 1
-    on_plus = position == members // 2
+    on_minus, on_plus = fault_side()
     m, o = mine[...], other[...]
     minus = jnp.where(odd, m, o)
     plus = jnp.where(odd, o, m)
@@ -416,89 +493,98 @@
     for k, (comp, i) in enumerate(((0, 0), (1, 0), (1, 1), (2, 0), (2, 1))):
         xd[k] = v[comp, :, e.x(i), :]
     if last:
-        back, tmp = refs[13:]
-        tmp[0] = rate
-        tmp[1] = state
-        count = nx // back.shape[0]
-        for k in range(back.shape[0]):
-            for q in range(2):
-                for z in range(tmp.shape[1]):
-                    back[k, q * count : (q + 1) * count, tile(z)] = tmp[
-                        q, z, k * count : (k + 1) * count, :
-                    ]
-        pad = back.shape[1] - 2 * count
-        if pad:
-            back[:, 2 * count :, :] = jnp.zeros((back.shape[0], pad, back.shape[2]), F32)
-
-
-def stress_edges_body(nx, ny, last, rows, *refs):
-    s_in, w, xl, xh, yl, yh, minus, plus, traction = refs[:9]
+        (back,) = refs[13:]
+        half = nx // 2
+        upper = position >= members // 2
+        for q, value in enumerate((rate, state)):
+            back[q] = jnp.where(upper, value[:, half:, :], value[:, :half, :])
+
+
+def choose_body(holders, mine, got, out):
+    out[...] = jnp.where(holds(holders), mine[...], got[...])
+
+
+def holds(holders):
+    position = lax.axis_index("normal")
+    return functools.reduce(lambda p, q: p | q, [position == h for h in holders])
+
+
+def stress_edges_body(nx, ny, s_in, w, xl, xh, yl, yh, minus, plus, traction, s, xu, xd, yu, yd):
     del s_in
     e = Edges(nx, ny)
-    fxl, fxh, fyl, fyh = sides()
-    position = lax.axis_index("normal")
-    members = lax.axis_size("normal")
-    on_minus = position == members // 2 - 1
-    on_plus = position == members // 2
-    if last:
-        recv, s, out, slip, state, sem = refs[9:]
-    else:
-        s, xu, xd, yu, yd = refs[9:]
-    a = [xl[k] * fxl for k in range(4)]
-    b = [xh[k] * fxh for k in range(5)]
-    for i, value in minus_edges(nx, a[0:2], b[0:1]):
-        add_rows(s, SXX, w, e.x(i), 3.0, value)
-        add_rows(s, SYY, w, e.x(i), 1.0, value)
-        add_rows(s, SZZ, w, e.x(i), 1.0, value)
-    for i, value in plus_edges(nx, a[2:3], b[1:3]):
-        add_rows(s, SXY, w, e.x(i), 1.0, value)
-    for i, value in plus_edges(nx, a[3:4], b[3:5]):
-        add_rows(s, SXZ, w, e.x(i), 1.0, value)
-    a = [yl[k] * fyl for k in range(4)]
-    b = [yh[k] * fyh for k in range(5)]
-    a[2] = jnp.where(on_plus, minus[...], a[2])
-    b[1] = jnp.where(on_minus, plus[...], b[1])
-    for i, value in minus_edges(ny, a[0:2], b[0:1]):
-        add_rows(s, SXX, w, e.y(i), 1.0, value)
-        add_rows(s, SYY, w, e.y(i), 3.0, value)
-        add_rows(s, SZZ, w, e.y(i), 1.0, value)
-    for i, value in plus_edges(ny, a[2:3], b[1:3]):
-        add_rows(s, SXY, w, e.y(i), 1.0, value)
-    for i, value in plus_edges(ny, a[3:4], b[3:5]):
-        add_rows(s, SYZ, w, e.y(i), 1.0, value)
+    on_minus, _ = fault_side()
+    stress_x_terms(s, w, e, nx, xl, xh)
+    stress_y_terms(s, w, e, ny, yl, yh, minus, plus)
     s[SXY, :, e.y(ny - 1), :] = jnp.where(on_minus, traction[...], s[SXY, :, e.y(ny - 1), :])
-    if last:
-        copies = []
+    pack_stress_x(s, e, xu, xd)
+    pack_stress_y(s, e, yu, yd)
+
+
+def stress_last_body(nx, ny, rows, holders, s, w, xl, xh, traction, mine, got, o_in, out, slip, state, sem):
+    del o_in
+    e = Edges(nx, ny)
+    on_minus, _ = fault_side()
+    stress_x_terms(s, w, e, nx, xl, xh)
+    copies = []
+    for x in (0, 1, nx - 2, nx - 1):
+        at = pl.ds(x * ny + ny - 1, 1)
+        s[SXY, :, at, :] = jnp.where(on_minus, traction[:, x : x + 1, :], s[SXY, :, at, :])
+    for j, x in enumerate((0, nx - 2)):
+        span = pl.ds(x * ny, 2 * ny)
         for c in range(6):
-            copies += from_tiles(s.at[c], out.at[c], sem.at[c])
-        for copy in copies:
-            copy.start()
-        slip[...] = recv[members // 2, 0:rows, :]
-        state[...] = recv[members // 2, rows : 2 * rows, :]
-        for copy in copies:
-            copy.wait()
-    else:
-        pack_stress_x(s, e, xu, xd)
-        pack_stress_y(s, e, yu, yd)
-
-
-def own_body(state, mask, ids, out):
+            for k in range(s.shape[1]):
+                copies.append(
+                    pltpu.make_async_copy(
+                        s.at[c, k, span], out.at[c, span, tile(k)], sem.at[j * 6 + c, k]
+                    )
+                )
+    for c in copies:
+        c.start()
+    half = lax.axis_size("normal") // 2
+    at = pl.ds(rows * lax.rem(lax.axis_index("normal"), half), rows)
+    have = holds(holders)
+    for k in range(s.shape[1]):
+        slip[:, tile(k)] = jnp.where(have, mine[0, k, at, :], got[0, k, at, :])
+        state[:, tile(k)] = jnp.where(have, mine[1, k, at, :], got[1, k, at, :])
+    for c in copies:
+        c.wait()
+
+
+def own_body(state, mask, ids, out, st, mk, rg, sem):
     rows = state.shape[0]
-    block = jnp.concatenate((state[...], mask[...].astype(F32), ids[...].astype(F32)), 0)
+    run(
+        [
+            pltpu.make_async_copy(a, b, sem.at[0, k])
+            for k, (a, b) in enumerate(((state, st), (mask, mk), (ids, rg)))
+        ]
+    )
+    out[0, 0:rows, :] = st[...]
+    out[0, rows : 2 * rows, :] = mk[...].astype(F32)
+    out[0, 2 * rows : 3 * rows, :] = rg[...].astype(F32)
     pad = out.shape[1] - 3 * rows
     if pad:
-        block = jnp.concatenate((block, jnp.zeros((pad, block.shape[1]), F32)), 0)
-    for k in range(out.shape[0]):
-        out[k] = block
-
-
-def parameters_body(rows, recv, table, st, par, tmp):
-    for k in range(recv.shape[0]):
+        out[0, 3 * rows :, :] = jnp.zeros((pad, out.shape[2]), F32)
+
+
+def merge_body(bit, mine, got, out):
+    upper = lax.rem(lax.axis_index("normal") // bit, 2) == 1
+    n = mine.shape[0]
+    a, b = mine[...], got[...]
+    out[0:n] = jnp.where(upper, b, a)
+    out[n : 2 * n] = jnp.where(upper, a, b)
+
+
+def parameters_body(rows, mine, got, table, st, par, tmp):
+    half = mine.shape[0]
+    upper = lax.axis_index("normal") >= half
+    for k in range(2 * half):
         at = slice(k * rows, (k + 1) * rows)
+        a, b = (mine, got) if k < half else (got, mine)
+        block = jnp.where(upper, b[k % half], a[k % half])
         for z in range(st.shape[0]):
-            st[z, at, :] = recv[k, 0:rows, tile(z)]
-            par[0, z, at, :] = recv[k, rows : 2 * rows, tile(z)]
-            tmp[z, at, :] = recv[k, 2 * rows : 3 * rows, tile(z)]
+            st[z, at, :] = block[0:rows, tile(z)]
+            par[0, z, at, :] = block[rows : 2 * rows, tile(z)]
+            tmp[z, at, :] = block[2 * rows : 3 * rows, tile(z)]
     ids = tmp[...]
     for j in range(4):
         p = jnp.zeros_like(ids)
@@ -521,100 +607,114 @@
     side_cost = pl.CostEstimate(flops=1_000_000, bytes_accessed=1_000_000, transcendentals=0)
 
     depth = -(-3 * rows // 8) * 8
-    (spread,) = call(
-        own_body, [VMEM] * 3, [((members, depth, nz), VMEM)],
-        (fault_state, fault_mask, region_ids), cost=side_cost, name="own",
+    (known,) = call(
+        own_body, [HBM] * 3, [((1, depth, nz), VMEM)], (fault_state, fault_mask, region_ids),
+        scratch=[pltpu.VMEM((rows, nz), F32)] + [pltpu.VMEM((rows, nz), jnp.int32)] * 2 + [dma(1)],
+        cost=side_cost, name="own",
     )
     s, xu, xd, yu, yd = call(
-        functools.partial(load_body, nx, ny), [ANY],
+        functools.partial(load_body, nx, ny), [HBM],
         [((6, nt, flat, LANES), VMEM), ((5, nt, ny, LANES), VMEM), ((4, nt, ny, LANES), VMEM),
          ((5, nt, nx, LANES), VMEM), ((4, nt, nx, LANES), VMEM)],
         (str_in,), scratch=[dma(6)], cost=side_cost, name="load",
     )
-    recv = lax.all_to_all(spread, "normal", 0, 0, tiled=True)
+    bit = 1
+    while 2 * bit < members:
+        (known,) = call(
+            functools.partial(merge_body, bit), [VMEM] * 2, [((2 * bit, depth, nz), VMEM)],
+            (known, swap(known, bit)), cost=side_cost, name="merge",
+        )
+        bit *= 2
     state, par = call(
-        functools.partial(parameters_body, rows), [VMEM, SMEM],
-        [((nt, nx, LANES), VMEM), ((5, nt, nx, LANES), VMEM)], (recv, friction_table),
+        functools.partial(parameters_body, rows), [VMEM, VMEM, SMEM],
+        [((nt, nx, LANES), VMEM), ((5, nt, nx, LANES), VMEM)],
+        (known, swap(known, bit), friction_table),
         scratch=[pltpu.VMEM((nt, nx, LANES), F32)], cost=side_cost, name="parameters",
     )
+    block_v = ((3, nt, flat, LANES), VMEM)
+    block_s = ((6, nt, flat, LANES), VMEM)
+    block_1 = ((nt, flat, LANES), VMEM)
+    row_1 = ((nt, nx, LANES), VMEM)
     v = w = m = None
     for step in range(STEPS):
         first, last = step == 0, step == STEPS - 1
         xl, xh = shift_up(xu, "strike"), shift_down(xd, "strike")
         yl, yh = shift_up(yu, "normal"), shift_down(yd, "normal")
         if first:
-            v, w = call(
-                functools.partial(velocity_body, nx, ny, True), [VMEM, ANY, ANY],
-                [((3, nt, flat, LANES), VMEM), ((nt, flat, LANES), VMEM)], (s, vel_in, buo_in),
-                scratch=[dma(4)], cost=stage_cost, name="velocity_first",
+            v, w, m = call(
+                functools.partial(velocity_body, nx, ny, True), [VMEM, HBM, HBM, HBM],
+                [block_v, block_1, block_1], (s, vel_in, buo_in, mod_in),
+                scratch=[dma(5)], cost=stage_cost, name="velocity_first",
             )
         else:
             (v,) = call(
-                functools.partial(velocity_body, nx, ny, False),
-                [VMEM] * 3, [((3, nt, flat, LANES), VMEM)], (s, v, w),
+                functools.partial(velocity_body, nx, ny, False), [VMEM] * 3, [block_v], (s, v, w),
                 aliases={1: 0}, cost=stage_cost, name="velocity",
             )
         v, yu, yd, mine, traction = call(
             functools.partial(velocity_edges_body, nx, ny), [VMEM] * 7,
-            [((3, nt, flat, LANES), VMEM), ((4, nt, nx, LANES), VMEM), ((5, nt, nx, LANES), VMEM),
-             ((nt, nx, LANES), VMEM), ((nt, nx, LANES), VMEM)],
+            [block_v, ((4, nt, nx, LANES), VMEM), ((5, nt, nx, LANES), VMEM), row_1, row_1],
             (v, w, s, xl, xh, yl, yh), aliases={0: 0}, cost=side_cost, name="velocity_edges",
         )
         other = swap_odd(mine, "normal")
         yl, yh = shift_up(yu, "normal"), shift_down(yd, "normal")
-        back_depth = -(-2 * rows // 8) * 8
-        outs = [((3, nt, flat, LANES), VMEM), ((4, nt, ny, LANES), VMEM), ((5, nt, ny, LANES), VMEM)]
-        outs += [((nt, nx, LANES), VMEM)] * 4
+        outs = [block_v, ((4, nt, ny, LANES), VMEM), ((5, nt, ny, LANES), VMEM)] + [row_1] * 4
         if last:
-            outs.append(((members, back_depth, nz), VMEM))
+            outs.append(((2, nt, nx // 2, LANES), VMEM))
         got = call(
             functools.partial(fault_body, nx, ny, last), [VMEM] * 6, outs,
-            (mine, other, traction, par, state, v),
-            scratch=[pltpu.VMEM((2, nt, nx, LANES), F32)] if last else [],
-            aliases={5: 0}, cost=side_cost, name="fault",
+            (mine, other, traction, par, state, v), aliases={5: 0}, cost=side_cost, name="fault",
         )
         v, xu, xd, state, minus, plus, trac_new = got[:7]
         xl, xh = shift_up(xu, "strike"), shift_down(xd, "strike")
-        outs = [((6, nt, flat, LANES), VMEM)]
+        body = functools.partial(stress_body, nx, ny, first, last)
+        if last:
+            back, holders = got[7], [members // 2 - 1, members // 2]
+            bit = members // 4
+            while bit > 1:
+                (back,) = call(
+                    functools.partial(choose_body, tuple(holders)), [VMEM] * 2,
+                    [((2, nt, nx // 2, LANES), VMEM)], (back, swap(back, bit)),
+                    cost=side_cost, name="choose",
+                )
+                holders += [h ^ bit for h in holders]
+                bit //= 2
+            brought = swap(back, 1)
+            s, v_out, s_out = call(
+                body, [VMEM] * 8, [block_s, ((3, flat, nz), HBM), ((6, flat, nz), HBM)],
+                (v, s, m, yl, yh, minus, plus, trac_new),
+                scratch=[dma(9)], aliases={1: 0}, cost=stage_cost, name="stress_last",
+            )
+            s_out, slip, state_out = call(
+                functools.partial(stress_last_body, nx, ny, rows, tuple(holders)),
+                [VMEM] * 7 + [HBM], [((6, flat, nz), HBM), ((rows, nz), VMEM), ((rows, nz), VMEM)],
+                (s, m, xl, xh, trac_new, back, brought, s_out), scratch=[dma(12)],
+                aliases={7: 0}, cost=side_cost, name="edges_last",
+            )
+            continue
         if first:
-            outs.append(((nt, flat, LANES), VMEM))
-        if last:
-            outs.append(((3, flat, nz), ANY))
-        got_s = call(
-            functools.partial(stress_body, nx, ny, first, last),
-            [VMEM, VMEM, ANY if first else VMEM], outs, (v, s, mod_in if first else m),
-            scratch=[dma(3)] if first or last else [], aliases={1: 0}, cost=stage_cost,
-            name="stress",
-        )
-        s = got_s[0]
-        if first:
-            m = got_s[1]
-        edge_in = (s, m, xl, xh, yl, yh, minus, plus, trac_new)
-        if last:
-            v_out = got_s[-1]
-            recv = lax.all_to_all(got[7], "normal", 0, 0, tiled=True)
-            _, s_out, slip, state_out = call(
-                functools.partial(stress_edges_body, nx, ny, True, rows), [VMEM] * 10,
-                [((6, nt, flat, LANES), VMEM), ((6, flat, nz), ANY), ((rows, nz), ANY_VMEM), ((rows, nz), ANY_VMEM)],
-                edge_in + (recv,), scratch=[dma(6)], aliases={0: 0}, cost=side_cost,
-                name="stress_edges_last",
+            s, m = call(
+                body, [VMEM] * 3, [block_s, block_1], (v, s, m), aliases={1: 0, 2: 1},
+                cost=stage_cost, name="stress_first",
             )
         else:
-            s, xu, xd, yu, yd = call(
-                functools.partial(stress_edges_body, nx, ny, False, rows), [VMEM] * 9,
-                [((6, nt, flat, LANES), VMEM), ((5, nt, ny, LANES), VMEM), ((4, nt, ny, LANES), VMEM),
-                 ((5, nt, nx, LANES), VMEM), ((4, nt, nx, LANES), VMEM)],
-                edge_in, aliases={0: 0}, cost=side_cost, name="stress_edges",
+            (s,) = call(
+                body, [VMEM] * 3, [block_s], (v, s, m), aliases={1: 0}, cost=stage_cost,
+                name="stress",
             )
+        s, xu, xd, yu, yd = call(
+            functools.partial(stress_edges_body, nx, ny), [VMEM] * 9,
+            [block_s, ((5, nt, ny, LANES), VMEM), ((4, nt, ny, LANES), VMEM),
+             ((5, nt, nx, LANES), VMEM), ((4, nt, nx, LANES), VMEM)],
+            (s, m, xl, xh, yl, yh, minus, plus, trac_new), aliases={0: 0}, cost=side_cost,
+            name="stress_edges",
+        )
     return (
         v_out.reshape(3, nx, ny, nz),
         s_out.reshape(6, nx, ny, nz),
         slip,
         state_out,
     )
-
-
-ANY_VMEM = pl.BlockSpec(memory_space=pltpu.MemorySpace.VMEM)
 
 
 def solution(mesh):

time: 110 us -> 98.4 us (0.89); the launches traced: 109 us -> 98.2 us
  local copies, waits for them, and re-layouts: 24 us -> 5.55 us
  waiting for transfers between devices: 1.85 us -> 9.41 us
  starting transfers between devices: 50.5 us -> 55.9 us
  Pallas kernels: 31.3 us -> 26.5 us
    unnamed x58 -> x18, local copies, waits for them, and re-layouts: 24 us -> 5.55 us
    ppermute x0 -> x7, starting transfers between devices: none -> 17.2 us  [swap(): return lax.ppermute(x, 'normal', [(i, i ^ bit) for i in range(count)])]
    all_to_all x2 -> x0, starting transfers between devices: 14.8 us -> none  [the longest x1 7.86 us: local(): recv = lax.all_to_all(got[7], 'normal', 0, 0, tiled=True)]
    ppermute x0 -> x7, waiting for transfers between devices: none -> 5.44 us  [swap(): return lax.ppermute(x, 'normal', [(i, i ^ bit) for i in range(count)])]
    pallas_call x13 -> x18, Pallas kernels: 31.3 us -> 26.5 us  [call(): pl.pallas_call(body, out_shape=shapes, in_specs=ins, out_specs=[spec for...]
    ppermute x2, waiting for transfers between devices: 0.01 us -> 3.51 us  [swap_odd(): return lax.ppermute(x, axis, pairs)]
    ppermute x8, starting transfers between devices: 28.9 us -> 31.4 us  [shift_down(): return lax.ppermute(x, axis, [((i + 1) % count, i) for i in range(count)])]
    ppermute x8, starting transfers between devices: 3.01 us -> 5.53 us  [shift_up(): return lax.ppermute(x, axis, [(i, (i + 1) % count) for i in range(count)])]
  transfers between devices with their start and end apart: 20 -> 25, of which waited for: 1 -> 5; matrix products, arithmetic and copies ran while one was open for 0% -> 0% of each run, Pallas kernels for 21% -> 24%
where the time goes in v1:
time: 98.4 us; the launch traced here: 98.2 us
  starting transfers between devices  55.9 us (57%)
  Pallas kernels  26.5 us (27%)
  waiting for transfers between devices  9.41 us (10%)
  local copies, waits for them, and re-layouts  5.55 us (6%)
    ppermute x8, starting transfers between devices, shift_down(): return lax.ppermute(x, axis, [((i + 1) % count, i) for i in range(count)])  31.4 us
    pallas_call x18, Pallas kernels, call(): pl.pallas_call(body, out_shape=shapes, in_specs=ins, out_specs=[spec for...  26.5 us
    ppermute x7, starting transfers between devices, swap(): return lax.ppermute(x, 'normal', [(i, i ^ bit) for i in range(count)])  17.2 us
    unnamed x18, local copies, waits for them, and re-layouts  5.55 us
    ppermute x8, starting transfers between devices, shift_up(): return lax.ppermute(x, axis, [(i, (i + 1) % count) for i in range(count)])  5.53 us
    ppermute x7, waiting for transfers between devices, swap(): return lax.ppermute(x, 'normal', [(i, i ^ bit) for i in range(count)])  5.44 us
    ppermute x2, waiting for transfers between devices, swap_odd(): return lax.ppermute(x, axis, pairs)  3.51 us
  transfers between devices with their start and end apart: 25, of which 5 were waited for; matrix products, arithmetic and copies ran while one was open for 0% of the time, Pallas kernels for 24%

profile of v1, /device:TPU:1, one launch (start us, length us, event | category | flops | bytes accessed | tf_op | source)
XLA Modules:
  0.0 98.2 jit_solution(11010120586373836895)
XLA Ops:
  2.7 1.5 %collective-permute-start.5 = (f32[1,8,384]{2,1,0:T(8,128)S(1)}, f32[1,8,384]{2,1,0:T(8,128)S(1)}, u32[]{:S(2)}, u32[]{:S(2)}) collective-permute-start(f32[1,8,384]{2,1,0:T(8,128)S(1)} %own.1.mine), channel_id=1, source_target_pairs={{0,1},{1,0},{2,3},{3,2},{4,5},{5,4},{6,7},{7,6},{8,9},{9,8},{10,11... | collective-permute-start | bytes 36872 | tf_op jit(solution)/shard_map/ppermute | solution.py:43
  5.1 1.4 %collective-permute-start.6 = (f32[2,8,384]{2,1,0:T(8,128)S(1)}, f32[2,8,384]{2,1,0:T(8,128)S(1)}, u32[]{:S(2)}, u32[]{:S(2)}) collective-permute-start(f32[2,8,384]{2,1,0:T(8,128)S(1)} %merge.3.mine), channel_id=1, source_target_pairs={{0,2},{1,3},{2,0},{3,1},{4,6},{5,7},{6,4},{7,5},{8,10},{9,11},{10,... | collective-permute-start | bytes 73736 | tf_op jit(solution)/shard_map/ppermute | solution.py:43
  6.5 1.3 %collective-permute-done.6.got = f32[2,8,384]{2,1,0:T(8,128)S(1)} collective-permute-done((f32[2,8,384]{2,1,0:T(8,128)S(1)}, f32[2,8,384]{2,1,0:T(8,128)S(1)}, u32[]{:S(2)}, u32[]{:S(2)}) %collective-permute-start.6) | collective-permute-done | bytes 24608 | tf_op jit(solution)/shard_map/ppermute | solution.py:43
  7.8 3.1 %collective-permute-start.7 = (f32[4,8,384]{2,1,0:T(8,128)S(1)}, f32[4,8,384]{2,1,0:T(8,128)S(1)}, u32[]{:S(2)}, u32[]{:S(2)}) collective-permute-start(f32[4,8,384]{2,1,0:T(8,128)S(1)} %merge.4.mine), channel_id=1, source_target_pairs={{0,4},{1,5},{2,6},{3,7},{4,0},{5,1},{6,2},{7,3},{8,12},{9,13},{10,... | collective-permute-start | bytes 147464 | tf_op jit(solution)/shard_map/ppermute | solution.py:43
  10.8 2.3 %copy-done = f32[6,32,16,384]{3,2,1,0:T(8,128)S(1)} copy-done((f32[6,32,16,384]{3,2,1,0:T(8,128)S(1)}, f32[6,32,16,384]{3,2,1,0:T(8,128)}, u32[]{:S(2)}) %copy-start) | copy-done | bytes 4718616
  13.9 2.8 %collective-permute-start = (f32[5,3,16,128]{3,2,1,0:T(8,128)S(1)}, f32[5,3,16,128]{3,2,1,0:T(8,128)S(1)}, u32[]{:S(2)}, u32[]{:S(2)}) collective-permute-start(f32[5,3,16,128]{3,2,1,0:T(8,128)S(1)} %get-tuple-element.54), channel_id=1, source_target_pairs={{0,16},{16,32},{32,48},{48,64},{64,80},{80,96},{96,112},{112,0},{1... | collective-permute-start | bytes 368648 | tf_op jit(solution)/shard_map/ppermute | solution.py:24
  16.7 3.6 %collective-permute-start.1 = (f32[4,3,16,128]{3,2,1,0:T(8,128)S(1)}, f32[4,3,16,128]{3,2,1,0:T(8,128)S(1)}, u32[]{:S(2)}, u32[]{:S(2)}) collective-permute-start(f32[4,3,16,128]{3,2,1,0:T(8,128)S(1)} %get-tuple-element.55), channel_id=1, source_target_pairs={{16,0},{32,16},{48,32},{64,48},{80,64},{96,80},{112,96},{0,112},{1... | collective-permute-start | bytes 294920 | tf_op jit(solution)/shard_map/ppermute | solution.py:29
  20.2 2.3 %collective-permute-start.2 = (f32[5,3,32,128]{3,2,1,0:T(8,128)S(1)}, f32[5,3,32,128]{3,2,1,0:T(8,128)S(1)}, u32[]{:S(2)}, u32[]{:S(2)}) collective-permute-start(f32[5,3,32,128]{3,2,1,0:T(8,128)S(1)} %get-tuple-element.56), channel_id=1, source_target_pairs={{0,1},{1,2},{2,3},{3,4},{4,5},{5,6},{6,7},{7,8},{8,9},{9,10},{10,1... | collective-permute-start | bytes 737288 | tf_op jit(solution)/shard_map/ppermute | solution.py:24
  23.0 4.5 %velocity_first.1 = (f32[3,3,512,128]{3,2,1,0:T(8,128)S(1)}, f32[3,512,128]{2,1,0:T(8,128)S(1)}, f32[3,512,128]{2,1,0:T(8,128)S(1)}) custom-call(f32[6,3,512,128]{3,2,1,0:T(8,128)S(1)} %get-tuple-element.51.s.s_in, f32[3,512,384]{2,1,0:T(8,128)S(1)} %bitcast.7, f32[512,384]{1,0:T(8,128)S(1)} %bitcast.8, f32[512,384]{1,0:T(8,128)S(1)} %bitcast.9), custom_call_target="tpu_custom_call" | custom-call | flops 4000000000 | bytes 16000000 | tf_op jit(solution)/shard_map/velocity_first/pallas_call | solution.py:56
  28.7 1.7 %collective-permute-start.4 = (f32[3,32,128]{2,1,0:T(8,128)S(1)}, f32[3,32,128]{2,1,0:T(8,128)S(1)}, u32[]{:S(2)}, u32[]{:S(2)}) collective-permute-start(f32[3,32,128]{2,1,0:T(8,128)S(1)} %get-tuple-element.58.refs_0_), channel_id=1, source_target_pairs={{1,2},{2,1},{3,4},{4,3},{5,6},{6,5},{7,8},{8,7},{9,10},{10,9},{11,... | collective-permute-start | bytes 147464 | tf_op jit(solution)/shard_map/ppermute | solution.py:38
  31.3 3.7 %collective-permute-start.12 = (f32[5,3,32,128]{3,2,1,0:T(8,128)S(1)}, f32[5,3,32,128]{3,2,1,0:T(8,128)S(1)}, u32[]{:S(2)}, u32[]{:S(2)}) collective-permute-start(f32[5,3,32,128]{3,2,1,0:T(8,128)S(1)} %get-tuple-element.70), channel_id=1, source_target_pairs={{1,0},{2,1},{3,2},{4,3},{5,4},{6,5},{7,6},{8,7},{9,8},{10,9},{11,1... | collective-permute-start | bytes 737288 | tf_op jit(solution)/shard_map/ppermute | solution.py:29
  35.6 5.1 %collective-permute-start.10 = (f32[5,3,16,128]{3,2,1,0:T(8,128)S(1)}, f32[5,3,16,128]{3,2,1,0:T(8,128)S(1)}, u32[]{:S(2)}, u32[]{:S(2)}) collective-permute-start(f32[5,3,16,128]{3,2,1,0:T(8,128)S(1)} %get-tuple-element.68), channel_id=1, source_target_pairs={{16,0},{32,16},{48,32},{64,48},{80,64},{96,80},{112,96},{0,112},{1... | collective-permute-start | bytes 368648 | tf_op jit(solution)/shard_map/ppermute | solution.py:29
  40.7 5.1 %stress_first.1 = (f32[6,3,512,128]{3,2,1,0:T(8,128)S(1)}, f32[3,512,128]{2,1,0:T(8,128)S(1)}) custom-call(f32[3,3,512,128]{3,2,1,0:T(8,128)S(1)} %get-tuple-element.63.v.v_in, f32[6,3,512,128]{3,2,1,0:T(8,128)S(1)} %get-tuple-element.51.s.s_in, f32[3,512,128]{2,1,0:T(8,128)S(1)} %get-tuple-element.64.m_in), custom_call_target="tpu_custom_call", output_to_operand_aliasing={{0}: (1, {}), {1}: (2, {})} | custom-call | flops 4000000000 | bytes 16000000 | tf_op jit(solution)/shard_map/stress_first/pallas_call | solution.py:56
  47.0 5.1 %collective-permute-start.14 = (f32[4,3,16,128]{3,2,1,0:T(8,128)S(1)}, f32[4,3,16,128]{3,2,1,0:T(8,128)S(1)}, u32[]{:S(2)}, u32[]{:S(2)}) collective-permute-start(f32[4,3,16,128]{3,2,1,0:T(8,128)S(1)} %get-tuple-element.76), channel_id=1, source_target_pairs={{16,0},{32,16},{48,32},{64,48},{80,64},{96,80},{112,96},{0,112},{1... | collective-permute-start | bytes 294920 | tf_op jit(solution)/shard_map/ppermute | solution.py:29
  52.1 4.9 %collective-permute-start.16 = (f32[4,3,32,128]{3,2,1,0:T(8,128)S(1)}, f32[4,3,32,128]{3,2,1,0:T(8,128)S(1)}, u32[]{:S(2)}, u32[]{:S(2)}) collective-permute-start(f32[4,3,32,128]{3,2,1,0:T(8,128)S(1)} %get-tuple-element.78), channel_id=1, source_target_pairs={{1,0},{2,1},{3,2},{4,3},{5,4},{6,5},{7,6},{8,7},{9,8},{10,9},{11,1... | collective-permute-start | bytes 589832 | tf_op jit(solution)/shard_map/ppermute | solution.py:29
  56.9 4.1 %velocity.1.v_in = f32[3,3,512,128]{3,2,1,0:T(8,128)S(1)} custom-call(f32[6,3,512,128]{3,2,1,0:T(8,128)S(1)} %get-tuple-element.74.s.s_in, f32[3,3,512,128]{3,2,1,0:T(8,128)S(1)} %get-tuple-element.63.v.v_in, f32[3,512,128]{2,1,0:T(8,128)S(1)} %get-tuple-element.53.w.b_in), custom_call_target="tpu_custom_call", output_to_operand_aliasing={{}: (1, {})} | custom-call | flops 4000000000 | bytes 16000000 | tf_op jit(solution)/shard_map/velocity/pallas_call | solution.py:56
  61.9 4.1 %collective-permute-start.19 = (f32[5,3,32,128]{3,2,1,0:T(8,128)S(1)}, f32[5,3,32,128]{3,2,1,0:T(8,128)S(1)}, u32[]{:S(2)}, u32[]{:S(2)}) collective-permute-start(f32[5,3,32,128]{3,2,1,0:T(8,128)S(1)} %get-tuple-element.85), channel_id=1, source_target_pairs={{1,0},{2,1},{3,2},{4,3},{5,4},{6,5},{7,6},{8,7},{9,8},{10,9},{11,1... | collective-permute-start | bytes 737288 | tf_op jit(solution)/shard_map/ppermute | solution.py:29
  66.0 3.5 %collective-permute-done.17.refs_1_ = f32[3,32,128]{2,1,0:T(8,128)S(1)} collective-permute-done((f32[3,32,128]{2,1,0:T(8,128)S(1)}, f32[3,32,128]{2,1,0:T(8,128)S(1)}, u32[]{:S(2)}, u32[]{:S(2)}) %collective-permute-start.17) | collective-permute-done | bytes 49184 | tf_op jit(solution)/shard_map/ppermute | solution.py:38
  70.6 1.7 %collective-permute-start.22 = (f32[2,3,16,128]{3,2,1,0:T(8,128)S(1)}, f32[2,3,16,128]{3,2,1,0:T(8,128)S(1)}, u32[]{:S(2)}, u32[]{:S(2)}) collective-permute-start(f32[2,3,16,128]{3,2,1,0:T(8,128)S(1)} %get-tuple-element.93.mine), channel_id=1, source_target_pairs={{0,4},{1,5},{2,6},{3,7},{4,0},{5,1},{6,2},{7,3},{8,12},{9,13},{10,... | collective-permute-start | bytes 147464 | tf_op jit(solution)/shard_map/ppermute | solution.py:43
  72.2 3.3 %collective-permute-done.22.got = f32[2,3,16,128]{3,2,1,0:T(8,128)S(1)} collective-permute-done((f32[2,3,16,128]{3,2,1,0:T(8,128)S(1)}, f32[2,3,16,128]{3,2,1,0:T(8,128)S(1)}, u32[]{:S(2)}, u32[]{:S(2)}) %collective-permute-start.22) | collective-permute-done | bytes 49184 | tf_op jit(solution)/shard_map/ppermute | solution.py:43
  75.6 4.9 %collective-permute-start.23 = (f32[2,3,16,128]{3,2,1,0:T(8,128)S(1)}, f32[2,3,16,128]{3,2,1,0:T(8,128)S(1)}, u32[]{:S(2)}, u32[]{:S(2)}) collective-permute-start(f32[2,3,16,128]{3,2,1,0:T(8,128)S(1)} %choose.2.mine), channel_id=1, source_target_pairs={{0,2},{1,3},{2,0},{3,1},{4,6},{5,7},{6,4},{7,5},{8,10},{9,11},{10,... | collective-permute-start | bytes 147464 | tf_op jit(solution)/shard_map/ppermute | solution.py:43
  80.4 5.1 %collective-permute-start.21 = (f32[5,3,16,128]{3,2,1,0:T(8,128)S(1)}, f32[5,3,16,128]{3,2,1,0:T(8,128)S(1)}, u32[]{:S(2)}, u32[]{:S(2)}) collective-permute-start(f32[5,3,16,128]{3,2,1,0:T(8,128)S(1)} %get-tuple-element.92), channel_id=1, source_target_pairs={{16,0},{32,16},{48,32},{64,48},{80,64},{96,80},{112,96},{0,112},{1... | collective-permute-start | bytes 368648 | tf_op jit(solution)/shard_map/ppermute | solution.py:29
  85.5 4.3 %collective-permute-start.24 = (f32[2,3,16,128]{3,2,1,0:T(8,128)S(1)}, f32[2,3,16,128]{3,2,1,0:T(8,128)S(1)}, u32[]{:S(2)}, u32[]{:S(2)}) collective-permute-start(f32[2,3,16,128]{3,2,1,0:T(8,128)S(1)} %choose.3.mine), channel_id=1, source_target_pairs={{0,1},{1,0},{2,3},{3,2},{4,5},{5,4},{6,7},{7,6},{8,9},{9,8},{10,11... | collective-permute-start | bytes 147464 | tf_op jit(solution)/shard_map/ppermute | solution.py:43
  89.8 6.0 %stress_last.1 = (f32[6,3,512,128]{3,2,1,0:T(8,128)S(1)}, f32[3,512,384]{2,1,0:T(8,128)}, f32[6,512,384]{2,1,0:T(8,128)}) custom-call(f32[3,3,512,128]{3,2,1,0:T(8,128)S(1)} %get-tuple-element.83.v, f32[6,3,512,128]{3,2,1,0:T(8,128)S(1)} %get-tuple-element.74.s.s_in, f32[3,512,128]{2,1,0:T(8,128)S(1)} %get-tuple-element.66.w.m_in, ...), custom_call_target="tpu_custom_call", output_to_operand_aliasing={{0}: (1, {})} | custom-call | flops 4000000000 | bytes 16000000 | tf_op jit(solution)/shard_map/stress_last/pallas_call | solution.py:56
  (62 shorter events, 12.0 us)
Async XLA Ops:
  5.1 2.7 %collective-permute-start.6 = (f32[2,8,384]{2,1,0:T(8,128)S(1)}, f32[2,8,384]{2,1,0:T(8,128)S(1)}, u32[]{:S(2)}, u32[]{:S(2)}) collective-permute-start(f32[2,8,384]{2,1,0:T(8,128)S(1)} %merge.3.mine), channel_id=1, source_target_pairs={{0,2},{1,3},{2,0},{3,1},{4,6},{5,7},{6,4},{7,5},{8,10},{9,11},{10,... | collective-permute-start | bytes 73736 | tf_op jit(solution)/shard_map/ppermute | solution.py:43
  7.8 14.8 %collective-permute-start.7 = (f32[4,8,384]{2,1,0:T(8,128)S(1)}, f32[4,8,384]{2,1,0:T(8,128)S(1)}, u32[]{:S(2)}, u32[]{:S(2)}) collective-permute-start(f32[4,8,384]{2,1,0:T(8,128)S(1)} %merge.4.mine), channel_id=1, source_target_pairs={{0,4},{1,5},{2,6},{3,7},{4,0},{5,1},{6,2},{7,3},{8,12},{9,13},{10,... | collective-permute-start | bytes 147464 | tf_op jit(solution)/shard_map/ppermute | solution.py:43
  13.9 13.7 %collective-permute-start = (f32[5,3,16,128]{3,2,1,0:T(8,128)S(1)}, f32[5,3,16,128]{3,2,1,0:T(8,128)S(1)}, u32[]{:S(2)}, u32[]{:S(2)}) collective-permute-start(f32[5,3,16,128]{3,2,1,0:T(8,128)S(1)} %get-tuple-element.54), channel_id=1, source_target_pairs={{0,16},{16,32},{32,48},{48,64},{64,80},{80,96},{96,112},{112,0},{1... | collective-permute-start | bytes 368648 | tf_op jit(solution)/shard_map/ppermute | solution.py:24
  16.7 10.9 %collective-permute-start.1 = (f32[4,3,16,128]{3,2,1,0:T(8,128)S(1)}, f32[4,3,16,128]{3,2,1,0:T(8,128)S(1)}, u32[]{:S(2)}, u32[]{:S(2)}) collective-permute-start(f32[4,3,16,128]{3,2,1,0:T(8,128)S(1)} %get-tuple-element.55), channel_id=1, source_target_pairs={{16,0},{32,16},{48,32},{64,48},{80,64},{96,80},{112,96},{0,112},{1... | collective-permute-start | bytes 294920 | tf_op jit(solution)/shard_map/ppermute | solution.py:29
  20.2 7.7 %collective-permute-start.2 = (f32[5,3,32,128]{3,2,1,0:T(8,128)S(1)}, f32[5,3,32,128]{3,2,1,0:T(8,128)S(1)}, u32[]{:S(2)}, u32[]{:S(2)}) collective-permute-start(f32[5,3,32,128]{3,2,1,0:T(8,128)S(1)} %get-tuple-element.56), channel_id=1, source_target_pairs={{0,1},{1,2},{2,3},{3,4},{4,5},{5,6},{6,7},{7,8},{8,9},{9,10},{10,1... | collective-permute-start | bytes 737288 | tf_op jit(solution)/shard_map/ppermute | solution.py:24
  22.6 5.4 %collective-permute-start.3 = (f32[4,3,32,128]{3,2,1,0:T(8,128)S(1)}, f32[4,3,32,128]{3,2,1,0:T(8,128)S(1)}, u32[]{:S(2)}, u32[]{:S(2)}) collective-permute-start(f32[4,3,32,128]{3,2,1,0:T(8,128)S(1)} %get-tuple-element.57), channel_id=1, source_target_pairs={{1,0},{2,1},{3,2},{4,3},{5,4},{6,5},{7,6},{8,7},{9,8},{10,9},{11,1... | collective-permute-start | bytes 589832 | tf_op jit(solution)/shard_map/ppermute | solution.py:29
  22.6 7.8 %collective-permute-start.8 = (f32[8,8,384]{2,1,0:T(8,128)S(1)}, f32[8,8,384]{2,1,0:T(8,128)S(1)}, u32[]{:S(2)}, u32[]{:S(2)}) collective-permute-start(f32[8,8,384]{2,1,0:T(8,128)S(1)} %merge.5.mine), channel_id=1, source_target_pairs={{0,8},{1,9},{2,10},{3,11},{4,12},{5,13},{6,14},{7,15},{8,0},{9,1},... | collective-permute-start | bytes 294920 | tf_op jit(solution)/shard_map/ppermute | solution.py:43
  28.7 6.3 %collective-permute-start.4 = (f32[3,32,128]{2,1,0:T(8,128)S(1)}, f32[3,32,128]{2,1,0:T(8,128)S(1)}, u32[]{:S(2)}, u32[]{:S(2)}) collective-permute-start(f32[3,32,128]{2,1,0:T(8,128)S(1)} %get-tuple-element.58.refs_0_), channel_id=1, source_target_pairs={{1,2},{2,1},{3,4},{4,3},{5,6},{6,5},{7,8},{8,7},{9,10},{10,9},{11,... | collective-permute-start | bytes 147464 | tf_op jit(solution)/shard_map/ppermute | solution.py:38
  31.1 14.7 %collective-permute-start.11 = (f32[4,3,32,128]{3,2,1,0:T(8,128)S(1)}, f32[4,3,32,128]{3,2,1,0:T(8,128)S(1)}, u32[]{:S(2)}, u32[]{:S(2)}) collective-permute-start(f32[4,3,32,128]{3,2,1,0:T(8,128)S(1)} %get-tuple-element.69), channel_id=1, source_target_pairs={{0,1},{1,2},{2,3},{3,4},{4,5},{5,6},{6,7},{7,8},{8,9},{9,10},{10,1... | collective-permute-start | bytes 589832 | tf_op jit(solution)/shard_map/ppermute | solution.py:24
  31.3 14.5 %collective-permute-start.12 = (f32[5,3,32,128]{3,2,1,0:T(8,128)S(1)}, f32[5,3,32,128]{3,2,1,0:T(8,128)S(1)}, u32[]{:S(2)}, u32[]{:S(2)}) collective-permute-start(f32[5,3,32,128]{3,2,1,0:T(8,128)S(1)} %get-tuple-element.70), channel_id=1, source_target_pairs={{1,0},{2,1},{3,2},{4,3},{5,4},{6,5},{7,6},{8,7},{9,8},{10,9},{11,1... | collective-permute-start | bytes 737288 | tf_op jit(solution)/shard_map/ppermute | solution.py:29
  35.5 10.3 %collective-permute-start.9 = (f32[4,3,16,128]{3,2,1,0:T(8,128)S(1)}, f32[4,3,16,128]{3,2,1,0:T(8,128)S(1)}, u32[]{:S(2)}, u32[]{:S(2)}) collective-permute-start(f32[4,3,16,128]{3,2,1,0:T(8,128)S(1)} %get-tuple-element.67), channel_id=1, source_target_pairs={{0,16},{16,32},{32,48},{48,64},{64,80},{80,96},{96,112},{112,0},{1... | collective-permute-start | bytes 294920 | tf_op jit(solution)/shard_map/ppermute | solution.py:24
  35.6 10.2 %collective-permute-start.10 = (f32[5,3,16,128]{3,2,1,0:T(8,128)S(1)}, f32[5,3,16,128]{3,2,1,0:T(8,128)S(1)}, u32[]{:S(2)}, u32[]{:S(2)}) collective-permute-start(f32[5,3,16,128]{3,2,1,0:T(8,128)S(1)} %get-tuple-element.68), channel_id=1, source_target_pairs={{16,0},{32,16},{48,32},{64,48},{80,64},{96,80},{112,96},{0,112},{1... | collective-permute-start | bytes 368648 | tf_op jit(solution)/shard_map/ppermute | solution.py:29
  46.9 14.2 %collective-permute-start.13 = (f32[5,3,16,128]{3,2,1,0:T(8,128)S(1)}, f32[5,3,16,128]{3,2,1,0:T(8,128)S(1)}, u32[]{:S(2)}, u32[]{:S(2)}) collective-permute-start(f32[5,3,16,128]{3,2,1,0:T(8,128)S(1)} %get-tuple-element.75), channel_id=1, source_target_pairs={{0,16},{16,32},{32,48},{48,64},{64,80},{80,96},{96,112},{112,0},{1... | collective-permute-start | bytes 368648 | tf_op jit(solution)/shard_map/ppermute | solution.py:24
  47.0 14.1 %collective-permute-start.14 = (f32[4,3,16,128]{3,2,1,0:T(8,128)S(1)}, f32[4,3,16,128]{3,2,1,0:T(8,128)S(1)}, u32[]{:S(2)}, u32[]{:S(2)}) collective-permute-start(f32[4,3,16,128]{3,2,1,0:T(8,128)S(1)} %get-tuple-element.76), channel_id=1, source_target_pairs={{16,0},{32,16},{48,32},{64,48},{80,64},{96,80},{112,96},{0,112},{1... | collective-permute-start | bytes 294920 | tf_op jit(solution)/shard_map/ppermute | solution.py:29
  52.1 9.1 %collective-permute-start.15 = (f32[5,3,32,128]{3,2,1,0:T(8,128)S(1)}, f32[5,3,32,128]{3,2,1,0:T(8,128)S(1)}, u32[]{:S(2)}, u32[]{:S(2)}) collective-permute-start(f32[5,3,32,128]{3,2,1,0:T(8,128)S(1)} %get-tuple-element.77), channel_id=1, source_target_pairs={{0,1},{1,2},{2,3},{3,4},{4,5},{5,6},{6,7},{7,8},{8,9},{9,10},{10,1... | collective-permute-start | bytes 737288 | tf_op jit(solution)/shard_map/ppermute | solution.py:24
  52.1 9.0 %collective-permute-start.16 = (f32[4,3,32,128]{3,2,1,0:T(8,128)S(1)}, f32[4,3,32,128]{3,2,1,0:T(8,128)S(1)}, u32[]{:S(2)}, u32[]{:S(2)}) collective-permute-start(f32[4,3,32,128]{3,2,1,0:T(8,128)S(1)} %get-tuple-element.78), channel_id=1, source_target_pairs={{1,0},{2,1},{3,2},{4,3},{5,4},{6,5},{7,6},{8,7},{9,8},{10,9},{11,1... | collective-permute-start | bytes 589832 | tf_op jit(solution)/shard_map/ppermute | solution.py:29
  61.9 27.9 %collective-permute-start.19 = (f32[5,3,32,128]{3,2,1,0:T(8,128)S(1)}, f32[5,3,32,128]{3,2,1,0:T(8,128)S(1)}, u32[]{:S(2)}, u32[]{:S(2)}) collective-permute-start(f32[5,3,32,128]{3,2,1,0:T(8,128)S(1)} %get-tuple-element.85), channel_id=1, source_target_pairs={{1,0},{2,1},{3,2},{4,3},{5,4},{6,5},{7,6},{8,7},{9,8},{10,9},{11,1... | collective-permute-start | bytes 737288 | tf_op jit(solution)/shard_map/ppermute | solution.py:29
  66.0 23.8 %collective-permute-start.18 = (f32[4,3,32,128]{3,2,1,0:T(8,128)S(1)}, f32[4,3,32,128]{3,2,1,0:T(8,128)S(1)}, u32[]{:S(2)}, u32[]{:S(2)}) collective-permute-start(f32[4,3,32,128]{3,2,1,0:T(8,128)S(1)} %get-tuple-element.84), channel_id=1, source_target_pairs={{0,1},{1,2},{2,3},{3,4},{4,5},{5,6},{6,7},{7,8},{8,9},{9,10},{10,1... | collective-permute-start | bytes 589832 | tf_op jit(solution)/shard_map/ppermute | solution.py:24
  66.0 3.5 %collective-permute-start.17 = (f32[3,32,128]{2,1,0:T(8,128)S(1)}, f32[3,32,128]{2,1,0:T(8,128)S(1)}, u32[]{:S(2)}, u32[]{:S(2)}) collective-permute-start(f32[3,32,128]{2,1,0:T(8,128)S(1)} %get-tuple-element.79.refs_0_), channel_id=1, source_target_pairs={{1,2},{2,1},{3,4},{4,3},{5,6},{6,5},{7,8},{8,7},{9,10},{10,9},{11,... | collective-permute-start | bytes 147464 | tf_op jit(solution)/shard_map/ppermute | solution.py:38
  70.6 5.0 %collective-permute-start.22 = (f32[2,3,16,128]{3,2,1,0:T(8,128)S(1)}, f32[2,3,16,128]{3,2,1,0:T(8,128)S(1)}, u32[]{:S(2)}, u32[]{:S(2)}) collective-permute-start(f32[2,3,16,128]{3,2,1,0:T(8,128)S(1)} %get-tuple-element.93.mine), channel_id=1, source_target_pairs={{0,4},{1,5},{2,6},{3,7},{4,0},{5,1},{6,2},{7,3},{8,12},{9,13},{10,... | collective-permute-start | bytes 147464 | tf_op jit(solution)/shard_map/ppermute | solution.py:43
  75.6 10.0 %collective-permute-start.23 = (f32[2,3,16,128]{3,2,1,0:T(8,128)S(1)}, f32[2,3,16,128]{3,2,1,0:T(8,128)S(1)}, u32[]{:S(2)}, u32[]{:S(2)}) collective-permute-start(f32[2,3,16,128]{3,2,1,0:T(8,128)S(1)} %choose.2.mine), channel_id=1, source_target_pairs={{0,2},{1,3},{2,0},{3,1},{4,6},{5,7},{6,4},{7,5},{8,10},{9,11},{10,... | collective-permute-start | bytes 147464 | tf_op jit(solution)/shard_map/ppermute | solution.py:43
  80.4 15.4 %collective-permute-start.20 = (f32[4,3,16,128]{3,2,1,0:T(8,128)S(1)}, f32[4,3,16,128]{3,2,1,0:T(8,128)S(1)}, u32[]{:S(2)}, u32[]{:S(2)}) collective-permute-start(f32[4,3,16,128]{3,2,1,0:T(8,128)S(1)} %get-tuple-element.91), channel_id=1, source_target_pairs={{0,16},{16,32},{32,48},{48,64},{64,80},{80,96},{96,112},{112,0},{1... | collective-permute-start | bytes 294920 | tf_op jit(solution)/shard_map/ppermute | solution.py:24
  80.4 15.4 %collective-permute-start.21 = (f32[5,3,16,128]{3,2,1,0:T(8,128)S(1)}, f32[5,3,16,128]{3,2,1,0:T(8,128)S(1)}, u32[]{:S(2)}, u32[]{:S(2)}) collective-permute-start(f32[5,3,16,128]{3,2,1,0:T(8,128)S(1)} %get-tuple-element.92), channel_id=1, source_target_pairs={{16,0},{32,16},{48,32},{64,48},{80,64},{96,80},{112,96},{0,112},{1... | collective-permute-start | bytes 368648 | tf_op jit(solution)/shard_map/ppermute | solution.py:29
  85.5 10.3 %collective-permute-start.24 = (f32[2,3,16,128]{3,2,1,0:T(8,128)S(1)}, f32[2,3,16,128]{3,2,1,0:T(8,128)S(1)}, u32[]{:S(2)}, u32[]{:S(2)}) collective-permute-start(f32[2,3,16,128]{3,2,1,0:T(8,128)S(1)} %choose.3.mine), channel_id=1, source_target_pairs={{0,1},{1,0},{2,3},{3,2},{4,5},{5,4},{6,7},{7,6},{8,9},{9,8},{10,11... | collective-permute-start | bytes 147464 | tf_op jit(solution)/shard_map/ppermute | solution.py:43
  (9 other events, 38.7 us)

commit v2 on v1

--- a/solution.py
+++ b/solution.py
@@ -224,23 +224,7 @@
             c.wait()
 
 
-def stress_body(nx, ny, first, last, v, s_in, m_in, *refs):
-    if last:
-        yl, yh, minus, plus, traction, s, v_out, s_out, sem = refs
-        md = m_in
-        out = []
-        for c in range(3):
-            out += from_tiles(v.at[c], v_out.at[c], sem.at[c])
-        for c in out:
-            c.start()
-        e = Edges(nx, ny)
-        stress_y_terms(s, md, e, ny, yl, yh, minus, plus)
-        s_in = s
-    elif first:
-        s, md = refs
-    else:
-        (s,) = refs
-        md = m_in
+def stress_slabs(nx, ny, v, s_in, s, m_in, md):
     tiles = s.shape[1]
     cf = Coefs(ny)
 
@@ -257,11 +241,10 @@
         eyz = add(cf.z_plus(vy), cf.y_plus(vz))
         tr = add(exx, eyy, ezz)
         for k in range(tiles):
-            if first:
-                w = DT * m_in[k, at, :]
+            w = m_in[k, at, :]
+            if md is not None:
+                w = DT * w
                 md[k, at, :] = w
-            else:
-                w = md[k, at, :]
             s[SXX, k, at, :] = s_in[SXX, k, at, :] + w * (tr[k] + 2.0 * exx[k])
             s[SYY, k, at, :] = s_in[SYY, k, at, :] + w * (tr[k] + 2.0 * eyy[k])
             s[SZZ, k, at, :] = s_in[SZZ, k, at, :] + w * (tr[k] + 2.0 * ezz[k])
@@ -269,29 +252,51 @@
             s[SXZ, k, at, :] = s_in[SXZ, k, at, :] + w * exz[k]
             s[SYZ, k, at, :] = s_in[SYZ, k, at, :] + w * eyz[k]
 
-    if not last:
-        over_x(nx, body)
-        return
-
+    return body
+
+
+def stress_body(nx, ny, first, v, s_in, m_in, s, *md):
+    over_x(nx, stress_slabs(nx, ny, v, s_in, s, m_in, md[0] if first else None))
+
+
+def last_begin_body(nx, ny, v, s_in, m, back_in, s, back):
+    del s_in
+    body = stress_slabs(nx, ny, v, s, s, m, None)
     for x in (0, 1, nx - 2, nx - 1):
         body(x, True)
+    back[...] = back_in[...]
+
+
+def last_slabs_body(nx, ny, begin, end, first, v, s_in, m, traction, *refs):
+    del s_in
+    out = []
+    if first:
+        yl, yh, minus, plus, s, s_out, v_out, sem = refs
+        for c in range(3):
+            out += from_tiles(v.at[c], v_out.at[c], sem.at[6 + c])
+        for c in out:
+            c.start()
+        stress_y_terms(s, m, Edges(nx, ny), ny, yl, yh, minus, plus)
+    else:
+        _, s, s_out, sem = refs
+    body = stress_slabs(nx, ny, v, s, s, m, None)
     on_minus, _ = fault_side()
 
     def step(x, carry):
         body(x, False)
         return carry
 
-    begin, width = 2, -(-(nx - 4) // 4)
-    for stop in range(begin + width, nx - 2 + width, width):
-        stop = min(stop, nx - 2)
+    width = -(-(end - begin) // 2)
+    while begin < end:
+        stop = min(begin + width, end)
         lax.fori_loop(begin, stop, step, 0)
         at = pl.ds(begin * ny + ny - 1, stop - begin, stride=ny)
         s[SXY, :, at, :] = jnp.where(on_minus, traction[:, begin:stop, :], s[SXY, :, at, :])
         span = pl.ds(begin * ny, (stop - begin) * ny)
         for c in range(6):
-            for k in range(tiles):
+            for k in range(s.shape[1]):
                 copy = pltpu.make_async_copy(
-                    s.at[c, k, span], s_out.at[c, span, tile(k)], sem.at[3 + c, k]
+                    s.at[c, k, span], s_out.at[c, span, tile(k)], sem.at[c, k]
                 )
                 copy.start()
                 out.append(copy)
@@ -417,7 +422,7 @@
     wait(SZZ)
 
 
-def velocity_edges_body(nx, ny, v_in, w, s, xl, xh, yl, yh, v, yu, yd, mine, traction):
+def velocity_edges_body(nx, ny, v_in, w, s, xl, xh, yl, yh, v, mine, traction):
     del v_in
     e = Edges(nx, ny)
     fxl, fxh, fyl, fyh = sides()
@@ -442,6 +447,10 @@
     odd = lax.rem(lax.axis_index("normal"), 2) == 1
     mine[...] = jnp.where(odd, v[0, :, e.y(ny - 1), :], v[0, :, e.y(0), :])
     traction[...] = jnp.where(odd, s[SXY, :, e.y(ny - 1), :], yl[2])
+
+
+def pack_velocity_y_body(nx, ny, v, yu, yd):
+    e = Edges(nx, ny)
     for k, (c, i) in enumerate(((1, ny - 2), (1, ny - 1), (0, ny - 1), (2, ny - 1))):
         yu[k] = v[c, :, e.y(i), :]
     for k, (c, i) in enumerate(((1, 0), (0, 0), (0, 1), (2, 0), (2, 1))):
@@ -520,7 +529,9 @@
     pack_stress_y(s, e, yu, yd)
 
 
-def stress_last_body(nx, ny, rows, holders, s, w, xl, xh, traction, mine, got, o_in, out, slip, state, sem):
+def stress_last_body(
+    nx, ny, rows, holders, s, w, xl, xh, traction, mine, got, o_in, out, slip, state, own, sem
+):
     del o_in
     e = Edges(nx, ny)
     on_minus, _ = fault_side()
@@ -544,8 +555,12 @@
     at = pl.ds(rows * lax.rem(lax.axis_index("normal"), half), rows)
     have = holds(holders)
     for k in range(s.shape[1]):
-        slip[:, tile(k)] = jnp.where(have, mine[0, k, at, :], got[0, k, at, :])
-        state[:, tile(k)] = jnp.where(have, mine[1, k, at, :], got[1, k, at, :])
+        for q in range(2):
+            own[q, :, tile(k)] = jnp.where(have, mine[q, k, at, :], got[q, k, at, :])
+    for q, target in enumerate((slip, state)):
+        copy = pltpu.make_async_copy(own.at[q], target, sem.at[12, q])
+        copy.start()
+        copies.append(copy)
     for c in copies:
         c.wait()
 
@@ -598,17 +613,20 @@
     _, nx, ny, nz = velocity.shape
     rows = fault_state.shape[0]
     flat, nt = nx * ny, nz // LANES
-    vel_in = velocity.reshape(3, flat, nz)
-    str_in = stress.reshape(6, flat, nz)
-    mod_in = modulus.reshape(flat, nz)
-    buo_in = buoyancy.reshape(flat, nz)
+    pin = lambda x: pltpu.with_memory_space_constraint(x, pltpu.HBM)
+    vel_in = pin(velocity.reshape(3, flat, nz))
+    str_in = pin(stress.reshape(6, flat, nz))
+    mod_in = pin(modulus.reshape(flat, nz))
+    buo_in = pin(buoyancy.reshape(flat, nz))
+    fault_in = (pin(fault_state), pin(fault_mask), pin(region_ids))
     dma = lambda n: pltpu.SemaphoreType.DMA((n, nt))
     stage_cost = pl.CostEstimate(flops=4_000_000_000, bytes_accessed=16_000_000, transcendentals=0)
+    part_cost = pl.CostEstimate(flops=2_000_000_000, bytes_accessed=8_000_000, transcendentals=0)
     side_cost = pl.CostEstimate(flops=1_000_000, bytes_accessed=1_000_000, transcendentals=0)
 
     depth = -(-3 * rows // 8) * 8
     (known,) = call(
-        own_body, [HBM] * 3, [((1, depth, nz), VMEM)], (fault_state, fault_mask, region_ids),
+        own_body, [HBM] * 3, [((1, depth, nz), VMEM)], fault_in,
         scratch=[pltpu.VMEM((rows, nz), F32)] + [pltpu.VMEM((rows, nz), jnp.int32)] * 2 + [dma(1)],
         cost=side_cost, name="own",
     )
@@ -618,19 +636,19 @@
          ((5, nt, nx, LANES), VMEM), ((4, nt, nx, LANES), VMEM)],
         (str_in,), scratch=[dma(6)], cost=side_cost, name="load",
     )
-    bit = 1
-    while 2 * bit < members:
-        (known,) = call(
+    tie = lax.optimization_barrier
+
+    def merge(known, got, bit):
+        return call(
             functools.partial(merge_body, bit), [VMEM] * 2, [((2 * bit, depth, nz), VMEM)],
-            (known, swap(known, bit)), cost=side_cost, name="merge",
-        )
-        bit *= 2
-    state, par = call(
-        functools.partial(parameters_body, rows), [VMEM, VMEM, SMEM],
-        [((nt, nx, LANES), VMEM), ((5, nt, nx, LANES), VMEM)],
-        (known, swap(known, bit), friction_table),
-        scratch=[pltpu.VMEM((nt, nx, LANES), F32)], cost=side_cost, name="parameters",
-    )
+            (known, got), cost=side_cost, name="merge",
+        )[0]
+
+    got = swap(known, 1)
+    known, got, xu, xd, yu, yd = tie((known, got, xu, xd, yu, yd))
+    known = merge(known, got, 1)
+    known = merge(known, swap(known, 2), 2)
+    bit = 4
     block_v = ((3, nt, flat, LANES), VMEM)
     block_s = ((6, nt, flat, LANES), VMEM)
     block_1 = ((nt, flat, LANES), VMEM)
@@ -646,18 +664,33 @@
                 [block_v, block_1, block_1], (s, vel_in, buo_in, mod_in),
                 scratch=[dma(5)], cost=stage_cost, name="velocity_first",
             )
+            while 2 * bit < members:
+                known = merge(known, swap(known, bit), bit)
+                bit *= 2
+            known, v = tie((known, v))
+            state, par = call(
+                functools.partial(parameters_body, rows), [VMEM, VMEM, SMEM],
+                [((nt, nx, LANES), VMEM), ((5, nt, nx, LANES), VMEM)],
+                (known, swap(known, bit), friction_table),
+                scratch=[pltpu.VMEM((nt, nx, LANES), F32)], cost=side_cost, name="parameters",
+            )
         else:
             (v,) = call(
                 functools.partial(velocity_body, nx, ny, False), [VMEM] * 3, [block_v], (s, v, w),
                 aliases={1: 0}, cost=stage_cost, name="velocity",
             )
-        v, yu, yd, mine, traction = call(
-            functools.partial(velocity_edges_body, nx, ny), [VMEM] * 7,
-            [block_v, ((4, nt, nx, LANES), VMEM), ((5, nt, nx, LANES), VMEM), row_1, row_1],
+        v, mine, traction = call(
+            functools.partial(velocity_edges_body, nx, ny), [VMEM] * 7, [block_v, row_1, row_1],
             (v, w, s, xl, xh, yl, yh), aliases={0: 0}, cost=side_cost, name="velocity_edges",
         )
         other = swap_odd(mine, "normal")
-        yl, yh = shift_up(yu, "normal"), shift_down(yd, "normal")
+        yu, yd = call(
+            functools.partial(pack_velocity_y_body, nx, ny), [VMEM],
+            [((4, nt, nx, LANES), VMEM), ((5, nt, nx, LANES), VMEM)], (v,), cost=side_cost,
+            name="pack_normal",
+        )
+        if not last:
+            yl, yh = shift_up(yu, "normal"), shift_down(yd, "normal")
         outs = [block_v, ((4, nt, ny, LANES), VMEM), ((5, nt, ny, LANES), VMEM)] + [row_1] * 4
         if last:
             outs.append(((2, nt, nx // 2, LANES), VMEM))
@@ -666,29 +699,64 @@
             (mine, other, traction, par, state, v), aliases={5: 0}, cost=side_cost, name="fault",
         )
         v, xu, xd, state, minus, plus, trac_new = got[:7]
+        if last:
+            xu, xd, yu, yd = tie((xu, xd, yu, yd))
+            yl, yh = shift_up(yu, "normal"), shift_down(yd, "normal")
         xl, xh = shift_up(xu, "strike"), shift_down(xd, "strike")
-        body = functools.partial(stress_body, nx, ny, first, last)
+        body = functools.partial(stress_body, nx, ny, first)
         if last:
+            half_rows = ((2, nt, nx // 2, LANES), VMEM)
             back, holders = got[7], [members // 2 - 1, members // 2]
+            s, back = call(
+                functools.partial(last_begin_body, nx, ny), [VMEM] * 4, [block_s, half_rows],
+                (v, s, m, back), aliases={1: 0}, cost=side_cost,
+                name="last_begin",
+            )
+            edges, bits = [2], []
             bit = members // 4
-            while bit > 1:
-                (back,) = call(
-                    functools.partial(choose_body, tuple(holders)), [VMEM] * 2,
-                    [((2, nt, nx // 2, LANES), VMEM)], (back, swap(back, bit)),
-                    cost=side_cost, name="choose",
-                )
-                holders += [h ^ bit for h in holders]
+            while bit >= 1:
+                bits.append(bit)
                 bit //= 2
-            brought = swap(back, 1)
-            s, v_out, s_out = call(
-                body, [VMEM] * 8, [block_s, ((3, flat, nz), HBM), ((6, flat, nz), HBM)],
-                (v, s, m, yl, yh, minus, plus, trac_new),
-                scratch=[dma(9)], aliases={1: 0}, cost=stage_cost, name="stress_last",
-            )
+            parts = max(len(bits) - 1, 1)
+            for j in range(parts):
+                edges.append(2 + (nx - 4) * (j + 1) // parts)
+            s_out = v_out = None
+            for j, bit in enumerate(bits):
+                came = swap(back, bit)
+                if j < parts:
+                    outs = [block_s, ((6, flat, nz), HBM)]
+                    ins = [VMEM] * 4
+                    args = [v, s, m, trac_new]
+                    aliases = {1: 0}
+                    if j == 0:
+                        ins, args = ins + [VMEM] * 4, args + [yl, yh, minus, plus]
+                        outs.append(((3, flat, nz), HBM))
+                    else:
+                        ins, args = ins + [HBM], args + [s_out]
+                        aliases[4] = 1
+                    parts_out = call(
+                        functools.partial(
+                            last_slabs_body, nx, ny, edges[j], edges[j + 1], j == 0
+                        ),
+                        ins, outs, args, scratch=[dma(9)], aliases=aliases, cost=part_cost,
+                        name=f"last_slabs_{j}",
+                    )
+                    s, s_out = parts_out[:2]
+                    if j == 0:
+                        v_out = parts_out[2]
+                if j < len(bits) - 1:
+                    came, s = tie((came, s))
+                    (back,) = call(
+                        functools.partial(choose_body, tuple(holders)), [VMEM] * 2, [half_rows],
+                        (back, came), cost=side_cost, name="choose",
+                    )
+                    holders += [h ^ bit for h in holders]
             s_out, slip, state_out = call(
                 functools.partial(stress_last_body, nx, ny, rows, tuple(holders)),
-                [VMEM] * 7 + [HBM], [((6, flat, nz), HBM), ((rows, nz), VMEM), ((rows, nz), VMEM)],
-                (s, m, xl, xh, trac_new, back, brought, s_out), scratch=[dma(12)],
+                [VMEM] * 7 + [HBM],
+                [((6, flat, nz), HBM), ((rows, nz), HBM), ((rows, nz), HBM)],
+                (s, m, xl, xh, trac_new, back, came, s_out),
+                scratch=[pltpu.VMEM((2, rows, nz), F32), dma(13)],
                 aliases={7: 0}, cost=side_cost, name="edges_last",
             )
             continue

time: 98.4 us -> 85.3 us (0.87)
  starting transfers between devices: 55.9 us -> 45.5 us
  local copies, waits for them, and re-layouts: 5.55 us -> 0.01 us
  Pallas kernels: 26.5 us -> 31.9 us
  waiting for transfers between devices: 9.41 us -> 6.6 us
    ppermute x7, starting transfers between devices: 17.2 us -> 10.5 us  [swap(): return lax.ppermute(x, 'normal', [(i, i ^ bit) for i in range(count)])]
    unnamed x18 -> x2, local copies, waits for them, and re-layouts: 5.55 us -> 0.01 us
    pallas_call x18 -> x22, Pallas kernels: 26.5 us -> 31.9 us  [call(): pl.pallas_call(body, out_shape=shapes, in_specs=ins, out_specs=[spec for...]
    ppermute x8, starting transfers between devices: 5.53 us -> 1.78 us  [shift_up(): return lax.ppermute(x, axis, [(i, (i + 1) % count) for i in range(count)])]
    ppermute x2, waiting for transfers between devices: 3.51 us -> 1.68 us  [swap_odd(): return lax.ppermute(x, axis, pairs)]
  transfers between devices with their start and end apart: 25 -> 25, of which waited for: 5 -> 3; matrix products, arithmetic and copies ran while one was open for 0% -> 0% of each run, Pallas kernels for 24% -> 32%
where the time goes in v2:
time: 85.3 us; the launch traced here: 85.2 us
  starting transfers between devices  45.5 us (53%)
  Pallas kernels  31.9 us (37%)
  waiting for transfers between devices  6.6 us (8%)
  between operations  1.11 us (1%)
    pallas_call x22, Pallas kernels, call(): pl.pallas_call(body, out_shape=shapes, in_specs=ins, out_specs=[spec for...  31.9 us
    ppermute x8, starting transfers between devices, shift_down(): return lax.ppermute(x, axis, [((i + 1) % count, i) for i in range(count)])  31.3 us
    ppermute x7, starting transfers between devices, swap(): return lax.ppermute(x, 'normal', [(i, i ^ bit) for i in range(count)])  10.5 us
    ppermute x7, waiting for transfers between devices, swap(): return lax.ppermute(x, 'normal', [(i, i ^ bit) for i in range(count)])  4.88 us
    ppermute x2, starting transfers between devices, swap_odd(): return lax.ppermute(x, axis, pairs)  2.01 us
    ppermute x8, starting transfers between devices, shift_up(): return lax.ppermute(x, axis, [(i, (i + 1) % count) for i in range(count)])  1.78 us
  transfers between devices with their start and end apart: 25, of which 3 were waited for; matrix products, arithmetic and copies ran while one was open for 0% of the time, Pallas kernels for 32%

profile of v2, /device:TPU:1, one launch (start us, length us, event | category | flops | bytes accessed | tf_op | source)
XLA Modules:
  0.0 85.2 jit_solution(17321273364901580493)
XLA Ops:
  1.4 1.5 %collective-permute-start = (f32[1,8,384]{2,1,0:T(8,128)S(1)}, f32[1,8,384]{2,1,0:T(8,128)S(1)}, u32[]{:S(2)}, u32[]{:S(2)}) collective-permute-start(f32[1,8,384]{2,1,0:T(8,128)S(1)} %own.1.mine), channel_id=1, source_target_pairs={{0,1},{1,0},{2,3},{3,2},{4,5},{5,4},{6,7},{7,6},{8,9},{9,8},{10,11... | collective-permute-start | bytes 36872 | tf_op jit(solution)/shard_map/ppermute | solution.py:43
  2.9 2.5 %load.1 = (f32[6,3,512,128]{3,2,1,0:T(8,128)S(1)}, f32[5,3,16,128]{3,2,1,0:T(8,128)S(1)}, f32[4,3,16,128]{3,2,1,0:T(8,128)S(1)}, f32[5,3,32,128]{3,2,1,0:T(8,128)S(1)}, f32[4,3,32,128]{3,2,1,0:T(8,128)S(1)}) custom-call(f32[6,512,384]{2,1,0:T(8,128)} %bitcast.7), custom_call_target="tpu_custom_call" | custom-call | flops 1000000 | bytes 1000000 | tf_op jit(solution)/shard_map/load/pallas_call | solution.py:56
  5.4 1.5 %collective-permute-start.1 = (f32[2,8,384]{2,1,0:T(8,128)S(1)}, f32[2,8,384]{2,1,0:T(8,128)S(1)}, u32[]{:S(2)}, u32[]{:S(2)}) collective-permute-start(f32[2,8,384]{2,1,0:T(8,128)S(1)} %merge.3.mine), channel_id=1, source_target_pairs={{0,2},{1,3},{2,0},{3,1},{4,6},{5,7},{6,4},{7,5},{8,10},{9,11},{10,... | collective-permute-start | bytes 73736 | tf_op jit(solution)/shard_map/ppermute | solution.py:43
  6.9 6.2 %collective-permute-start.4 = (f32[4,3,16,128]{3,2,1,0:T(8,128)S(1)}, f32[4,3,16,128]{3,2,1,0:T(8,128)S(1)}, u32[]{:S(2)}, u32[]{:S(2)}) collective-permute-start(f32[4,3,16,128]{3,2,1,0:T(8,128)S(1)} %get-tuple-element.82), channel_id=1, source_target_pairs={{16,0},{32,16},{48,32},{64,48},{80,64},{96,80},{112,96},{0,112},{1... | collective-permute-start | bytes 294920 | tf_op jit(solution)/shard_map/ppermute | solution.py:29
  13.7 1.2 %collective-permute-start.5 = (f32[5,3,32,128]{3,2,1,0:T(8,128)S(1)}, f32[5,3,32,128]{3,2,1,0:T(8,128)S(1)}, u32[]{:S(2)}, u32[]{:S(2)}) collective-permute-start(f32[5,3,32,128]{3,2,1,0:T(8,128)S(1)} %get-tuple-element.83), channel_id=1, source_target_pairs={{0,1},{1,2},{2,3},{3,4},{4,5},{5,6},{6,7},{7,8},{8,9},{9,10},{10,1... | collective-permute-start | bytes 737288 | tf_op jit(solution)/shard_map/ppermute | solution.py:24
  14.9 2.7 %collective-permute-start.2 = (f32[4,8,384]{2,1,0:T(8,128)S(1)}, f32[4,8,384]{2,1,0:T(8,128)S(1)}, u32[]{:S(2)}, u32[]{:S(2)}) collective-permute-start(f32[4,8,384]{2,1,0:T(8,128)S(1)} %merge.4.mine), channel_id=1, source_target_pairs={{0,4},{1,5},{2,6},{3,7},{4,0},{5,1},{6,2},{7,3},{8,12},{9,13},{10,... | collective-permute-start | bytes 147464 | tf_op jit(solution)/shard_map/ppermute | solution.py:43
  17.6 6.1 %velocity_first.1 = (f32[3,3,512,128]{3,2,1,0:T(8,128)S(1)}, f32[3,512,128]{2,1,0:T(8,128)S(1)}, f32[3,512,128]{2,1,0:T(8,128)S(1)}) custom-call(f32[6,3,512,128]{3,2,1,0:T(8,128)S(1)} %get-tuple-element.77.s.s_in, f32[3,512,384]{2,1,0:T(8,128)} %bitcast.8, f32[512,384]{1,0:T(8,128)} %bitcast.10, f32[512,384]{1,0:T(8,128)} %bitcast.11), custom_call_target="tpu_custom_call" | custom-call | flops 4000000000 | bytes 16000000 | tf_op jit(solution)/shard_map/velocity_first/pallas_call | solution.py:56
  24.9 3.7 %collective-permute-done.8.got = f32[8,8,384]{2,1,0:T(8,128)S(1)} collective-permute-done((f32[8,8,384]{2,1,0:T(8,128)S(1)}, f32[8,8,384]{2,1,0:T(8,128)S(1)}, u32[]{:S(2)}, u32[]{:S(2)}) %collective-permute-start.8) | collective-permute-done | bytes 98336 | tf_op jit(solution)/shard_map/ppermute | solution.py:43
  31.0 4.8 %collective-permute-start.10 = (f32[5,3,16,128]{3,2,1,0:T(8,128)S(1)}, f32[5,3,16,128]{3,2,1,0:T(8,128)S(1)}, u32[]{:S(2)}, u32[]{:S(2)}) collective-permute-start(f32[5,3,16,128]{3,2,1,0:T(8,128)S(1)} %get-tuple-element.96), channel_id=1, source_target_pairs={{16,0},{32,16},{48,32},{64,48},{80,64},{96,80},{112,96},{0,112},{1... | collective-permute-start | bytes 368648 | tf_op jit(solution)/shard_map/ppermute | solution.py:29
  35.8 5.1 %stress_first.1 = (f32[6,3,512,128]{3,2,1,0:T(8,128)S(1)}, f32[3,512,128]{2,1,0:T(8,128)S(1)}) custom-call(f32[3,3,512,128]{3,2,1,0:T(8,128)S(1)} %get-tuple-element.91.v.v_in, f32[6,3,512,128]{3,2,1,0:T(8,128)S(1)} %get-tuple-element.77.s.s_in, f32[3,512,128]{2,1,0:T(8,128)S(1)} %get-tuple-element.92.m_in), custom_call_target="tpu_custom_call", output_to_operand_aliasing={{0}: (1, {}), {1}: (2, {})} | custom-call | flops 4000000000 | bytes 16000000 | tf_op jit(solution)/shard_map/stress_first/pallas_call | solution.py:56
  40.9 1.0 %stress_edges.1 = (f32[6,3,512,128]{3,2,1,0:T(8,128)S(1)}, f32[5,3,16,128]{3,2,1,0:T(8,128)S(1)}, f32[4,3,16,128]{3,2,1,0:T(8,128)S(1)}, f32[5,3,32,128]{3,2,1,0:T(8,128)S(1)}, f32[4,3,32,128]{3,2,1,0:T(8,128)S(1)}) custom-call(f32[6,3,512,128]{3,2,1,0:T(8,128)S(1)} %get-tuple-element.93.s_in, ...), custom_call_target="tpu_custom_call", output_to_operand_aliasing={{0}: (0, {})} | custom-call | flops 1000000 | bytes 1000000 | tf_op jit(solution)/shard_map/stress_edges/pallas_call | solution.py:56
  42.0 3.6 %collective-permute-start.14 = (f32[4,3,16,128]{3,2,1,0:T(8,128)S(1)}, f32[4,3,16,128]{3,2,1,0:T(8,128)S(1)}, u32[]{:S(2)}, u32[]{:S(2)}) collective-permute-start(f32[4,3,16,128]{3,2,1,0:T(8,128)S(1)} %get-tuple-element.104), channel_id=1, source_target_pairs={{16,0},{32,16},{48,32},{64,48},{80,64},{96,80},{112,96},{0,112},{1... | collective-permute-start | bytes 294920 | tf_op jit(solution)/shard_map/ppermute | solution.py:29
  45.6 4.3 %collective-permute-start.16 = (f32[4,3,32,128]{3,2,1,0:T(8,128)S(1)}, f32[4,3,32,128]{3,2,1,0:T(8,128)S(1)}, u32[]{:S(2)}, u32[]{:S(2)}) collective-permute-start(f32[4,3,32,128]{3,2,1,0:T(8,128)S(1)} %get-tuple-element.106), channel_id=1, source_target_pairs={{1,0},{2,1},{3,2},{4,3},{5,4},{6,5},{7,6},{8,7},{9,8},{10,9},{11,1... | collective-permute-start | bytes 589832 | tf_op jit(solution)/shard_map/ppermute | solution.py:29
  50.0 4.1 %velocity.1.v_in = f32[3,3,512,128]{3,2,1,0:T(8,128)S(1)} custom-call(f32[6,3,512,128]{3,2,1,0:T(8,128)S(1)} %get-tuple-element.102.s.s_in, f32[3,3,512,128]{3,2,1,0:T(8,128)S(1)} %get-tuple-element.91.v.v_in, f32[3,512,128]{2,1,0:T(8,128)S(1)} %get-tuple-element.80.w.b_in), custom_call_target="tpu_custom_call", output_to_operand_aliasing={{}: (1, {})} | custom-call | flops 4000000000 | bytes 16000000 | tf_op jit(solution)/shard_map/velocity/pallas_call | solution.py:56
  54.8 1.9 %collective-permute-start.17 = (f32[3,32,128]{2,1,0:T(8,128)S(1)}, f32[3,32,128]{2,1,0:T(8,128)S(1)}, u32[]{:S(2)}, u32[]{:S(2)}) collective-permute-start(f32[3,32,128]{2,1,0:T(8,128)S(1)} %get-tuple-element.107.refs_0_), channel_id=1, source_target_pairs={{1,2},{2,1},{3,4},{4,3},{5,6},{6,5},{7,8},{8,7},{9,10},{10,9},{11,... | collective-permute-start | bytes 147464 | tf_op jit(solution)/shard_map/ppermute | solution.py:38
  56.9 1.7 %collective-permute-done.17.refs_1_ = f32[3,32,128]{2,1,0:T(8,128)S(1)} collective-permute-done((f32[3,32,128]{2,1,0:T(8,128)S(1)}, f32[3,32,128]{2,1,0:T(8,128)S(1)}, u32[]{:S(2)}, u32[]{:S(2)}) %collective-permute-start.17) | collective-permute-done | bytes 49184 | tf_op jit(solution)/shard_map/ppermute | solution.py:38
  58.6 1.1 %fault.3 = (f32[3,3,512,128]{3,2,1,0:T(8,128)S(1)}, f32[4,3,16,128]{3,2,1,0:T(8,128)S(1)}, f32[5,3,16,128]{3,2,1,0:T(8,128)S(1)}, f32[3,32,128]{2,1,0:T(8,128)},...) custom-call(f32[3,32,128]{2,1,0:T(8,128)S(1)} %get-tuple-element.107, ...), custom_call_target="tpu_custom_call", output_to_operand_aliasing={{0}: (5, {})} | custom-call | flops 1000000 | bytes 1000000 | tf_op jit(solution)/shard_map/fault/pallas_call | solution.py:56
  59.6 6.1 %collective-permute-start.19 = (f32[5,3,32,128]{3,2,1,0:T(8,128)S(1)}, f32[5,3,32,128]{3,2,1,0:T(8,128)S(1)}, u32[]{:S(2)}, u32[]{:S(2)}) collective-permute-start(f32[5,3,32,128]{3,2,1,0:T(8,128)S(1)} %get-tuple-element.120), channel_id=1, source_target_pairs={{1,0},{2,1},{3,2},{4,3},{5,4},{6,5},{7,6},{8,7},{9,8},{10,9},{11,1... | collective-permute-start | bytes 737288 | tf_op jit(solution)/shard_map/ppermute | solution.py:29
  66.2 5.1 %collective-permute-start.23 = (f32[5,3,16,128]{3,2,1,0:T(8,128)S(1)}, f32[5,3,16,128]{3,2,1,0:T(8,128)S(1)}, u32[]{:S(2)}, u32[]{:S(2)}) collective-permute-start(f32[5,3,16,128]{3,2,1,0:T(8,128)S(1)} %get-tuple-element.132), channel_id=1, source_target_pairs={{16,0},{32,16},{48,32},{64,48},{80,64},{96,80},{112,96},{0,112},{1... | collective-permute-start | bytes 368648 | tf_op jit(solution)/shard_map/ppermute | solution.py:29
  71.3 3.8 %last_slabs_0.1 = (f32[6,3,512,128]{3,2,1,0:T(8,128)S(1)}, f32[6,512,384]{2,1,0:T(8,128)}, f32[3,512,384]{2,1,0:T(8,128)}) custom-call(f32[3,3,512,128]{3,2,1,0:T(8,128)S(1)} %get-tuple-element.111.v, f32[6,3,512,128]{3,2,1,0:T(8,128)S(1)} %get-tuple-element.113.s_in, f32[3,512,128]{2,1,0:T(8,128)S(1)} %get-tuple-element.94.w.m, ...), custom_call_target="tpu_custom_call", output_to_operand_aliasing={{0}: (1, {})} | custom-call | flops 2000000000 | bytes 8000000 | tf_op jit(solution)/shard_map/last_slabs_0/pallas_call | solution.py:56
  75.1 4.2 %collective-permute-start.21 = (f32[2,3,16,128]{3,2,1,0:T(8,128)S(1)}, f32[2,3,16,128]{3,2,1,0:T(8,128)S(1)}, u32[]{:S(2)}, u32[]{:S(2)}) collective-permute-start(f32[2,3,16,128]{3,2,1,0:T(8,128)S(1)} %choose.2.mine), channel_id=1, source_target_pairs={{0,2},{1,3},{2,0},{3,1},{4,6},{5,7},{6,4},{7,5},{8,10},{9,11},{10,... | collective-permute-start | bytes 147464 | tf_op jit(solution)/shard_map/ppermute | solution.py:43
  79.4 3.1 %last_slabs_1.1 = (f32[6,3,512,128]{3,2,1,0:T(8,128)S(1)}, f32[6,512,384]{2,1,0:T(8,128)}) custom-call(f32[3,3,512,128]{3,2,1,0:T(8,128)S(1)} %get-tuple-element.111.v, f32[6,3,512,128]{3,2,1,0:T(8,128)S(1)} %get-tuple-element.127.s_in, f32[3,512,128]{2,1,0:T(8,128)S(1)} %get-tuple-element.94.w.m, ...), custom_call_target="tpu_custom_call", output_to_operand_aliasing={{0}: (1, {}), {1}: (4, {})} | custom-call | flops 2000000000 | bytes 8000000 | tf_op jit(solution)/shard_map/last_slabs_1/pallas_call | solution.py:56
  82.6 1.2 %collective-permute-done.24.got = f32[2,3,16,128]{3,2,1,0:T(8,128)S(1)} collective-permute-done((f32[2,3,16,128]{3,2,1,0:T(8,128)S(1)}, f32[2,3,16,128]{3,2,1,0:T(8,128)S(1)}, u32[]{:S(2)}, u32[]{:S(2)}) %collective-permute-start.24) | collective-permute-done | bytes 49184 | tf_op jit(solution)/shard_map/ppermute | solution.py:43
  83.8 1.2 %edges_last.1 = (f32[6,512,384]{2,1,0:T(8,128)}, f32[2,384]{1,0:T(2,128)}, f32[2,384]{1,0:T(2,128)}) custom-call(f32[6,3,512,128]{3,2,1,0:T(8,128)S(1)} %get-tuple-element.130.s, f32[3,512,128]{2,1,0:T(8,128)S(1)} %get-tuple-element.94.w.m, f32[4,3,16,128]{3,2,1,0:T(8,128)S(1)} %collective-permute-done.22.xl, ...), custom_call_target="tpu_custom_call", output_to_operand_aliasing={{0}: (7, {})} | custom-call | flops 1000000 | bytes 1000000 | tf_op jit(solution)/shard_map/edges_last/pallas_call | solution.py:56
  (50 shorter events, 6.4 us)
Async XLA Ops:
  1.4 4.0 %collective-permute-start = (f32[1,8,384]{2,1,0:T(8,128)S(1)}, f32[1,8,384]{2,1,0:T(8,128)S(1)}, u32[]{:S(2)}, u32[]{:S(2)}) collective-permute-start(f32[1,8,384]{2,1,0:T(8,128)S(1)} %own.1.mine), channel_id=1, source_target_pairs={{0,1},{1,0},{2,3},{3,2},{4,5},{5,4},{6,7},{7,6},{8,9},{9,8},{10,11... | collective-permute-start | bytes 36872 | tf_op jit(solution)/shard_map/ppermute | solution.py:43
  5.4 9.4 %collective-permute-start.1 = (f32[2,8,384]{2,1,0:T(8,128)S(1)}, f32[2,8,384]{2,1,0:T(8,128)S(1)}, u32[]{:S(2)}, u32[]{:S(2)}) collective-permute-start(f32[2,8,384]{2,1,0:T(8,128)S(1)} %merge.3.mine), channel_id=1, source_target_pairs={{0,2},{1,3},{2,0},{3,1},{4,6},{5,7},{6,4},{7,5},{8,10},{9,11},{10,... | collective-permute-start | bytes 73736 | tf_op jit(solution)/shard_map/ppermute | solution.py:43
  6.9 17.2 %collective-permute-start.4 = (f32[4,3,16,128]{3,2,1,0:T(8,128)S(1)}, f32[4,3,16,128]{3,2,1,0:T(8,128)S(1)}, u32[]{:S(2)}, u32[]{:S(2)}) collective-permute-start(f32[4,3,16,128]{3,2,1,0:T(8,128)S(1)} %get-tuple-element.82), channel_id=1, source_target_pairs={{16,0},{32,16},{48,32},{64,48},{80,64},{96,80},{112,96},{0,112},{1... | collective-permute-start | bytes 294920 | tf_op jit(solution)/shard_map/ppermute | solution.py:29
  13.1 11.0 %collective-permute-start.3 = (f32[5,3,16,128]{3,2,1,0:T(8,128)S(1)}, f32[5,3,16,128]{3,2,1,0:T(8,128)S(1)}, u32[]{:S(2)}, u32[]{:S(2)}) collective-permute-start(f32[5,3,16,128]{3,2,1,0:T(8,128)S(1)} %get-tuple-element.81), channel_id=1, source_target_pairs={{0,16},{16,32},{32,48},{48,64},{64,80},{80,96},{96,112},{112,0},{1... | collective-permute-start | bytes 368648 | tf_op jit(solution)/shard_map/ppermute | solution.py:24
  13.1 11.0 %collective-permute-start.6 = (f32[4,3,32,128]{3,2,1,0:T(8,128)S(1)}, f32[4,3,32,128]{3,2,1,0:T(8,128)S(1)}, u32[]{:S(2)}, u32[]{:S(2)}) collective-permute-start(f32[4,3,32,128]{3,2,1,0:T(8,128)S(1)} %get-tuple-element.84), channel_id=1, source_target_pairs={{1,0},{2,1},{3,2},{4,3},{5,4},{6,5},{7,6},{8,7},{9,8},{10,9},{11,1... | collective-permute-start | bytes 589832 | tf_op jit(solution)/shard_map/ppermute | solution.py:29
  13.7 10.4 %collective-permute-start.5 = (f32[5,3,32,128]{3,2,1,0:T(8,128)S(1)}, f32[5,3,32,128]{3,2,1,0:T(8,128)S(1)}, u32[]{:S(2)}, u32[]{:S(2)}) collective-permute-start(f32[5,3,32,128]{3,2,1,0:T(8,128)S(1)} %get-tuple-element.83), channel_id=1, source_target_pairs={{0,1},{1,2},{2,3},{3,4},{4,5},{5,6},{6,7},{7,8},{8,9},{9,10},{10,1... | collective-permute-start | bytes 737288 | tf_op jit(solution)/shard_map/ppermute | solution.py:24
  14.9 8.8 %collective-permute-start.2 = (f32[4,8,384]{2,1,0:T(8,128)S(1)}, f32[4,8,384]{2,1,0:T(8,128)S(1)}, u32[]{:S(2)}, u32[]{:S(2)}) collective-permute-start(f32[4,8,384]{2,1,0:T(8,128)S(1)} %merge.4.mine), channel_id=1, source_target_pairs={{0,4},{1,5},{2,6},{3,7},{4,0},{5,1},{6,2},{7,3},{8,12},{9,13},{10,... | collective-permute-start | bytes 147464 | tf_op jit(solution)/shard_map/ppermute | solution.py:43
  23.7 4.8 %collective-permute-start.8 = (f32[8,8,384]{2,1,0:T(8,128)S(1)}, f32[8,8,384]{2,1,0:T(8,128)S(1)}, u32[]{:S(2)}, u32[]{:S(2)}) collective-permute-start(f32[8,8,384]{2,1,0:T(8,128)S(1)} %merge.5.mine), channel_id=1, source_target_pairs={{0,8},{1,9},{2,10},{3,11},{4,12},{5,13},{6,14},{7,15},{8,0},{9,1},... | collective-permute-start | bytes 294920 | tf_op jit(solution)/shard_map/ppermute | solution.py:43
  24.8 5.3 %collective-permute-start.7 = (f32[3,32,128]{2,1,0:T(8,128)S(1)}, f32[3,32,128]{2,1,0:T(8,128)S(1)}, u32[]{:S(2)}, u32[]{:S(2)}) collective-permute-start(f32[3,32,128]{2,1,0:T(8,128)S(1)} %get-tuple-element.85.refs_0_), channel_id=1, source_target_pairs={{1,2},{2,1},{3,4},{4,3},{5,6},{6,5},{7,8},{8,7},{9,10},{10,9},{11,... | collective-permute-start | bytes 147464 | tf_op jit(solution)/shard_map/ppermute | solution.py:38
  29.4 11.5 %collective-permute-start.11 = (f32[4,3,32,128]{3,2,1,0:T(8,128)S(1)}, f32[4,3,32,128]{3,2,1,0:T(8,128)S(1)}, u32[]{:S(2)}, u32[]{:S(2)}) collective-permute-start(f32[4,3,32,128]{3,2,1,0:T(8,128)S(1)} %get-tuple-element.97), channel_id=1, source_target_pairs={{0,1},{1,2},{2,3},{3,4},{4,5},{5,6},{6,7},{7,8},{8,9},{9,10},{10,1... | collective-permute-start | bytes 589832 | tf_op jit(solution)/shard_map/ppermute | solution.py:24
  29.5 11.4 %collective-permute-start.12 = (f32[5,3,32,128]{3,2,1,0:T(8,128)S(1)}, f32[5,3,32,128]{3,2,1,0:T(8,128)S(1)}, u32[]{:S(2)}, u32[]{:S(2)}) collective-permute-start(f32[5,3,32,128]{3,2,1,0:T(8,128)S(1)} %get-tuple-element.98), channel_id=1, source_target_pairs={{1,0},{2,1},{3,2},{4,3},{5,4},{6,5},{7,6},{8,7},{9,8},{10,9},{11,1... | collective-permute-start | bytes 737288 | tf_op jit(solution)/shard_map/ppermute | solution.py:29
  30.5 10.3 %collective-permute-start.9 = (f32[4,3,16,128]{3,2,1,0:T(8,128)S(1)}, f32[4,3,16,128]{3,2,1,0:T(8,128)S(1)}, u32[]{:S(2)}, u32[]{:S(2)}) collective-permute-start(f32[4,3,16,128]{3,2,1,0:T(8,128)S(1)} %get-tuple-element.95), channel_id=1, source_target_pairs={{0,16},{16,32},{32,48},{48,64},{64,80},{80,96},{96,112},{112,0},{1... | collective-permute-start | bytes 294920 | tf_op jit(solution)/shard_map/ppermute | solution.py:24
  31.0 9.9 %collective-permute-start.10 = (f32[5,3,16,128]{3,2,1,0:T(8,128)S(1)}, f32[5,3,16,128]{3,2,1,0:T(8,128)S(1)}, u32[]{:S(2)}, u32[]{:S(2)}) collective-permute-start(f32[5,3,16,128]{3,2,1,0:T(8,128)S(1)} %get-tuple-element.96), channel_id=1, source_target_pairs={{16,0},{32,16},{48,32},{64,48},{80,64},{96,80},{112,96},{0,112},{1... | collective-permute-start | bytes 368648 | tf_op jit(solution)/shard_map/ppermute | solution.py:29
  42.0 12.1 %collective-permute-start.14 = (f32[4,3,16,128]{3,2,1,0:T(8,128)S(1)}, f32[4,3,16,128]{3,2,1,0:T(8,128)S(1)}, u32[]{:S(2)}, u32[]{:S(2)}) collective-permute-start(f32[4,3,16,128]{3,2,1,0:T(8,128)S(1)} %get-tuple-element.104), channel_id=1, source_target_pairs={{16,0},{32,16},{48,32},{64,48},{80,64},{96,80},{112,96},{0,112},{1... | collective-permute-start | bytes 294920 | tf_op jit(solution)/shard_map/ppermute | solution.py:29
  45.6 8.5 %collective-permute-start.13 = (f32[5,3,16,128]{3,2,1,0:T(8,128)S(1)}, f32[5,3,16,128]{3,2,1,0:T(8,128)S(1)}, u32[]{:S(2)}, u32[]{:S(2)}) collective-permute-start(f32[5,3,16,128]{3,2,1,0:T(8,128)S(1)} %get-tuple-element.103), channel_id=1, source_target_pairs={{0,16},{16,32},{32,48},{48,64},{64,80},{80,96},{96,112},{112,0},{1... | collective-permute-start | bytes 368648 | tf_op jit(solution)/shard_map/ppermute | solution.py:24
  45.6 8.5 %collective-permute-start.16 = (f32[4,3,32,128]{3,2,1,0:T(8,128)S(1)}, f32[4,3,32,128]{3,2,1,0:T(8,128)S(1)}, u32[]{:S(2)}, u32[]{:S(2)}) collective-permute-start(f32[4,3,32,128]{3,2,1,0:T(8,128)S(1)} %get-tuple-element.106), channel_id=1, source_target_pairs={{1,0},{2,1},{3,2},{4,3},{5,4},{6,5},{7,6},{8,7},{9,8},{10,9},{11,1... | collective-permute-start | bytes 589832 | tf_op jit(solution)/shard_map/ppermute | solution.py:29
  50.0 4.2 %collective-permute-start.15 = (f32[5,3,32,128]{3,2,1,0:T(8,128)S(1)}, f32[5,3,32,128]{3,2,1,0:T(8,128)S(1)}, u32[]{:S(2)}, u32[]{:S(2)}) collective-permute-start(f32[5,3,32,128]{3,2,1,0:T(8,128)S(1)} %get-tuple-element.105), channel_id=1, source_target_pairs={{0,1},{1,2},{2,3},{3,4},{4,5},{5,6},{6,7},{7,8},{8,9},{9,10},{10,1... | collective-permute-start | bytes 737288 | tf_op jit(solution)/shard_map/ppermute | solution.py:24
  54.8 3.8 %collective-permute-start.17 = (f32[3,32,128]{2,1,0:T(8,128)S(1)}, f32[3,32,128]{2,1,0:T(8,128)S(1)}, u32[]{:S(2)}, u32[]{:S(2)}) collective-permute-start(f32[3,32,128]{2,1,0:T(8,128)S(1)} %get-tuple-element.107.refs_0_), channel_id=1, source_target_pairs={{1,2},{2,1},{3,4},{4,3},{5,6},{6,5},{7,8},{8,7},{9,10},{10,9},{11,... | collective-permute-start | bytes 147464 | tf_op jit(solution)/shard_map/ppermute | solution.py:38
  59.6 11.7 %collective-permute-start.19 = (f32[5,3,32,128]{3,2,1,0:T(8,128)S(1)}, f32[5,3,32,128]{3,2,1,0:T(8,128)S(1)}, u32[]{:S(2)}, u32[]{:S(2)}) collective-permute-start(f32[5,3,32,128]{3,2,1,0:T(8,128)S(1)} %get-tuple-element.120), channel_id=1, source_target_pairs={{1,0},{2,1},{3,2},{4,3},{5,4},{6,5},{7,6},{8,7},{9,8},{10,9},{11,1... | collective-permute-start | bytes 737288 | tf_op jit(solution)/shard_map/ppermute | solution.py:29
  65.7 5.6 %collective-permute-start.18 = (f32[4,3,32,128]{3,2,1,0:T(8,128)S(1)}, f32[4,3,32,128]{3,2,1,0:T(8,128)S(1)}, u32[]{:S(2)}, u32[]{:S(2)}) collective-permute-start(f32[4,3,32,128]{3,2,1,0:T(8,128)S(1)} %get-tuple-element.119), channel_id=1, source_target_pairs={{0,1},{1,2},{2,3},{3,4},{4,5},{5,6},{6,7},{7,8},{8,9},{9,10},{10,1... | collective-permute-start | bytes 589832 | tf_op jit(solution)/shard_map/ppermute | solution.py:24
  66.1 9.0 %collective-permute-start.20 = (f32[2,3,16,128]{3,2,1,0:T(8,128)S(1)}, f32[2,3,16,128]{3,2,1,0:T(8,128)S(1)}, u32[]{:S(2)}, u32[]{:S(2)}) collective-permute-start(f32[2,3,16,128]{3,2,1,0:T(8,128)S(1)} %get-tuple-element.124.mine), channel_id=1, source_target_pairs={{0,4},{1,5},{2,6},{3,7},{4,0},{5,1},{6,2},{7,3},{8,12},{9,13},{10,... | collective-permute-start | bytes 147464 | tf_op jit(solution)/shard_map/ppermute | solution.py:43
  66.2 16.4 %collective-permute-start.22 = (f32[4,3,16,128]{3,2,1,0:T(8,128)S(1)}, f32[4,3,16,128]{3,2,1,0:T(8,128)S(1)}, u32[]{:S(2)}, u32[]{:S(2)}) collective-permute-start(f32[4,3,16,128]{3,2,1,0:T(8,128)S(1)} %get-tuple-element.131), channel_id=1, source_target_pairs={{0,16},{16,32},{32,48},{48,64},{64,80},{80,96},{96,112},{112,0},{1... | collective-permute-start | bytes 294920 | tf_op jit(solution)/shard_map/ppermute | solution.py:24
  66.2 16.3 %collective-permute-start.23 = (f32[5,3,16,128]{3,2,1,0:T(8,128)S(1)}, f32[5,3,16,128]{3,2,1,0:T(8,128)S(1)}, u32[]{:S(2)}, u32[]{:S(2)}) collective-permute-start(f32[5,3,16,128]{3,2,1,0:T(8,128)S(1)} %get-tuple-element.132), channel_id=1, source_target_pairs={{16,0},{32,16},{48,32},{64,48},{80,64},{96,80},{112,96},{0,112},{1... | collective-permute-start | bytes 368648 | tf_op jit(solution)/shard_map/ppermute | solution.py:29
  75.1 7.3 %collective-permute-start.21 = (f32[2,3,16,128]{3,2,1,0:T(8,128)S(1)}, f32[2,3,16,128]{3,2,1,0:T(8,128)S(1)}, u32[]{:S(2)}, u32[]{:S(2)}) collective-permute-start(f32[2,3,16,128]{3,2,1,0:T(8,128)S(1)} %choose.2.mine), channel_id=1, source_target_pairs={{0,2},{1,3},{2,0},{3,1},{4,6},{5,7},{6,4},{7,5},{8,10},{9,11},{10,... | collective-permute-start | bytes 147464 | tf_op jit(solution)/shard_map/ppermute | solution.py:43
  (2 other events, 6.2 us)

commit v3 on v2

--- a/solution.py
+++ b/solution.py
@@ -10,9 +10,10 @@
 STEPS = 2
 NEWTON = 4
 
-C1 = 9.0 / 8.0
 C2 = -1.0 / 24.0
+RATIO = (9.0 / 8.0) / C2
 DT = 0.1
+STEP = DT * C2
 ETA = 1.0
 
 F32 = jnp.float32
@@ -66,61 +67,81 @@
     )(*args)
 
 
-LANES = 128
-
-
-def masked(shape, offset, value):
-    i = lax.broadcasted_iota(jnp.int32, shape, 0)
-    n = shape[0]
-    keep = i >= -offset if offset < 0 else i < n - offset
-    return jnp.where(keep, jnp.asarray(value, F32), 0.0)
-
-
-class Coefs:
+SUB, LANES = 8, 128
+
+
+class Shifts:
     def __init__(self, ny):
-        self.ny = ny
-        self.t = {}
-        for offset, value in ((-1, C1), (1, C2), (-2, C2), (1, C1), (2, C2), (-1, C2)):
-            self.t[offset, value] = masked((ny, LANES), offset, value)
-        self.lane = lax.broadcasted_iota(jnp.int32, (ny, LANES), 1)
-
-    def y(self, f, offset, value):
-        return pltpu.roll(f, (-offset) % self.ny, 0) * self.t[offset, value]
-
-    def y_minus(self, fs):
+        self.count = ny // SUB
+        self.row = lax.broadcasted_iota(jnp.int32, (SUB, LANES), 0)
+        self.lane = lax.broadcasted_iota(jnp.int32, (SUB, LANES), 1)
+
+    def rows(self, here, ref, comp, slab, offset):
+        edge = offset > 0
+        keep = self.row < SUB - offset if edge else self.row >= -offset
+        outer = self.count - 1 if edge else 0
+        if here.static:
+            turned = [[pltpu.roll(f, (-offset) % SUB, 0) for f in fs] for fs in slab]
+            out = []
+            for fs in turned:
+                line = []
+                for h, f in enumerate(fs):
+                    j = h + 1 if edge else h - 1
+                    line.append(jnp.where(keep, f, 0.0 if h == outer else fs[j]))
+                out.append(line)
+            return out
         return [
-            C1 * f - self.y(f, -1, C1) + self.y(f, 1, C2) - self.y(f, -2, C2) for f in fs
+            [jnp.where(keep, f, 0.0) if h == outer else f for h, f in enumerate(fs)]
+            for fs in here.load(ref, comp, 0, offset)
         ]
 
-    def y_plus(self, fs):
-        return [
-            self.y(f, 1, C1) - C1 * f + self.y(f, 2, C2) - self.y(f, -1, C2) for f in fs
-        ]
-
-    def z(self, fs, offset):
-        rolls = [pltpu.roll(f, (-offset) % LANES, 1) for f in fs]
-        keep = self.lane < LANES - offset if offset > 0 else self.lane >= -offset
-        out = []
-        for k, r in enumerate(rolls):
-            j = k + 1 if offset > 0 else k - 1
-            out.append(jnp.where(keep, r, rolls[j] if 0 <= j < len(fs) else 0.0))
-        return out
-
-    def z_minus(self, fs):
-        return [
-            C1 * (f - b) + C2 * (c - d)
-            for f, b, c, d in zip(fs, self.z(fs, -1), self.z(fs, 1), self.z(fs, -2))
-        ]
-
-    def z_plus(self, fs):
-        return [
-            C1 * (b - f) + C2 * (c - d)
-            for f, b, c, d in zip(fs, self.z(fs, 1), self.z(fs, 2), self.z(fs, -1))
-        ]
-
-
-def add(*lists):
-    return [functools.reduce(lambda p, q: p + q, parts) for parts in zip(*lists)]
+    def y_minus(self, here, ref, comp, slab):
+        near = [self.rows(here, ref, comp, slab, o) for o in (-1, 1, -2)]
+        return each(lambda f, b, c, d: RATIO * (f - b) + (c - d), slab, *near)
+
+    def y_plus(self, here, ref, comp, slab):
+        near = [self.rows(here, ref, comp, slab, o) for o in (1, 2, -1)]
+        return each(lambda f, b, c, d: RATIO * (b - f) + (c - d), slab, *near)
+
+    def lines(self, f, slab):
+        columns = [f([fs[h] for fs in slab]) for h in range(self.count)]
+        return [[column[k] for column in columns] for k in range(len(slab))]
+
+    def z_minus(self, slab):
+        def line(fs):
+            n, lane = len(fs), self.lane
+            r = [pltpu.roll(f, LANES - 1, 1) for f in fs]
+            p = [jnp.where(lane < LANES - 1, r[k], r[k + 1] if k + 1 < n else 0.0) for k in range(n)]
+            w = [RATIO * p[k] + fs[k] for k in range(n)]
+            end = jnp.where(lane == LANES - 1, RATIO * r[0], 0.0)
+            w[-1] = jnp.where(lane < LANES - 2, w[-1], end)
+            q = [pltpu.roll(x, 2, 1) for x in w]
+            return [RATIO * fs[k] + p[k] - jnp.where(lane >= 2, q[k], q[k - 1]) for k in range(n)]
+
+        return self.lines(line, slab)
+
+    def z_plus(self, slab):
+        def line(fs):
+            n, lane = len(fs), self.lane
+            r = [pltpu.roll(f, 1, 1) for f in fs]
+            m = [jnp.where(lane >= 1, r[k], r[k - 1] if k else 0.0) for k in range(n)]
+            w = [RATIO * m[k] + fs[k] for k in range(n)]
+            w[0] = jnp.where(lane >= 2, w[0], jnp.where(lane == 0, RATIO * r[-1], 0.0))
+            q = [pltpu.roll(x, LANES - 2, 1) for x in w]
+            return [
+                jnp.where(lane < LANES - 2, q[k], q[(k + 1) % n]) - (RATIO * fs[k] + m[k])
+                for k in range(n)
+            ]
+
+        return self.lines(line, slab)
+
+
+def each(f, *slabs):
+    return [[f(*pieces) for pieces in zip(*lines)] for lines in zip(*slabs)]
+
+
+def add(*slabs):
+    return each(lambda *parts: functools.reduce(lambda p, q: p + q, parts), *slabs)
 
 
 def tile(k):
@@ -148,120 +169,164 @@
         c.wait()
 
 
-MINUS = ((0, C1), (-1, -C1), (1, C2), (-2, -C2))
-PLUS = ((1, C1), (0, -C1), (2, C2), (-1, -C2))
-
-
-def slab(ref, comp, at):
-    if comp is None:
-        return [ref[k, at, :] for k in range(ref.shape[0])]
-    return [ref[comp, k, at, :] for k in range(ref.shape[1])]
-
-
-def x_terms(ref, comp, x, nx, ny, static, pairs):
-    total = None
-    for offset, coef in pairs:
-        if static and not 0 <= x + offset < nx:
-            continue
-        start = (x + offset) * ny
-        if not static:
-            start = pl.multiple_of(start, 8)
-        term = [coef * f for f in slab(ref, comp, pl.ds(start, ny))]
-        total = term if total is None else add(total, term)
-    return total
-
-
-def over_x(nx, body):
-    for x in (0, 1, nx - 2, nx - 1):
-        body(x, True)
-
-    def step(x, carry):
-        body(x, False)
+class Slabs:
+    def __init__(self, x, nx, ny, static):
+        self.x, self.nx, self.ny, self.static = x, nx, ny, static
+
+    def at(self, h, offset=0, row=0):
+        start = (self.x + offset) * self.ny + h * SUB
+        if not self.static:
+            start = pl.multiple_of(start, SUB)
+        return pl.ds(start + row, SUB)
+
+    def load(self, ref, comp, offset=0, row=0):
+        return [
+            [ref[comp, k, self.at(h, offset, row), :] for h in range(self.ny // SUB)]
+            for k in range(ref.shape[1])
+        ]
+
+    def near(self, ref, comp, offset):
+        if self.static and not 0 <= self.x + offset < self.nx:
+            return None
+        return self.load(ref, comp, offset)
+
+    def difference(self, ref, comp, a, b, c, d):
+        total = None
+        for p, q, factor in ((a, b, RATIO), (c, d, None)):
+            p, q = self.near(ref, comp, p), self.near(ref, comp, q)
+            if p is None and q is None:
+                continue
+            if p is None:
+                term = each(lambda f: -f, q)
+            else:
+                term = p if q is None else each(lambda f, g: f - g, p, q)
+            if factor is not None:
+                term = each(lambda f: factor * f, term)
+            total = term if total is None else add(total, term)
+        return total
+
+    def minus(self, ref, comp):
+        return self.difference(ref, comp, 0, -1, 1, -2)
+
+    def plus(self, ref, comp):
+        return self.difference(ref, comp, 1, 0, 2, -1)
+
+
+def run_slabs(begin, end, body):
+    def step(i, carry):
+        body(begin + 2 * i, False)
+        body(begin + 2 * i + 1, False)
         return carry
 
-    lax.fori_loop(2, nx - 2, step, 0)
+    lax.fori_loop(0, (end - begin) // 2, step, 0)
+    if (end - begin) % 2:
+        body(end - 1, True)
+
+
+def over_x(nx, body, parts=1, before=None):
+    for j in range(parts):
+        begin, end = nx * j // parts, nx * (j + 1) // parts
+        if before is not None:
+            before(j)
+        first, last = max(begin, 2), min(end, nx - 2)
+        for x in range(begin, first):
+            body(x, True)
+        run_slabs(first, last, body)
+        for x in range(last, end):
+            body(x, True)
+
+
+LOADS = 4
 
 
 def velocity_body(nx, ny, first, s, v_in, b_in, *refs):
     tiles = s.shape[1]
+    before = None
     if first:
         m_in, v, bd, md, sem = refs
-        copies = to_tiles(b_in, bd, sem.at[3])
-        for c in range(3):
-            copies += to_tiles(v_in.at[c], v.at[c], sem.at[c])
-        late = to_tiles(m_in, md, sem.at[4])
-        for c in copies + late:
+        loads = []
+        for j in range(LOADS):
+            at = pl.ds(nx * j // LOADS * ny, nx // LOADS * ny)
+            pairs = [(b_in, bd)] + [(v_in.at[c], v.at[c]) for c in range(3)]
+            loads.append(
+                [
+                    pltpu.make_async_copy(p.at[at, tile(k)], q.at[k, at], sem.at[4 * j + i, k])
+                    for i, (p, q) in enumerate(pairs)
+                    for k in range(tiles)
+                ]
+            )
+        late = to_tiles(m_in, md, sem.at[4 * LOADS])
+        for c in sum(loads, []) + late:
             c.start()
-        for c in copies:
-            c.wait()
+
+        def before(j):
+            for c in loads[j]:
+                c.wait()
+
     else:
         (v,) = refs
-    cf = Coefs(ny)
+    sh = Shifts(ny)
 
     def body(x, static):
-        start = x * ny if static else pl.multiple_of(x * ny, 8)
-        at = pl.ds(start, ny)
-        xt = functools.partial(x_terms, s, x=x, nx=nx, ny=ny, static=static)
-        sxy, sxz, syz = slab(s, SXY, at), slab(s, SXZ, at), slab(s, SYZ, at)
+        here = Slabs(x, nx, ny, static)
+        sxy, sxz, syz = here.load(s, SXY), here.load(s, SXZ), here.load(s, SYZ)
+        syy = here.load(s, SYY)
         a = (
-            add(xt(SXX, pairs=PLUS), cf.y_minus(sxy), cf.z_minus(sxz)),
-            add(xt(SXY, pairs=MINUS), cf.y_plus(slab(s, SYY, at)), cf.z_minus(syz)),
-            add(xt(SXZ, pairs=MINUS), cf.y_minus(syz), cf.z_plus(slab(s, SZZ, at))),
+            add(here.plus(s, SXX), sh.y_minus(here, s, SXY, sxy), sh.z_minus(sxz)),
+            add(here.minus(s, SXY), sh.y_plus(here, s, SYY, syy), sh.z_minus(syz)),
+            add(here.minus(s, SXZ), sh.y_minus(here, s, SYZ, syz), sh.z_plus(here.load(s, SZZ))),
         )
-        src = v if first else v_in
         for k in range(tiles):
-            if first:
-                w = DT * bd[k, at, :]
-                bd[k, at, :] = w
-            else:
-                w = b_in[k, at, :]
-            for c in range(3):
-                v[c, k, at, :] = src[c, k, at, :] + w * a[c][k]
-
-    over_x(nx, body)
+            for h in range(ny // SUB):
+                at = here.at(h)
+                if first:
+                    w = STEP * bd[k, at, :]
+                    bd[k, at, :] = w
+                else:
+                    w = b_in[k, at, :]
+                for c in range(3):
+                    v[c, k, at, :] = v[c, k, at, :] + w * a[c][k][h]
+
+    over_x(nx, body, LOADS if first else 1, before)
     if first:
         for c in late:
             c.wait()
 
 
-def stress_slabs(nx, ny, v, s_in, s, m_in, md):
-    tiles = s.shape[1]
-    cf = Coefs(ny)
+def stress_slabs(nx, ny, v, s, m_in, md):
+    sh = Shifts(ny)
 
     def body(x, static):
-        start = x * ny if static else pl.multiple_of(x * ny, 8)
-        at = pl.ds(start, ny)
-        xt = functools.partial(x_terms, v, x=x, nx=nx, ny=ny, static=static)
-        vx, vy, vz = slab(v, 0, at), slab(v, 1, at), slab(v, 2, at)
-        exx = xt(0, pairs=MINUS)
-        eyy = cf.y_minus(vy)
-        ezz = cf.z_minus(vz)
-        exy = add(xt(1, pairs=PLUS), cf.y_plus(vx))
-        exz = add(xt(2, pairs=PLUS), cf.z_plus(vx))
-        eyz = add(cf.z_plus(vy), cf.y_plus(vz))
+        here = Slabs(x, nx, ny, static)
+        vx, vy, vz = here.load(v, 0), here.load(v, 1), here.load(v, 2)
+        exx, eyy, ezz = here.minus(v, 0), sh.y_minus(here, v, 1, vy), sh.z_minus(vz)
+        exy = add(here.plus(v, 1), sh.y_plus(here, v, 0, vx))
+        exz = add(here.plus(v, 2), sh.z_plus(vx))
+        eyz = add(sh.z_plus(vy), sh.y_plus(here, v, 2, vz))
         tr = add(exx, eyy, ezz)
-        for k in range(tiles):
-            w = m_in[k, at, :]
-            if md is not None:
-                w = DT * w
-                md[k, at, :] = w
-            s[SXX, k, at, :] = s_in[SXX, k, at, :] + w * (tr[k] + 2.0 * exx[k])
-            s[SYY, k, at, :] = s_in[SYY, k, at, :] + w * (tr[k] + 2.0 * eyy[k])
-            s[SZZ, k, at, :] = s_in[SZZ, k, at, :] + w * (tr[k] + 2.0 * ezz[k])
-            s[SXY, k, at, :] = s_in[SXY, k, at, :] + w * exy[k]
-            s[SXZ, k, at, :] = s_in[SXZ, k, at, :] + w * exz[k]
-            s[SYZ, k, at, :] = s_in[SYZ, k, at, :] + w * eyz[k]
+        for k in range(s.shape[1]):
+            for h in range(ny // SUB):
+                at = here.at(h)
+                w = m_in[k, at, :]
+                if md is not None:
+                    w = STEP * w
+                    md[k, at, :] = w
+                for c, e in ((SXX, exx), (SYY, eyy), (SZZ, ezz)):
+                    s[c, k, at, :] = s[c, k, at, :] + w * (tr[k][h] + 2.0 * e[k][h])
+                for c, e in ((SXY, exy), (SXZ, exz), (SYZ, eyz)):
+                    s[c, k, at, :] = s[c, k, at, :] + w * e[k][h]
 
     return body
 
 
 def stress_body(nx, ny, first, v, s_in, m_in, s, *md):
-    over_x(nx, stress_slabs(nx, ny, v, s_in, s, m_in, md[0] if first else None))
+    del s_in
+    over_x(nx, stress_slabs(nx, ny, v, s, m_in, md[0] if first else None))
 
 
 def last_begin_body(nx, ny, v, s_in, m, back_in, s, back):
     del s_in
-    body = stress_slabs(nx, ny, v, s, s, m, None)
+    body = stress_slabs(nx, ny, v, s, m, None)
     for x in (0, 1, nx - 2, nx - 1):
         body(x, True)
     back[...] = back_in[...]
@@ -279,17 +344,13 @@
         stress_y_terms(s, m, Edges(nx, ny), ny, yl, yh, minus, plus)
     else:
         _, s, s_out, sem = refs
-    body = stress_slabs(nx, ny, v, s, s, m, None)
+    body = stress_slabs(nx, ny, v, s, m, None)
     on_minus, _ = fault_side()
 
-    def step(x, carry):
-        body(x, False)
-        return carry
-
-    width = -(-(end - begin) // 2)
+    width = -(-(end - begin) // 4) * 2
     while begin < end:
         stop = min(begin + width, end)
-        lax.fori_loop(begin, stop, step, 0)
+        run_slabs(begin, stop, body)
         at = pl.ds(begin * ny + ny - 1, stop - begin, stride=ny)
         s[SXY, :, at, :] = jnp.where(on_minus, traction[:, begin:stop, :], s[SXY, :, at, :])
         span = pl.ds(begin * ny, (stop - begin) * ny)
@@ -318,17 +379,17 @@
 
 def minus_edges(n, low, high):
     return (
-        (0, -C1 * low[1] - C2 * low[0]),
-        (1, -C2 * low[1]),
-        (n - 1, C2 * high[0]),
+        (0, -RATIO * low[1] - low[0]),
+        (1, -low[1]),
+        (n - 1, high[0]),
     )
 
 
 def plus_edges(n, low, high):
     return (
-        (0, -C2 * low[0]),
-        (n - 1, C1 * high[0] + C2 * high[1]),
-        (n - 2, C2 * high[0]),
+        (0, -low[0]),
+        (n - 1, RATIO * high[0] + high[1]),
+        (n - 2, high[0]),
     )
 
 
@@ -662,7 +723,7 @@
             v, w, m = call(
                 functools.partial(velocity_body, nx, ny, True), [VMEM, HBM, HBM, HBM],
                 [block_v, block_1, block_1], (s, vel_in, buo_in, mod_in),
-                scratch=[dma(5)], cost=stage_cost, name="velocity_first",
+                scratch=[dma(4 * LOADS + 1)], cost=stage_cost, name="velocity_first",
             )
             while 2 * bit < members:
                 known = merge(known, swap(known, bit), bit)
@@ -689,8 +750,7 @@
             [((4, nt, nx, LANES), VMEM), ((5, nt, nx, LANES), VMEM)], (v,), cost=side_cost,
             name="pack_normal",
         )
-        if not last:
-            yl, yh = shift_up(yu, "normal"), shift_down(yd, "normal")
+        yl, yh = shift_up(yu, "normal"), shift_down(yd, "normal")
         outs = [block_v, ((4, nt, ny, LANES), VMEM), ((5, nt, ny, LANES), VMEM)] + [row_1] * 4
         if last:
             outs.append(((2, nt, nx // 2, LANES), VMEM))
@@ -699,9 +759,6 @@
             (mine, other, traction, par, state, v), aliases={5: 0}, cost=side_cost, name="fault",
         )
         v, xu, xd, state, minus, plus, trac_new = got[:7]
-        if last:
-            xu, xd, yu, yd = tie((xu, xd, yu, yd))
-            yl, yh = shift_up(yu, "normal"), shift_down(yd, "normal")
         xl, xh = shift_up(xu, "strike"), shift_down(xd, "strike")
         body = functools.partial(stress_body, nx, ny, first)
         if last:
@@ -709,7 +766,7 @@
             back, holders = got[7], [members // 2 - 1, members // 2]
             s, back = call(
                 functools.partial(last_begin_body, nx, ny), [VMEM] * 4, [block_s, half_rows],
-                (v, s, m, back), aliases={1: 0}, cost=side_cost,
+                (v, s, m, back), aliases={1: 0}, cost=stage_cost,
                 name="last_begin",
             )
             edges, bits = [2], []

time: 85.3 us -> 81 us (0.950)
  Pallas kernels: 31.9 us -> 27.4 us
  starting transfers between devices: 45.5 us -> 47.1 us
  waiting for transfers between devices: 6.6 us -> 5.36 us
    pallas_call x22, Pallas kernels: 31.9 us -> 27.4 us  [call(): pl.pallas_call(body, out_shape=shapes, in_specs=ins, out_specs=[spec for...]
    ppermute x7, starting transfers between devices: 10.5 us -> 12.5 us  [swap(): return lax.ppermute(x, 'normal', [(i, i ^ bit) for i in range(count)])]
    ppermute x2, waiting for transfers between devices: 1.68 us -> 0.01 us  [swap_odd(): return lax.ppermute(x, axis, pairs)]
    ppermute x8, starting transfers between devices: 31.3 us -> 30.3 us  [shift_down(): return lax.ppermute(x, axis, [((i + 1) % count, i) for i in range(count)])]
  transfers between devices with their start and end apart: 25 -> 25, of which waited for: 3 -> 4; matrix products, arithmetic and copies ran while one was open for 0% -> 0% of each run, Pallas kernels for 32% -> 29%
where the time goes in v3:
time: 81 us; the launch traced here: 80.9 us
  starting transfers between devices  47.1 us (58%)
  Pallas kernels  27.4 us (34%)
  waiting for transfers between devices  5.36 us (7%)
  between operations  1.05 us (1%)
    ppermute x8, starting transfers between devices, shift_down(): return lax.ppermute(x, axis, [((i + 1) % count, i) for i in range(count)])  30.3 us
    pallas_call x22, Pallas kernels, call(): pl.pallas_call(body, out_shape=shapes, in_specs=ins, out_specs=[spec for...  27.4 us
    ppermute x7, starting transfers between devices, swap(): return lax.ppermute(x, 'normal', [(i, i ^ bit) for i in range(count)])  12.5 us
    ppermute x7, waiting for transfers between devices, swap(): return lax.ppermute(x, 'normal', [(i, i ^ bit) for i in range(count)])  4.7 us
    ppermute x8, starting transfers between devices, shift_up(): return lax.ppermute(x, axis, [(i, (i + 1) % count) for i in range(count)])  2.2 us
    ppermute x2, starting transfers between devices, swap_odd(): return lax.ppermute(x, axis, pairs)  2.05 us
  transfers between devices with their start and end apart: 25, of which 4 were waited for; matrix products, arithmetic and copies ran while one was open for 0% of the time, Pallas kernels for 29%

profile of v3, /device:TPU:1, one launch (start us, length us, event | category | flops | bytes accessed | tf_op | source)
XLA Modules:
  0.0 80.9 jit_solution(9172930477071279495)
XLA Ops:
  1.4 1.5 %collective-permute-start = (f32[1,8,384]{2,1,0:T(8,128)S(1)}, f32[1,8,384]{2,1,0:T(8,128)S(1)}, u32[]{:S(2)}, u32[]{:S(2)}) collective-permute-start(f32[1,8,384]{2,1,0:T(8,128)S(1)} %own.1.mine), channel_id=1, source_target_pairs={{0,1},{1,0},{2,3},{3,2},{4,5},{5,4},{6,7},{7,6},{8,9},{9,8},{10,11... | collective-permute-start | bytes 36872 | tf_op jit(solution)/shard_map/ppermute | solution.py:44
  2.9 2.5 %load.1 = (f32[6,3,512,128]{3,2,1,0:T(8,128)S(1)}, f32[5,3,16,128]{3,2,1,0:T(8,128)S(1)}, f32[4,3,16,128]{3,2,1,0:T(8,128)S(1)}, f32[5,3,32,128]{3,2,1,0:T(8,128)S(1)}, f32[4,3,32,128]{3,2,1,0:T(8,128)S(1)}) custom-call(f32[6,512,384]{2,1,0:T(8,128)} %bitcast.7), custom_call_target="tpu_custom_call" | custom-call | flops 1000000 | bytes 1000000 | tf_op jit(solution)/shard_map/load/pallas_call | solution.py:57
  5.4 1.5 %collective-permute-start.1 = (f32[2,8,384]{2,1,0:T(8,128)S(1)}, f32[2,8,384]{2,1,0:T(8,128)S(1)}, u32[]{:S(2)}, u32[]{:S(2)}) collective-permute-start(f32[2,8,384]{2,1,0:T(8,128)S(1)} %merge.3.mine), channel_id=1, source_target_pairs={{0,2},{1,3},{2,0},{3,1},{4,6},{5,7},{6,4},{7,5},{8,10},{9,11},{10,... | collective-permute-start | bytes 73736 | tf_op jit(solution)/shard_map/ppermute | solution.py:44
  6.9 6.2 %collective-permute-start.4 = (f32[4,3,16,128]{3,2,1,0:T(8,128)S(1)}, f32[4,3,16,128]{3,2,1,0:T(8,128)S(1)}, u32[]{:S(2)}, u32[]{:S(2)}) collective-permute-start(f32[4,3,16,128]{3,2,1,0:T(8,128)S(1)} %get-tuple-element.78), channel_id=1, source_target_pairs={{16,0},{32,16},{48,32},{64,48},{80,64},{96,80},{112,96},{0,112},{1... | collective-permute-start | bytes 294920 | tf_op jit(solution)/shard_map/ppermute | solution.py:30
  13.7 1.2 %collective-permute-start.5 = (f32[5,3,32,128]{3,2,1,0:T(8,128)S(1)}, f32[5,3,32,128]{3,2,1,0:T(8,128)S(1)}, u32[]{:S(2)}, u32[]{:S(2)}) collective-permute-start(f32[5,3,32,128]{3,2,1,0:T(8,128)S(1)} %get-tuple-element.79), channel_id=1, source_target_pairs={{0,1},{1,2},{2,3},{3,4},{4,5},{5,6},{6,7},{7,8},{8,9},{9,10},{10,1... | collective-permute-start | bytes 737288 | tf_op jit(solution)/shard_map/ppermute | solution.py:25
  14.9 2.7 %collective-permute-start.2 = (f32[4,8,384]{2,1,0:T(8,128)S(1)}, f32[4,8,384]{2,1,0:T(8,128)S(1)}, u32[]{:S(2)}, u32[]{:S(2)}) collective-permute-start(f32[4,8,384]{2,1,0:T(8,128)S(1)} %merge.4.mine), channel_id=1, source_target_pairs={{0,4},{1,5},{2,6},{3,7},{4,0},{5,1},{6,2},{7,3},{8,12},{9,13},{10,... | collective-permute-start | bytes 147464 | tf_op jit(solution)/shard_map/ppermute | solution.py:44
  17.6 5.0 %velocity_first.1 = (f32[3,3,512,128]{3,2,1,0:T(8,128)S(1)}, f32[3,512,128]{2,1,0:T(8,128)S(1)}, f32[3,512,128]{2,1,0:T(8,128)S(1)}) custom-call(f32[6,3,512,128]{3,2,1,0:T(8,128)S(1)} %get-tuple-element.73.s.s_in, f32[3,512,384]{2,1,0:T(8,128)} %bitcast.8, f32[512,384]{1,0:T(8,128)} %bitcast.10, f32[512,384]{1,0:T(8,128)} %bitcast.11), custom_call_target="tpu_custom_call" | custom-call | flops 4000000000 | bytes 16000000 | tf_op jit(solution)/shard_map/velocity_first/pallas_call | solution.py:57
  23.8 3.7 %collective-permute-done.8.got = f32[8,8,384]{2,1,0:T(8,128)S(1)} collective-permute-done((f32[8,8,384]{2,1,0:T(8,128)S(1)}, f32[8,8,384]{2,1,0:T(8,128)S(1)}, u32[]{:S(2)}, u32[]{:S(2)}) %collective-permute-start.8) | collective-permute-done | bytes 98336 | tf_op jit(solution)/shard_map/ppermute | solution.py:44
  30.3 4.8 %collective-permute-start.10 = (f32[5,3,16,128]{3,2,1,0:T(8,128)S(1)}, f32[5,3,16,128]{3,2,1,0:T(8,128)S(1)}, u32[]{:S(2)}, u32[]{:S(2)}) collective-permute-start(f32[5,3,16,128]{3,2,1,0:T(8,128)S(1)} %get-tuple-element.92), channel_id=1, source_target_pairs={{16,0},{32,16},{48,32},{64,48},{80,64},{96,80},{112,96},{0,112},{1... | collective-permute-start | bytes 368648 | tf_op jit(solution)/shard_map/ppermute | solution.py:30
  35.1 3.4 %stress_first.1 = (f32[6,3,512,128]{3,2,1,0:T(8,128)S(1)}, f32[3,512,128]{2,1,0:T(8,128)S(1)}) custom-call(f32[3,3,512,128]{3,2,1,0:T(8,128)S(1)} %get-tuple-element.87.v.v_in, f32[6,3,512,128]{3,2,1,0:T(8,128)S(1)} %get-tuple-element.73.s.s_in, f32[3,512,128]{2,1,0:T(8,128)S(1)} %get-tuple-element.88.m_in), custom_call_target="tpu_custom_call", output_to_operand_aliasing={{0}: (1, {}), {1}: (2, {})} | custom-call | flops 4000000000 | bytes 16000000 | tf_op jit(solution)/shard_map/stress_first/pallas_call | solution.py:57
  38.5 1.0 %stress_edges.1 = (f32[6,3,512,128]{3,2,1,0:T(8,128)S(1)}, f32[5,3,16,128]{3,2,1,0:T(8,128)S(1)}, f32[4,3,16,128]{3,2,1,0:T(8,128)S(1)}, f32[5,3,32,128]{3,2,1,0:T(8,128)S(1)}, f32[4,3,32,128]{3,2,1,0:T(8,128)S(1)}) custom-call(f32[6,3,512,128]{3,2,1,0:T(8,128)S(1)} %get-tuple-element.89.s_in, ...), custom_call_target="tpu_custom_call", output_to_operand_aliasing={{0}: (0, {})} | custom-call | flops 1000000 | bytes 1000000 | tf_op jit(solution)/shard_map/stress_edges/pallas_call | solution.py:57
  39.6 5.3 %collective-permute-start.14 = (f32[4,3,16,128]{3,2,1,0:T(8,128)S(1)}, f32[4,3,16,128]{3,2,1,0:T(8,128)S(1)}, u32[]{:S(2)}, u32[]{:S(2)}) collective-permute-start(f32[4,3,16,128]{3,2,1,0:T(8,128)S(1)} %get-tuple-element.100), channel_id=1, source_target_pairs={{16,0},{32,16},{48,32},{64,48},{80,64},{96,80},{112,96},{0,112},{1... | collective-permute-start | bytes 294920 | tf_op jit(solution)/shard_map/ppermute | solution.py:30
  44.9 4.3 %collective-permute-start.16 = (f32[4,3,32,128]{3,2,1,0:T(8,128)S(1)}, f32[4,3,32,128]{3,2,1,0:T(8,128)S(1)}, u32[]{:S(2)}, u32[]{:S(2)}) collective-permute-start(f32[4,3,32,128]{3,2,1,0:T(8,128)S(1)} %get-tuple-element.102), channel_id=1, source_target_pairs={{1,0},{2,1},{3,2},{4,3},{5,4},{6,5},{7,6},{8,7},{9,8},{10,9},{11,1... | collective-permute-start | bytes 589832 | tf_op jit(solution)/shard_map/ppermute | solution.py:30
  49.3 3.3 %velocity.1.v_in = f32[3,3,512,128]{3,2,1,0:T(8,128)S(1)} custom-call(f32[6,3,512,128]{3,2,1,0:T(8,128)S(1)} %get-tuple-element.98.s.s_in, f32[3,3,512,128]{3,2,1,0:T(8,128)S(1)} %get-tuple-element.87.v.v_in, f32[3,512,128]{2,1,0:T(8,128)S(1)} %get-tuple-element.76.w.b_in), custom_call_target="tpu_custom_call", output_to_operand_aliasing={{}: (1, {})} | custom-call | flops 4000000000 | bytes 16000000 | tf_op jit(solution)/shard_map/velocity/pallas_call | solution.py:57
  53.8 2.0 %collective-permute-start.17 = (f32[3,32,128]{2,1,0:T(8,128)S(1)}, f32[3,32,128]{2,1,0:T(8,128)S(1)}, u32[]{:S(2)}, u32[]{:S(2)}) collective-permute-start(f32[3,32,128]{2,1,0:T(8,128)S(1)} %get-tuple-element.103.refs_0_), channel_id=1, source_target_pairs={{1,2},{2,1},{3,4},{4,3},{5,6},{6,5},{7,8},{8,7},{9,10},{10,9},{11,... | collective-permute-start | bytes 147464 | tf_op jit(solution)/shard_map/ppermute | solution.py:39
  56.1 3.5 %collective-permute-start.19 = (f32[5,3,32,128]{3,2,1,0:T(8,128)S(1)}, f32[5,3,32,128]{3,2,1,0:T(8,128)S(1)}, u32[]{:S(2)}, u32[]{:S(2)}) collective-permute-start(f32[5,3,32,128]{3,2,1,0:T(8,128)S(1)} %get-tuple-element.112), channel_id=1, source_target_pairs={{1,0},{2,1},{3,2},{4,3},{5,4},{6,5},{7,6},{8,7},{9,8},{10,9},{11,1... | collective-permute-start | bytes 737288 | tf_op jit(solution)/shard_map/ppermute | solution.py:30
  59.5 1.1 %fault.3 = (f32[3,3,512,128]{3,2,1,0:T(8,128)S(1)}, f32[4,3,16,128]{3,2,1,0:T(8,128)S(1)}, f32[5,3,16,128]{3,2,1,0:T(8,128)S(1)}, f32[3,32,128]{2,1,0:T(8,128)},...) custom-call(f32[3,32,128]{2,1,0:T(8,128)S(1)} %get-tuple-element.103, ...), custom_call_target="tpu_custom_call", output_to_operand_aliasing={{0}: (5, {})} | custom-call | flops 1000000 | bytes 1000000 | tf_op jit(solution)/shard_map/fault/pallas_call | solution.py:57
  61.6 5.1 %collective-permute-start.23 = (f32[5,3,16,128]{3,2,1,0:T(8,128)S(1)}, f32[5,3,16,128]{3,2,1,0:T(8,128)S(1)}, u32[]{:S(2)}, u32[]{:S(2)}) collective-permute-start(f32[5,3,16,128]{3,2,1,0:T(8,128)S(1)} %get-tuple-element.124), channel_id=1, source_target_pairs={{16,0},{32,16},{48,32},{64,48},{80,64},{96,80},{112,96},{0,112},{1... | collective-permute-start | bytes 368648 | tf_op jit(solution)/shard_map/ppermute | solution.py:30
  66.7 3.3 %last_slabs_0.1 = (f32[6,3,512,128]{3,2,1,0:T(8,128)S(1)}, f32[6,512,384]{2,1,0:T(8,128)}, f32[3,512,384]{2,1,0:T(8,128)}) custom-call(f32[3,3,512,128]{3,2,1,0:T(8,128)S(1)} %get-tuple-element.107.v, f32[6,3,512,128]{3,2,1,0:T(8,128)S(1)} %get-tuple-element.109.s_in, f32[3,512,128]{2,1,0:T(8,128)S(1)} %get-tuple-element.90.w.m, ...), custom_call_target="tpu_custom_call", output_to_operand_aliasing={{0}: (1, {})} | custom-call | flops 2000000000 | bytes 8000000 | tf_op jit(solution)/shard_map/last_slabs_0/pallas_call | solution.py:57
  70.0 4.1 %collective-permute-start.21 = (f32[2,3,16,128]{3,2,1,0:T(8,128)S(1)}, f32[2,3,16,128]{3,2,1,0:T(8,128)S(1)}, u32[]{:S(2)}, u32[]{:S(2)}) collective-permute-start(f32[2,3,16,128]{3,2,1,0:T(8,128)S(1)} %choose.2.mine), channel_id=1, source_target_pairs={{0,2},{1,3},{2,0},{3,1},{4,6},{5,7},{6,4},{7,5},{8,10},{9,11},{10,... | collective-permute-start | bytes 147464 | tf_op jit(solution)/shard_map/ppermute | solution.py:44
  74.1 2.7 %last_slabs_1.1 = (f32[6,3,512,128]{3,2,1,0:T(8,128)S(1)}, f32[6,512,384]{2,1,0:T(8,128)}) custom-call(f32[3,3,512,128]{3,2,1,0:T(8,128)S(1)} %get-tuple-element.107.v, f32[6,3,512,128]{3,2,1,0:T(8,128)S(1)} %get-tuple-element.119.s_in, f32[3,512,128]{2,1,0:T(8,128)S(1)} %get-tuple-element.90.w.m, ...), custom_call_target="tpu_custom_call", output_to_operand_aliasing={{0}: (1, {}), {1}: (4, {})} | custom-call | flops 2000000000 | bytes 8000000 | tf_op jit(solution)/shard_map/last_slabs_1/pallas_call | solution.py:57
  76.8 1.9 %collective-permute-start.24 = (f32[2,3,16,128]{3,2,1,0:T(8,128)S(1)}, f32[2,3,16,128]{3,2,1,0:T(8,128)S(1)}, u32[]{:S(2)}, u32[]{:S(2)}) collective-permute-start(f32[2,3,16,128]{3,2,1,0:T(8,128)S(1)} %choose.3.mine), channel_id=1, source_target_pairs={{0,1},{1,0},{2,3},{3,2},{4,5},{5,4},{6,7},{7,6},{8,9},{9,8},{10,11... | collective-permute-start | bytes 147464 | tf_op jit(solution)/shard_map/ppermute | solution.py:44
  78.7 0.9 %collective-permute-done.24.got = f32[2,3,16,128]{3,2,1,0:T(8,128)S(1)} collective-permute-done((f32[2,3,16,128]{3,2,1,0:T(8,128)S(1)}, f32[2,3,16,128]{3,2,1,0:T(8,128)S(1)}, u32[]{:S(2)}, u32[]{:S(2)}) %collective-permute-start.24) | collective-permute-done | bytes 49184 | tf_op jit(solution)/shard_map/ppermute | solution.py:44
  79.5 1.2 %edges_last.1 = (f32[6,512,384]{2,1,0:T(8,128)}, f32[2,384]{1,0:T(2,128)}, f32[2,384]{1,0:T(2,128)}) custom-call(f32[6,3,512,128]{3,2,1,0:T(8,128)S(1)} %get-tuple-element.122.s, f32[3,512,128]{2,1,0:T(8,128)S(1)} %get-tuple-element.90.w.m, f32[4,3,16,128]{3,2,1,0:T(8,128)S(1)} %collective-permute-done.22.xl, ...), custom_call_target="tpu_custom_call", output_to_operand_aliasing={{0}: (7, {})} | custom-call | flops 1000000 | bytes 1000000 | tf_op jit(solution)/shard_map/edges_last/pallas_call | solution.py:57
  (50 shorter events, 7.9 us)
Async XLA Ops:
  1.4 4.0 %collective-permute-start = (f32[1,8,384]{2,1,0:T(8,128)S(1)}, f32[1,8,384]{2,1,0:T(8,128)S(1)}, u32[]{:S(2)}, u32[]{:S(2)}) collective-permute-start(f32[1,8,384]{2,1,0:T(8,128)S(1)} %own.1.mine), channel_id=1, source_target_pairs={{0,1},{1,0},{2,3},{3,2},{4,5},{5,4},{6,7},{7,6},{8,9},{9,8},{10,11... | collective-permute-start | bytes 36872 | tf_op jit(solution)/shard_map/ppermute | solution.py:44
  5.4 9.4 %collective-permute-start.1 = (f32[2,8,384]{2,1,0:T(8,128)S(1)}, f32[2,8,384]{2,1,0:T(8,128)S(1)}, u32[]{:S(2)}, u32[]{:S(2)}) collective-permute-start(f32[2,8,384]{2,1,0:T(8,128)S(1)} %merge.3.mine), channel_id=1, source_target_pairs={{0,2},{1,3},{2,0},{3,1},{4,6},{5,7},{6,4},{7,5},{8,10},{9,11},{10,... | collective-permute-start | bytes 73736 | tf_op jit(solution)/shard_map/ppermute | solution.py:44
  6.9 16.1 %collective-permute-start.4 = (f32[4,3,16,128]{3,2,1,0:T(8,128)S(1)}, f32[4,3,16,128]{3,2,1,0:T(8,128)S(1)}, u32[]{:S(2)}, u32[]{:S(2)}) collective-permute-start(f32[4,3,16,128]{3,2,1,0:T(8,128)S(1)} %get-tuple-element.78), channel_id=1, source_target_pairs={{16,0},{32,16},{48,32},{64,48},{80,64},{96,80},{112,96},{0,112},{1... | collective-permute-start | bytes 294920 | tf_op jit(solution)/shard_map/ppermute | solution.py:30
  13.1 9.9 %collective-permute-start.3 = (f32[5,3,16,128]{3,2,1,0:T(8,128)S(1)}, f32[5,3,16,128]{3,2,1,0:T(8,128)S(1)}, u32[]{:S(2)}, u32[]{:S(2)}) collective-permute-start(f32[5,3,16,128]{3,2,1,0:T(8,128)S(1)} %get-tuple-element.77), channel_id=1, source_target_pairs={{0,16},{16,32},{32,48},{48,64},{64,80},{80,96},{96,112},{112,0},{1... | collective-permute-start | bytes 368648 | tf_op jit(solution)/shard_map/ppermute | solution.py:25
  13.1 9.9 %collective-permute-start.6 = (f32[4,3,32,128]{3,2,1,0:T(8,128)S(1)}, f32[4,3,32,128]{3,2,1,0:T(8,128)S(1)}, u32[]{:S(2)}, u32[]{:S(2)}) collective-permute-start(f32[4,3,32,128]{3,2,1,0:T(8,128)S(1)} %get-tuple-element.80), channel_id=1, source_target_pairs={{1,0},{2,1},{3,2},{4,3},{5,4},{6,5},{7,6},{8,7},{9,8},{10,9},{11,1... | collective-permute-start | bytes 589832 | tf_op jit(solution)/shard_map/ppermute | solution.py:30
  13.7 9.3 %collective-permute-start.5 = (f32[5,3,32,128]{3,2,1,0:T(8,128)S(1)}, f32[5,3,32,128]{3,2,1,0:T(8,128)S(1)}, u32[]{:S(2)}, u32[]{:S(2)}) collective-permute-start(f32[5,3,32,128]{3,2,1,0:T(8,128)S(1)} %get-tuple-element.79), channel_id=1, source_target_pairs={{0,1},{1,2},{2,3},{3,4},{4,5},{5,6},{6,7},{7,8},{8,9},{9,10},{10,1... | collective-permute-start | bytes 737288 | tf_op jit(solution)/shard_map/ppermute | solution.py:25
  14.9 7.8 %collective-permute-start.2 = (f32[4,8,384]{2,1,0:T(8,128)S(1)}, f32[4,8,384]{2,1,0:T(8,128)S(1)}, u32[]{:S(2)}, u32[]{:S(2)}) collective-permute-start(f32[4,8,384]{2,1,0:T(8,128)S(1)} %merge.4.mine), channel_id=1, source_target_pairs={{0,4},{1,5},{2,6},{3,7},{4,0},{5,1},{6,2},{7,3},{8,12},{9,13},{10,... | collective-permute-start | bytes 147464 | tf_op jit(solution)/shard_map/ppermute | solution.py:44
  22.7 4.8 %collective-permute-start.8 = (f32[8,8,384]{2,1,0:T(8,128)S(1)}, f32[8,8,384]{2,1,0:T(8,128)S(1)}, u32[]{:S(2)}, u32[]{:S(2)}) collective-permute-start(f32[8,8,384]{2,1,0:T(8,128)S(1)} %merge.5.mine), channel_id=1, source_target_pairs={{0,8},{1,9},{2,10},{3,11},{4,12},{5,13},{6,14},{7,15},{8,0},{9,1},... | collective-permute-start | bytes 294920 | tf_op jit(solution)/shard_map/ppermute | solution.py:44
  23.7 5.3 %collective-permute-start.7 = (f32[3,32,128]{2,1,0:T(8,128)S(1)}, f32[3,32,128]{2,1,0:T(8,128)S(1)}, u32[]{:S(2)}, u32[]{:S(2)}) collective-permute-start(f32[3,32,128]{2,1,0:T(8,128)S(1)} %get-tuple-element.81.refs_0_), channel_id=1, source_target_pairs={{1,2},{2,1},{3,4},{4,3},{5,6},{6,5},{7,8},{8,7},{9,10},{10,9},{11,... | collective-permute-start | bytes 147464 | tf_op jit(solution)/shard_map/ppermute | solution.py:39
  28.4 10.1 %collective-permute-start.11 = (f32[4,3,32,128]{3,2,1,0:T(8,128)S(1)}, f32[4,3,32,128]{3,2,1,0:T(8,128)S(1)}, u32[]{:S(2)}, u32[]{:S(2)}) collective-permute-start(f32[4,3,32,128]{3,2,1,0:T(8,128)S(1)} %get-tuple-element.93), channel_id=1, source_target_pairs={{0,1},{1,2},{2,3},{3,4},{4,5},{5,6},{6,7},{7,8},{8,9},{9,10},{10,1... | collective-permute-start | bytes 589832 | tf_op jit(solution)/shard_map/ppermute | solution.py:25
  28.5 10.1 %collective-permute-start.12 = (f32[5,3,32,128]{3,2,1,0:T(8,128)S(1)}, f32[5,3,32,128]{3,2,1,0:T(8,128)S(1)}, u32[]{:S(2)}, u32[]{:S(2)}) collective-permute-start(f32[5,3,32,128]{3,2,1,0:T(8,128)S(1)} %get-tuple-element.94), channel_id=1, source_target_pairs={{1,0},{2,1},{3,2},{4,3},{5,4},{6,5},{7,6},{8,7},{9,8},{10,9},{11,1... | collective-permute-start | bytes 737288 | tf_op jit(solution)/shard_map/ppermute | solution.py:30
  29.5 9.0 %collective-permute-start.9 = (f32[4,3,16,128]{3,2,1,0:T(8,128)S(1)}, f32[4,3,16,128]{3,2,1,0:T(8,128)S(1)}, u32[]{:S(2)}, u32[]{:S(2)}) collective-permute-start(f32[4,3,16,128]{3,2,1,0:T(8,128)S(1)} %get-tuple-element.91), channel_id=1, source_target_pairs={{0,16},{16,32},{32,48},{48,64},{64,80},{80,96},{96,112},{112,0},{1... | collective-permute-start | bytes 294920 | tf_op jit(solution)/shard_map/ppermute | solution.py:25
  30.3 8.2 %collective-permute-start.10 = (f32[5,3,16,128]{3,2,1,0:T(8,128)S(1)}, f32[5,3,16,128]{3,2,1,0:T(8,128)S(1)}, u32[]{:S(2)}, u32[]{:S(2)}) collective-permute-start(f32[5,3,16,128]{3,2,1,0:T(8,128)S(1)} %get-tuple-element.92), channel_id=1, source_target_pairs={{16,0},{32,16},{48,32},{64,48},{80,64},{96,80},{112,96},{0,112},{1... | collective-permute-start | bytes 368648 | tf_op jit(solution)/shard_map/ppermute | solution.py:30
  39.6 13.0 %collective-permute-start.14 = (f32[4,3,16,128]{3,2,1,0:T(8,128)S(1)}, f32[4,3,16,128]{3,2,1,0:T(8,128)S(1)}, u32[]{:S(2)}, u32[]{:S(2)}) collective-permute-start(f32[4,3,16,128]{3,2,1,0:T(8,128)S(1)} %get-tuple-element.100), channel_id=1, source_target_pairs={{16,0},{32,16},{48,32},{64,48},{80,64},{96,80},{112,96},{0,112},{1... | collective-permute-start | bytes 294920 | tf_op jit(solution)/shard_map/ppermute | solution.py:30
  44.9 8.3 %collective-permute-start.13 = (f32[5,3,16,128]{3,2,1,0:T(8,128)S(1)}, f32[5,3,16,128]{3,2,1,0:T(8,128)S(1)}, u32[]{:S(2)}, u32[]{:S(2)}) collective-permute-start(f32[5,3,16,128]{3,2,1,0:T(8,128)S(1)} %get-tuple-element.99), channel_id=1, source_target_pairs={{0,16},{16,32},{32,48},{48,64},{64,80},{80,96},{96,112},{112,0},{1... | collective-permute-start | bytes 368648 | tf_op jit(solution)/shard_map/ppermute | solution.py:25
  44.9 8.3 %collective-permute-start.16 = (f32[4,3,32,128]{3,2,1,0:T(8,128)S(1)}, f32[4,3,32,128]{3,2,1,0:T(8,128)S(1)}, u32[]{:S(2)}, u32[]{:S(2)}) collective-permute-start(f32[4,3,32,128]{3,2,1,0:T(8,128)S(1)} %get-tuple-element.102), channel_id=1, source_target_pairs={{1,0},{2,1},{3,2},{4,3},{5,4},{6,5},{7,6},{8,7},{9,8},{10,9},{11,1... | collective-permute-start | bytes 589832 | tf_op jit(solution)/shard_map/ppermute | solution.py:30
  49.3 3.9 %collective-permute-start.15 = (f32[5,3,32,128]{3,2,1,0:T(8,128)S(1)}, f32[5,3,32,128]{3,2,1,0:T(8,128)S(1)}, u32[]{:S(2)}, u32[]{:S(2)}) collective-permute-start(f32[5,3,32,128]{3,2,1,0:T(8,128)S(1)} %get-tuple-element.101), channel_id=1, source_target_pairs={{0,1},{1,2},{2,3},{3,4},{4,5},{5,6},{6,7},{7,8},{8,9},{9,10},{10,1... | collective-permute-start | bytes 737288 | tf_op jit(solution)/shard_map/ppermute | solution.py:25
  53.8 5.7 %collective-permute-start.17 = (f32[3,32,128]{2,1,0:T(8,128)S(1)}, f32[3,32,128]{2,1,0:T(8,128)S(1)}, u32[]{:S(2)}, u32[]{:S(2)}) collective-permute-start(f32[3,32,128]{2,1,0:T(8,128)S(1)} %get-tuple-element.103.refs_0_), channel_id=1, source_target_pairs={{1,2},{2,1},{3,4},{4,3},{5,6},{6,5},{7,8},{8,7},{9,10},{10,9},{11,... | collective-permute-start | bytes 147464 | tf_op jit(solution)/shard_map/ppermute | solution.py:39
  55.9 10.7 %collective-permute-start.18 = (f32[4,3,32,128]{3,2,1,0:T(8,128)S(1)}, f32[4,3,32,128]{3,2,1,0:T(8,128)S(1)}, u32[]{:S(2)}, u32[]{:S(2)}) collective-permute-start(f32[4,3,32,128]{3,2,1,0:T(8,128)S(1)} %get-tuple-element.111), channel_id=1, source_target_pairs={{0,1},{1,2},{2,3},{3,4},{4,5},{5,6},{6,7},{7,8},{8,9},{9,10},{10,1... | collective-permute-start | bytes 589832 | tf_op jit(solution)/shard_map/ppermute | solution.py:25
  56.1 10.6 %collective-permute-start.19 = (f32[5,3,32,128]{3,2,1,0:T(8,128)S(1)}, f32[5,3,32,128]{3,2,1,0:T(8,128)S(1)}, u32[]{:S(2)}, u32[]{:S(2)}) collective-permute-start(f32[5,3,32,128]{3,2,1,0:T(8,128)S(1)} %get-tuple-element.112), channel_id=1, source_target_pairs={{1,0},{2,1},{3,2},{4,3},{5,4},{6,5},{7,6},{8,7},{9,8},{10,9},{11,1... | collective-permute-start | bytes 737288 | tf_op jit(solution)/shard_map/ppermute | solution.py:30
  61.0 9.0 %collective-permute-start.20 = (f32[2,3,16,128]{3,2,1,0:T(8,128)S(1)}, f32[2,3,16,128]{3,2,1,0:T(8,128)S(1)}, u32[]{:S(2)}, u32[]{:S(2)}) collective-permute-start(f32[2,3,16,128]{3,2,1,0:T(8,128)S(1)} %get-tuple-element.116.mine), channel_id=1, source_target_pairs={{0,4},{1,5},{2,6},{3,7},{4,0},{5,1},{6,2},{7,3},{8,12},{9,13},{10,... | collective-permute-start | bytes 147464 | tf_op jit(solution)/shard_map/ppermute | solution.py:44
  61.6 17.1 %collective-permute-start.22 = (f32[4,3,16,128]{3,2,1,0:T(8,128)S(1)}, f32[4,3,16,128]{3,2,1,0:T(8,128)S(1)}, u32[]{:S(2)}, u32[]{:S(2)}) collective-permute-start(f32[4,3,16,128]{3,2,1,0:T(8,128)S(1)} %get-tuple-element.123), channel_id=1, source_target_pairs={{0,16},{16,32},{32,48},{48,64},{64,80},{80,96},{96,112},{112,0},{1... | collective-permute-start | bytes 294920 | tf_op jit(solution)/shard_map/ppermute | solution.py:25
  61.6 17.1 %collective-permute-start.23 = (f32[5,3,16,128]{3,2,1,0:T(8,128)S(1)}, f32[5,3,16,128]{3,2,1,0:T(8,128)S(1)}, u32[]{:S(2)}, u32[]{:S(2)}) collective-permute-start(f32[5,3,16,128]{3,2,1,0:T(8,128)S(1)} %get-tuple-element.124), channel_id=1, source_target_pairs={{16,0},{32,16},{48,32},{64,48},{80,64},{96,80},{112,96},{0,112},{1... | collective-permute-start | bytes 368648 | tf_op jit(solution)/shard_map/ppermute | solution.py:30
  70.0 6.8 %collective-permute-start.21 = (f32[2,3,16,128]{3,2,1,0:T(8,128)S(1)}, f32[2,3,16,128]{3,2,1,0:T(8,128)S(1)}, u32[]{:S(2)}, u32[]{:S(2)}) collective-permute-start(f32[2,3,16,128]{3,2,1,0:T(8,128)S(1)} %choose.2.mine), channel_id=1, source_target_pairs={{0,2},{1,3},{2,0},{3,1},{4,6},{5,7},{6,4},{7,5},{8,10},{9,11},{10,... | collective-permute-start | bytes 147464 | tf_op jit(solution)/shard_map/ppermute | solution.py:44
  (2 other events, 7.7 us)

commit v4 on v3

--- a/solution.py
+++ b/solution.py
@@ -324,44 +324,46 @@
     over_x(nx, stress_slabs(nx, ny, v, s, m_in, md[0] if first else None))
 
 
-def last_begin_body(nx, ny, v, s_in, m, back_in, s, back):
+def slabs_out(ny, begin, end, s, out, sems):
+    span = pl.ds(begin * ny, (end - begin) * ny)
+    return [
+        pltpu.make_async_copy(s.at[c, k, span], out.at[c, span, tile(k)], sems.at[c, k])
+        for c in range(s.shape[0])
+        for k in range(s.shape[1])
+    ]
+
+
+def last_slabs_body(nx, ny, part, before, begin, end, v, s_in, m, traction, *refs):
     del s_in
-    body = stress_slabs(nx, ny, v, s, m, None)
-    for x in (0, 1, nx - 2, nx - 1):
-        body(x, True)
-    back[...] = back_in[...]
-
-
-def last_slabs_body(nx, ny, begin, end, first, v, s_in, m, traction, *refs):
-    del s_in
-    out = []
-    if first:
-        yl, yh, minus, plus, s, s_out, v_out, sem = refs
+    e = Edges(nx, ny)
+    on_minus, _ = fault_side()
+
+    def fault_rows(begin, end):
+        at = pl.ds(begin * ny + ny - 1, end - begin, stride=ny)
+        s[SXY, :, at, :] = jnp.where(on_minus, traction[:, begin:end, :], s[SXY, :, at, :])
+
+    if part == 0:
+        s, v_out, sem = refs
+        out = []
         for c in range(3):
-            out += from_tiles(v.at[c], v_out.at[c], sem.at[6 + c])
+            out += from_tiles(v.at[c], v_out.at[c], sem.at[c])
         for c in out:
             c.start()
-        stress_y_terms(s, m, Edges(nx, ny), ny, yl, yh, minus, plus)
     else:
-        _, s, s_out, sem = refs
+        s, s_out, sem = refs[-3:]
+        if part == 1:
+            stress_y_terms(s, m, e, ny, *refs[:4])
+            fault_rows(before, begin)
+        out = slabs_out(ny, before, begin, s, s_out, sem)
+        for c in out:
+            c.start()
     body = stress_slabs(nx, ny, v, s, m, None)
-    on_minus, _ = fault_side()
-
-    width = -(-(end - begin) // 4) * 2
-    while begin < end:
-        stop = min(begin + width, end)
-        run_slabs(begin, stop, body)
-        at = pl.ds(begin * ny + ny - 1, stop - begin, stride=ny)
-        s[SXY, :, at, :] = jnp.where(on_minus, traction[:, begin:stop, :], s[SXY, :, at, :])
-        span = pl.ds(begin * ny, (stop - begin) * ny)
-        for c in range(6):
-            for k in range(s.shape[1]):
-                copy = pltpu.make_async_copy(
-                    s.at[c, k, span], s_out.at[c, span, tile(k)], sem.at[c, k]
-                )
-                copy.start()
-                out.append(copy)
-        begin = stop
+    if part == 0:
+        for x in (0, 1, nx - 2, nx - 1):
+            body(x, True)
+    run_slabs(begin, end, body)
+    if part > 0:
+        fault_rows(begin, end)
     for c in out:
         c.wait()
 
@@ -591,10 +593,13 @@
 
 
 def stress_last_body(
-    nx, ny, rows, holders, s, w, xl, xh, traction, mine, got, o_in, out, slip, state, own, sem
+    nx, ny, rows, begin, holders, s, w, xl, xh, traction, mine, got, o_in, out, slip, state, own, sem
 ):
     del o_in
     e = Edges(nx, ny)
+    early = slabs_out(ny, begin, nx - 2, s, out, sem)
+    for c in early:
+        c.start()
     on_minus, _ = fault_side()
     stress_x_terms(s, w, e, nx, xl, xh)
     copies = []
@@ -607,7 +612,7 @@
             for k in range(s.shape[1]):
                 copies.append(
                     pltpu.make_async_copy(
-                        s.at[c, k, span], out.at[c, span, tile(k)], sem.at[j * 6 + c, k]
+                        s.at[c, k, span], out.at[c, span, tile(k)], sem.at[6 + j * 6 + c, k]
                     )
                 )
     for c in copies:
@@ -619,10 +624,10 @@
         for q in range(2):
             own[q, :, tile(k)] = jnp.where(have, mine[q, k, at, :], got[q, k, at, :])
     for q, target in enumerate((slip, state)):
-        copy = pltpu.make_async_copy(own.at[q], target, sem.at[12, q])
+        copy = pltpu.make_async_copy(own.at[q], target, sem.at[18, q])
         copy.start()
         copies.append(copy)
-    for c in copies:
+    for c in early + copies:
         c.wait()
 
 
@@ -763,57 +768,50 @@
         body = functools.partial(stress_body, nx, ny, first)
         if last:
             half_rows = ((2, nt, nx // 2, LANES), VMEM)
-            back, holders = got[7], [members // 2 - 1, members // 2]
-            s, back = call(
-                functools.partial(last_begin_body, nx, ny), [VMEM] * 4, [block_s, half_rows],
-                (v, s, m, back), aliases={1: 0}, cost=stage_cost,
-                name="last_begin",
-            )
-            edges, bits = [2], []
+            block_out = ((6, flat, nz), HBM)
+            cuts = [2, 2 + (nx - 4) // 6 * 2 + 2, nx - 2 - (nx - 4) // 6 * 2, nx - 2]
+            holders = [members // 2 - 1, members // 2]
             bit = members // 4
-            while bit >= 1:
-                bits.append(bit)
-                bit //= 2
-            parts = max(len(bits) - 1, 1)
-            for j in range(parts):
-                edges.append(2 + (nx - 4) * (j + 1) // parts)
-            s_out = v_out = None
-            for j, bit in enumerate(bits):
-                came = swap(back, bit)
-                if j < parts:
-                    outs = [block_s, ((6, flat, nz), HBM)]
-                    ins = [VMEM] * 4
-                    args = [v, s, m, trac_new]
-                    aliases = {1: 0}
-                    if j == 0:
-                        ins, args = ins + [VMEM] * 4, args + [yl, yh, minus, plus]
-                        outs.append(((3, flat, nz), HBM))
-                    else:
-                        ins, args = ins + [HBM], args + [s_out]
-                        aliases[4] = 1
-                    parts_out = call(
-                        functools.partial(
-                            last_slabs_body, nx, ny, edges[j], edges[j + 1], j == 0
-                        ),
-                        ins, outs, args, scratch=[dma(9)], aliases=aliases, cost=part_cost,
-                        name=f"last_slabs_{j}",
-                    )
-                    s, s_out = parts_out[:2]
-                    if j == 0:
-                        v_out = parts_out[2]
-                if j < len(bits) - 1:
+            back, s_out = got[7], None
+            came = swap(back, bit)
+            for part in range(3):
+                ins, args, aliases, outs = [VMEM] * 4, [v, s, m, trac_new], {1: 0}, [block_s]
+                if part == 0:
+                    outs += [((3, flat, nz), HBM)]
+                elif part == 1:
+                    ins, args = ins + [VMEM] * 4, args + [yl, yh, minus, plus]
+                    outs += [block_out]
+                else:
+                    ins, args = ins + [HBM], args + [s_out]
+                    outs += [block_out]
+                    aliases[4] = 1
+                body = functools.partial(
+                    last_slabs_body, nx, ny, part, cuts[part - 1] if part else None, cuts[part],
+                    cuts[part + 1],
+                )
+                done = call(
+                    body, ins, outs, args, scratch=[dma(3 if part == 0 else 6)], aliases=aliases,
+                    cost=part_cost if part else stage_cost, name=f"last_slabs_{part}",
+                )
+                s = done[0]
+                if part == 0:
+                    v_out = done[1]
+                else:
+                    s_out = done[1]
+                if bit > 1:
                     came, s = tie((came, s))
                     (back,) = call(
                         functools.partial(choose_body, tuple(holders)), [VMEM] * 2, [half_rows],
                         (back, came), cost=side_cost, name="choose",
                     )
                     holders += [h ^ bit for h in holders]
+                    bit //= 2
+                    came = swap(back, bit)
             s_out, slip, state_out = call(
-                functools.partial(stress_last_body, nx, ny, rows, tuple(holders)),
-                [VMEM] * 7 + [HBM],
-                [((6, flat, nz), HBM), ((rows, nz), HBM), ((rows, nz), HBM)],
+                functools.partial(stress_last_body, nx, ny, rows, cuts[2], tuple(holders)),
+                [VMEM] * 7 + [HBM], [block_out, ((rows, nz), HBM), ((rows, nz), HBM)],
                 (s, m, xl, xh, trac_new, back, came, s_out),
-                scratch=[pltpu.VMEM((2, rows, nz), F32), dma(13)],
+                scratch=[pltpu.VMEM((2, rows, nz), F32), dma(19)],
                 aliases={7: 0}, cost=side_cost, name="edges_last",
             )
             continue

time: 81 us -> 79.6 us (0.983)
  Pallas kernels: 27.4 us -> 26.4 us
  waiting for transfers between devices: 5.36 us -> 4.49 us
    pallas_call x22, Pallas kernels: 27.4 us -> 26.4 us  [call(): pl.pallas_call(body, out_shape=shapes, in_specs=ins, out_specs=[spec for...]
    ppermute x7, waiting for transfers between devices: 4.7 us -> 3.83 us  [swap(): return lax.ppermute(x, 'normal', [(i, i ^ bit) for i in range(count)])]
  transfers between devices with their start and end apart: 25 -> 25, of which waited for: 4 -> 3; matrix products, arithmetic and copies ran while one was open for 0% -> 0% of each run, Pallas kernels for 29% -> 28%
where the time goes in v4:
time: 79.6 us; the launch traced here: 79.5 us
  starting transfers between devices  47.5 us (60%)
  Pallas kernels  26.4 us (33%)
  waiting for transfers between devices  4.49 us (6%)
  between operations  1.07 us (1%)
    ppermute x8, starting transfers between devices, shift_down(): return lax.ppermute(x, axis, [((i + 1) % count, i) for i in range(count)])  30.3 us
    pallas_call x22, Pallas kernels, call(): pl.pallas_call(body, out_shape=shapes, in_specs=ins, out_specs=[spec for...  26.4 us
    ppermute x7, starting transfers between devices, swap(): return lax.ppermute(x, 'normal', [(i, i ^ bit) for i in range(count)])  12.9 us
    ppermute x7, waiting for transfers between devices, swap(): return lax.ppermute(x, 'normal', [(i, i ^ bit) for i in range(count)])  3.83 us
    ppermute x8, starting transfers between devices, shift_up(): return lax.ppermute(x, axis, [(i, (i + 1) % count) for i in range(count)])  2.2 us
    ppermute x2, starting transfers between devices, swap_odd(): return lax.ppermute(x, axis, pairs)  2.05 us
  transfers between devices with their start and end apart: 25, of which 3 were waited for; matrix products, arithmetic and copies ran while one was open for 0% of the time, Pallas kernels for 28%

profile of v4, /device:TPU:1, one launch (start us, length us, event | category | flops | bytes accessed | tf_op | source)
XLA Modules:
  0.0 79.5 jit_solution(10548913696476581174)
XLA Ops:
  1.4 1.5 %collective-permute-start = (f32[1,8,384]{2,1,0:T(8,128)S(1)}, f32[1,8,384]{2,1,0:T(8,128)S(1)}, u32[]{:S(2)}, u32[]{:S(2)}) collective-permute-start(f32[1,8,384]{2,1,0:T(8,128)S(1)} %own.1.mine), channel_id=1, source_target_pairs={{0,1},{1,0},{2,3},{3,2},{4,5},{5,4},{6,7},{7,6},{8,9},{9,8},{10,11... | collective-permute-start | bytes 36872 | tf_op jit(solution)/shard_map/ppermute | solution.py:44
  2.9 2.5 %load.1 = (f32[6,3,512,128]{3,2,1,0:T(8,128)S(1)}, f32[5,3,16,128]{3,2,1,0:T(8,128)S(1)}, f32[4,3,16,128]{3,2,1,0:T(8,128)S(1)}, f32[5,3,32,128]{3,2,1,0:T(8,128)S(1)}, f32[4,3,32,128]{3,2,1,0:T(8,128)S(1)}) custom-call(f32[6,512,384]{2,1,0:T(8,128)} %bitcast.7), custom_call_target="tpu_custom_call" | custom-call | flops 1000000 | bytes 1000000 | tf_op jit(solution)/shard_map/load/pallas_call | solution.py:57
  5.4 1.5 %collective-permute-start.1 = (f32[2,8,384]{2,1,0:T(8,128)S(1)}, f32[2,8,384]{2,1,0:T(8,128)S(1)}, u32[]{:S(2)}, u32[]{:S(2)}) collective-permute-start(f32[2,8,384]{2,1,0:T(8,128)S(1)} %merge.3.mine), channel_id=1, source_target_pairs={{0,2},{1,3},{2,0},{3,1},{4,6},{5,7},{6,4},{7,5},{8,10},{9,11},{10,... | collective-permute-start | bytes 73736 | tf_op jit(solution)/shard_map/ppermute | solution.py:44
  6.9 6.2 %collective-permute-start.4 = (f32[4,3,16,128]{3,2,1,0:T(8,128)S(1)}, f32[4,3,16,128]{3,2,1,0:T(8,128)S(1)}, u32[]{:S(2)}, u32[]{:S(2)}) collective-permute-start(f32[4,3,16,128]{3,2,1,0:T(8,128)S(1)} %get-tuple-element.77), channel_id=1, source_target_pairs={{16,0},{32,16},{48,32},{64,48},{80,64},{96,80},{112,96},{0,112},{1... | collective-permute-start | bytes 294920 | tf_op jit(solution)/shard_map/ppermute | solution.py:30
  13.7 1.2 %collective-permute-start.5 = (f32[5,3,32,128]{3,2,1,0:T(8,128)S(1)}, f32[5,3,32,128]{3,2,1,0:T(8,128)S(1)}, u32[]{:S(2)}, u32[]{:S(2)}) collective-permute-start(f32[5,3,32,128]{3,2,1,0:T(8,128)S(1)} %get-tuple-element.78), channel_id=1, source_target_pairs={{0,1},{1,2},{2,3},{3,4},{4,5},{5,6},{6,7},{7,8},{8,9},{9,10},{10,1... | collective-permute-start | bytes 737288 | tf_op jit(solution)/shard_map/ppermute | solution.py:25
  14.9 2.7 %collective-permute-start.2 = (f32[4,8,384]{2,1,0:T(8,128)S(1)}, f32[4,8,384]{2,1,0:T(8,128)S(1)}, u32[]{:S(2)}, u32[]{:S(2)}) collective-permute-start(f32[4,8,384]{2,1,0:T(8,128)S(1)} %merge.4.mine), channel_id=1, source_target_pairs={{0,4},{1,5},{2,6},{3,7},{4,0},{5,1},{6,2},{7,3},{8,12},{9,13},{10,... | collective-permute-start | bytes 147464 | tf_op jit(solution)/shard_map/ppermute | solution.py:44
  17.6 5.0 %velocity_first.1 = (f32[3,3,512,128]{3,2,1,0:T(8,128)S(1)}, f32[3,512,128]{2,1,0:T(8,128)S(1)}, f32[3,512,128]{2,1,0:T(8,128)S(1)}) custom-call(f32[6,3,512,128]{3,2,1,0:T(8,128)S(1)} %get-tuple-element.72.s.s_in, f32[3,512,384]{2,1,0:T(8,128)} %bitcast.8, f32[512,384]{1,0:T(8,128)} %bitcast.9, f32[512,384]{1,0:T(8,128)} %bitcast.10), custom_call_target="tpu_custom_call" | custom-call | flops 4000000000 | bytes 16000000 | tf_op jit(solution)/shard_map/velocity_first/pallas_call | solution.py:57
  23.8 3.7 %collective-permute-done.8.got = f32[8,8,384]{2,1,0:T(8,128)S(1)} collective-permute-done((f32[8,8,384]{2,1,0:T(8,128)S(1)}, f32[8,8,384]{2,1,0:T(8,128)S(1)}, u32[]{:S(2)}, u32[]{:S(2)}) %collective-permute-start.8) | collective-permute-done | bytes 98336 | tf_op jit(solution)/shard_map/ppermute | solution.py:44
  30.3 4.8 %collective-permute-start.10 = (f32[5,3,16,128]{3,2,1,0:T(8,128)S(1)}, f32[5,3,16,128]{3,2,1,0:T(8,128)S(1)}, u32[]{:S(2)}, u32[]{:S(2)}) collective-permute-start(f32[5,3,16,128]{3,2,1,0:T(8,128)S(1)} %get-tuple-element.91), channel_id=1, source_target_pairs={{16,0},{32,16},{48,32},{64,48},{80,64},{96,80},{112,96},{0,112},{1... | collective-permute-start | bytes 368648 | tf_op jit(solution)/shard_map/ppermute | solution.py:30
  35.1 3.4 %stress_first.1 = (f32[6,3,512,128]{3,2,1,0:T(8,128)S(1)}, f32[3,512,128]{2,1,0:T(8,128)S(1)}) custom-call(f32[3,3,512,128]{3,2,1,0:T(8,128)S(1)} %get-tuple-element.86.v.v_in, f32[6,3,512,128]{3,2,1,0:T(8,128)S(1)} %get-tuple-element.72.s.s_in, f32[3,512,128]{2,1,0:T(8,128)S(1)} %get-tuple-element.87.m_in), custom_call_target="tpu_custom_call", output_to_operand_aliasing={{0}: (1, {}), {1}: (2, {})} | custom-call | flops 4000000000 | bytes 16000000 | tf_op jit(solution)/shard_map/stress_first/pallas_call | solution.py:57
  38.5 1.0 %stress_edges.1 = (f32[6,3,512,128]{3,2,1,0:T(8,128)S(1)}, f32[5,3,16,128]{3,2,1,0:T(8,128)S(1)}, f32[4,3,16,128]{3,2,1,0:T(8,128)S(1)}, f32[5,3,32,128]{3,2,1,0:T(8,128)S(1)}, f32[4,3,32,128]{3,2,1,0:T(8,128)S(1)}) custom-call(f32[6,3,512,128]{3,2,1,0:T(8,128)S(1)} %get-tuple-element.88.s_in, ...), custom_call_target="tpu_custom_call", output_to_operand_aliasing={{0}: (0, {})} | custom-call | flops 1000000 | bytes 1000000 | tf_op jit(solution)/shard_map/stress_edges/pallas_call | solution.py:57
  39.6 5.3 %collective-permute-start.14 = (f32[4,3,16,128]{3,2,1,0:T(8,128)S(1)}, f32[4,3,16,128]{3,2,1,0:T(8,128)S(1)}, u32[]{:S(2)}, u32[]{:S(2)}) collective-permute-start(f32[4,3,16,128]{3,2,1,0:T(8,128)S(1)} %get-tuple-element.99), channel_id=1, source_target_pairs={{16,0},{32,16},{48,32},{64,48},{80,64},{96,80},{112,96},{0,112},{1... | collective-permute-start | bytes 294920 | tf_op jit(solution)/shard_map/ppermute | solution.py:30
  44.9 4.3 %collective-permute-start.16 = (f32[4,3,32,128]{3,2,1,0:T(8,128)S(1)}, f32[4,3,32,128]{3,2,1,0:T(8,128)S(1)}, u32[]{:S(2)}, u32[]{:S(2)}) collective-permute-start(f32[4,3,32,128]{3,2,1,0:T(8,128)S(1)} %get-tuple-element.101), channel_id=1, source_target_pairs={{1,0},{2,1},{3,2},{4,3},{5,4},{6,5},{7,6},{8,7},{9,8},{10,9},{11,1... | collective-permute-start | bytes 589832 | tf_op jit(solution)/shard_map/ppermute | solution.py:30
  49.3 3.3 %velocity.1.v_in = f32[3,3,512,128]{3,2,1,0:T(8,128)S(1)} custom-call(f32[6,3,512,128]{3,2,1,0:T(8,128)S(1)} %get-tuple-element.97.s.s_in, f32[3,3,512,128]{3,2,1,0:T(8,128)S(1)} %get-tuple-element.86.v.v_in, f32[3,512,128]{2,1,0:T(8,128)S(1)} %get-tuple-element.75.w.b_in), custom_call_target="tpu_custom_call", output_to_operand_aliasing={{}: (1, {})} | custom-call | flops 4000000000 | bytes 16000000 | tf_op jit(solution)/shard_map/velocity/pallas_call | solution.py:57
  53.8 2.0 %collective-permute-start.17 = (f32[3,32,128]{2,1,0:T(8,128)S(1)}, f32[3,32,128]{2,1,0:T(8,128)S(1)}, u32[]{:S(2)}, u32[]{:S(2)}) collective-permute-start(f32[3,32,128]{2,1,0:T(8,128)S(1)} %get-tuple-element.102.refs_0_), channel_id=1, source_target_pairs={{1,2},{2,1},{3,4},{4,3},{5,6},{6,5},{7,8},{8,7},{9,10},{10,9},{11,... | collective-permute-start | bytes 147464 | tf_op jit(solution)/shard_map/ppermute | solution.py:39
  56.1 3.5 %collective-permute-start.21 = (f32[5,3,32,128]{3,2,1,0:T(8,128)S(1)}, f32[5,3,32,128]{3,2,1,0:T(8,128)S(1)}, u32[]{:S(2)}, u32[]{:S(2)}) collective-permute-start(f32[5,3,32,128]{3,2,1,0:T(8,128)S(1)} %get-tuple-element.114), channel_id=1, source_target_pairs={{1,0},{2,1},{3,2},{4,3},{5,4},{6,5},{7,6},{8,7},{9,8},{10,9},{11,1... | collective-permute-start | bytes 737288 | tf_op jit(solution)/shard_map/ppermute | solution.py:30
  59.5 1.1 %fault.3 = (f32[3,3,512,128]{3,2,1,0:T(8,128)S(1)}, f32[4,3,16,128]{3,2,1,0:T(8,128)S(1)}, f32[5,3,16,128]{3,2,1,0:T(8,128)S(1)}, f32[3,32,128]{2,1,0:T(8,128)},...) custom-call(f32[3,32,128]{2,1,0:T(8,128)S(1)} %get-tuple-element.102, ...), custom_call_target="tpu_custom_call", output_to_operand_aliasing={{0}: (5, {})} | custom-call | flops 1000000 | bytes 1000000 | tf_op jit(solution)/shard_map/fault/pallas_call | solution.py:57
  61.1 5.1 %collective-permute-start.23 = (f32[5,3,16,128]{3,2,1,0:T(8,128)S(1)}, f32[5,3,16,128]{3,2,1,0:T(8,128)S(1)}, u32[]{:S(2)}, u32[]{:S(2)}) collective-permute-start(f32[5,3,16,128]{3,2,1,0:T(8,128)S(1)} %get-tuple-element.122), channel_id=1, source_target_pairs={{16,0},{32,16},{48,32},{64,48},{80,64},{96,80},{112,96},{0,112},{1... | collective-permute-start | bytes 368648 | tf_op jit(solution)/shard_map/ppermute | solution.py:30
  66.1 1.6 %last_slabs_0.1 = (f32[6,3,512,128]{3,2,1,0:T(8,128)S(1)}, f32[3,512,384]{2,1,0:T(8,128)}) custom-call(f32[3,3,512,128]{3,2,1,0:T(8,128)S(1)} %get-tuple-element.106.v, f32[6,3,512,128]{3,2,1,0:T(8,128)S(1)} %get-tuple-element.97.s.s_in, f32[3,512,128]{2,1,0:T(8,128)S(1)} %get-tuple-element.89.w.m, ...), custom_call_target="tpu_custom_call", output_to_operand_aliasing={{0}: (1, {})} | custom-call | flops 4000000000 | bytes 16000000 | tf_op jit(solution)/shard_map/last_slabs_0/pallas_call | solution.py:57
  67.8 4.1 %collective-permute-start.19 = (f32[2,3,16,128]{3,2,1,0:T(8,128)S(1)}, f32[2,3,16,128]{3,2,1,0:T(8,128)S(1)}, u32[]{:S(2)}, u32[]{:S(2)}) collective-permute-start(f32[2,3,16,128]{3,2,1,0:T(8,128)S(1)} %choose.2.mine), channel_id=1, source_target_pairs={{0,2},{1,3},{2,0},{3,1},{4,6},{5,7},{6,4},{7,5},{8,10},{9,11},{10,... | collective-permute-start | bytes 147464 | tf_op jit(solution)/shard_map/ppermute | solution.py:44
  71.8 2.1 %last_slabs_1.1 = (f32[6,3,512,128]{3,2,1,0:T(8,128)S(1)}, f32[6,512,384]{2,1,0:T(8,128)}) custom-call(f32[3,3,512,128]{3,2,1,0:T(8,128)S(1)} %get-tuple-element.106.v, f32[6,3,512,128]{3,2,1,0:T(8,128)S(1)} %get-tuple-element.112.s_in, f32[3,512,128]{2,1,0:T(8,128)S(1)} %get-tuple-element.89.w.m, ...), custom_call_target="tpu_custom_call", output_to_operand_aliasing={{0}: (1, {})} | custom-call | flops 2000000000 | bytes 8000000 | tf_op jit(solution)/shard_map/last_slabs_1/pallas_call | solution.py:57
  74.0 2.4 %collective-permute-start.24 = (f32[2,3,16,128]{3,2,1,0:T(8,128)S(1)}, f32[2,3,16,128]{3,2,1,0:T(8,128)S(1)}, u32[]{:S(2)}, u32[]{:S(2)}) collective-permute-start(f32[2,3,16,128]{3,2,1,0:T(8,128)S(1)} %choose.3.mine), channel_id=1, source_target_pairs={{0,1},{1,0},{2,3},{3,2},{4,5},{5,4},{6,7},{7,6},{8,9},{9,8},{10,11... | collective-permute-start | bytes 147464 | tf_op jit(solution)/shard_map/ppermute | solution.py:44
  76.3 1.3 %last_slabs_2.1 = (f32[6,3,512,128]{3,2,1,0:T(8,128)S(1)}, f32[6,512,384]{2,1,0:T(8,128)}) custom-call(f32[3,3,512,128]{3,2,1,0:T(8,128)S(1)} %get-tuple-element.106.v, f32[6,3,512,128]{3,2,1,0:T(8,128)S(1)} %get-tuple-element.118.s_in, f32[3,512,128]{2,1,0:T(8,128)S(1)} %get-tuple-element.89.w.m, ...), custom_call_target="tpu_custom_call", output_to_operand_aliasing={{0}: (1, {}), {1}: (4, {})} | custom-call | flops 2000000000 | bytes 8000000 | tf_op jit(solution)/shard_map/last_slabs_2/pallas_call | solution.py:57
  77.6 1.7 %edges_last.1 = (f32[6,512,384]{2,1,0:T(8,128)}, f32[2,384]{1,0:T(2,128)}, f32[2,384]{1,0:T(2,128)}) custom-call(f32[6,3,512,128]{3,2,1,0:T(8,128)S(1)} %get-tuple-element.120.s, f32[3,512,128]{2,1,0:T(8,128)S(1)} %get-tuple-element.89.w.m, f32[4,3,16,128]{3,2,1,0:T(8,128)S(1)} %collective-permute-done.22.xl, ...), custom_call_target="tpu_custom_call", output_to_operand_aliasing={{0}: (7, {})} | custom-call | flops 1000000 | bytes 1000000 | tf_op jit(solution)/shard_map/edges_last/pallas_call | solution.py:57
  (50 shorter events, 7.4 us)
Async XLA Ops:
  1.4 4.0 %collective-permute-start = (f32[1,8,384]{2,1,0:T(8,128)S(1)}, f32[1,8,384]{2,1,0:T(8,128)S(1)}, u32[]{:S(2)}, u32[]{:S(2)}) collective-permute-start(f32[1,8,384]{2,1,0:T(8,128)S(1)} %own.1.mine), channel_id=1, source_target_pairs={{0,1},{1,0},{2,3},{3,2},{4,5},{5,4},{6,7},{7,6},{8,9},{9,8},{10,11... | collective-permute-start | bytes 36872 | tf_op jit(solution)/shard_map/ppermute | solution.py:44
  5.4 9.4 %collective-permute-start.1 = (f32[2,8,384]{2,1,0:T(8,128)S(1)}, f32[2,8,384]{2,1,0:T(8,128)S(1)}, u32[]{:S(2)}, u32[]{:S(2)}) collective-permute-start(f32[2,8,384]{2,1,0:T(8,128)S(1)} %merge.3.mine), channel_id=1, source_target_pairs={{0,2},{1,3},{2,0},{3,1},{4,6},{5,7},{6,4},{7,5},{8,10},{9,11},{10,... | collective-permute-start | bytes 73736 | tf_op jit(solution)/shard_map/ppermute | solution.py:44
  6.9 16.1 %collective-permute-start.4 = (f32[4,3,16,128]{3,2,1,0:T(8,128)S(1)}, f32[4,3,16,128]{3,2,1,0:T(8,128)S(1)}, u32[]{:S(2)}, u32[]{:S(2)}) collective-permute-start(f32[4,3,16,128]{3,2,1,0:T(8,128)S(1)} %get-tuple-element.77), channel_id=1, source_target_pairs={{16,0},{32,16},{48,32},{64,48},{80,64},{96,80},{112,96},{0,112},{1... | collective-permute-start | bytes 294920 | tf_op jit(solution)/shard_map/ppermute | solution.py:30
  13.1 9.9 %collective-permute-start.3 = (f32[5,3,16,128]{3,2,1,0:T(8,128)S(1)}, f32[5,3,16,128]{3,2,1,0:T(8,128)S(1)}, u32[]{:S(2)}, u32[]{:S(2)}) collective-permute-start(f32[5,3,16,128]{3,2,1,0:T(8,128)S(1)} %get-tuple-element.76), channel_id=1, source_target_pairs={{0,16},{16,32},{32,48},{48,64},{64,80},{80,96},{96,112},{112,0},{1... | collective-permute-start | bytes 368648 | tf_op jit(solution)/shard_map/ppermute | solution.py:25
  13.1 9.9 %collective-permute-start.6 = (f32[4,3,32,128]{3,2,1,0:T(8,128)S(1)}, f32[4,3,32,128]{3,2,1,0:T(8,128)S(1)}, u32[]{:S(2)}, u32[]{:S(2)}) collective-permute-start(f32[4,3,32,128]{3,2,1,0:T(8,128)S(1)} %get-tuple-element.79), channel_id=1, source_target_pairs={{1,0},{2,1},{3,2},{4,3},{5,4},{6,5},{7,6},{8,7},{9,8},{10,9},{11,1... | collective-permute-start | bytes 589832 | tf_op jit(solution)/shard_map/ppermute | solution.py:30
  13.7 9.3 %collective-permute-start.5 = (f32[5,3,32,128]{3,2,1,0:T(8,128)S(1)}, f32[5,3,32,128]{3,2,1,0:T(8,128)S(1)}, u32[]{:S(2)}, u32[]{:S(2)}) collective-permute-start(f32[5,3,32,128]{3,2,1,0:T(8,128)S(1)} %get-tuple-element.78), channel_id=1, source_target_pairs={{0,1},{1,2},{2,3},{3,4},{4,5},{5,6},{6,7},{7,8},{8,9},{9,10},{10,1... | collective-permute-start | bytes 737288 | tf_op jit(solution)/shard_map/ppermute | solution.py:25
  14.9 7.8 %collective-permute-start.2 = (f32[4,8,384]{2,1,0:T(8,128)S(1)}, f32[4,8,384]{2,1,0:T(8,128)S(1)}, u32[]{:S(2)}, u32[]{:S(2)}) collective-permute-start(f32[4,8,384]{2,1,0:T(8,128)S(1)} %merge.4.mine), channel_id=1, source_target_pairs={{0,4},{1,5},{2,6},{3,7},{4,0},{5,1},{6,2},{7,3},{8,12},{9,13},{10,... | collective-permute-start | bytes 147464 | tf_op jit(solution)/shard_map/ppermute | solution.py:44
  22.7 4.8 %collective-permute-start.8 = (f32[8,8,384]{2,1,0:T(8,128)S(1)}, f32[8,8,384]{2,1,0:T(8,128)S(1)}, u32[]{:S(2)}, u32[]{:S(2)}) collective-permute-start(f32[8,8,384]{2,1,0:T(8,128)S(1)} %merge.5.mine), channel_id=1, source_target_pairs={{0,8},{1,9},{2,10},{3,11},{4,12},{5,13},{6,14},{7,15},{8,0},{9,1},... | collective-permute-start | bytes 294920 | tf_op jit(solution)/shard_map/ppermute | solution.py:44
  23.7 5.3 %collective-permute-start.7 = (f32[3,32,128]{2,1,0:T(8,128)S(1)}, f32[3,32,128]{2,1,0:T(8,128)S(1)}, u32[]{:S(2)}, u32[]{:S(2)}) collective-permute-start(f32[3,32,128]{2,1,0:T(8,128)S(1)} %get-tuple-element.80.refs_0_), channel_id=1, source_target_pairs={{1,2},{2,1},{3,4},{4,3},{5,6},{6,5},{7,8},{8,7},{9,10},{10,9},{11,... | collective-permute-start | bytes 147464 | tf_op jit(solution)/shard_map/ppermute | solution.py:39
  28.4 10.1 %collective-permute-start.11 = (f32[4,3,32,128]{3,2,1,0:T(8,128)S(1)}, f32[4,3,32,128]{3,2,1,0:T(8,128)S(1)}, u32[]{:S(2)}, u32[]{:S(2)}) collective-permute-start(f32[4,3,32,128]{3,2,1,0:T(8,128)S(1)} %get-tuple-element.92), channel_id=1, source_target_pairs={{0,1},{1,2},{2,3},{3,4},{4,5},{5,6},{6,7},{7,8},{8,9},{9,10},{10,1... | collective-permute-start | bytes 589832 | tf_op jit(solution)/shard_map/ppermute | solution.py:25
  28.5 10.1 %collective-permute-start.12 = (f32[5,3,32,128]{3,2,1,0:T(8,128)S(1)}, f32[5,3,32,128]{3,2,1,0:T(8,128)S(1)}, u32[]{:S(2)}, u32[]{:S(2)}) collective-permute-start(f32[5,3,32,128]{3,2,1,0:T(8,128)S(1)} %get-tuple-element.93), channel_id=1, source_target_pairs={{1,0},{2,1},{3,2},{4,3},{5,4},{6,5},{7,6},{8,7},{9,8},{10,9},{11,1... | collective-permute-start | bytes 737288 | tf_op jit(solution)/shard_map/ppermute | solution.py:30
  29.5 9.0 %collective-permute-start.9 = (f32[4,3,16,128]{3,2,1,0:T(8,128)S(1)}, f32[4,3,16,128]{3,2,1,0:T(8,128)S(1)}, u32[]{:S(2)}, u32[]{:S(2)}) collective-permute-start(f32[4,3,16,128]{3,2,1,0:T(8,128)S(1)} %get-tuple-element.90), channel_id=1, source_target_pairs={{0,16},{16,32},{32,48},{48,64},{64,80},{80,96},{96,112},{112,0},{1... | collective-permute-start | bytes 294920 | tf_op jit(solution)/shard_map/ppermute | solution.py:25
  30.3 8.2 %collective-permute-start.10 = (f32[5,3,16,128]{3,2,1,0:T(8,128)S(1)}, f32[5,3,16,128]{3,2,1,0:T(8,128)S(1)}, u32[]{:S(2)}, u32[]{:S(2)}) collective-permute-start(f32[5,3,16,128]{3,2,1,0:T(8,128)S(1)} %get-tuple-element.91), channel_id=1, source_target_pairs={{16,0},{32,16},{48,32},{64,48},{80,64},{96,80},{112,96},{0,112},{1... | collective-permute-start | bytes 368648 | tf_op jit(solution)/shard_map/ppermute | solution.py:30
  39.6 13.0 %collective-permute-start.14 = (f32[4,3,16,128]{3,2,1,0:T(8,128)S(1)}, f32[4,3,16,128]{3,2,1,0:T(8,128)S(1)}, u32[]{:S(2)}, u32[]{:S(2)}) collective-permute-start(f32[4,3,16,128]{3,2,1,0:T(8,128)S(1)} %get-tuple-element.99), channel_id=1, source_target_pairs={{16,0},{32,16},{48,32},{64,48},{80,64},{96,80},{112,96},{0,112},{1... | collective-permute-start | bytes 294920 | tf_op jit(solution)/shard_map/ppermute | solution.py:30
  44.9 8.3 %collective-permute-start.13 = (f32[5,3,16,128]{3,2,1,0:T(8,128)S(1)}, f32[5,3,16,128]{3,2,1,0:T(8,128)S(1)}, u32[]{:S(2)}, u32[]{:S(2)}) collective-permute-start(f32[5,3,16,128]{3,2,1,0:T(8,128)S(1)} %get-tuple-element.98), channel_id=1, source_target_pairs={{0,16},{16,32},{32,48},{48,64},{64,80},{80,96},{96,112},{112,0},{1... | collective-permute-start | bytes 368648 | tf_op jit(solution)/shard_map/ppermute | solution.py:25
  44.9 8.3 %collective-permute-start.16 = (f32[4,3,32,128]{3,2,1,0:T(8,128)S(1)}, f32[4,3,32,128]{3,2,1,0:T(8,128)S(1)}, u32[]{:S(2)}, u32[]{:S(2)}) collective-permute-start(f32[4,3,32,128]{3,2,1,0:T(8,128)S(1)} %get-tuple-element.101), channel_id=1, source_target_pairs={{1,0},{2,1},{3,2},{4,3},{5,4},{6,5},{7,6},{8,7},{9,8},{10,9},{11,1... | collective-permute-start | bytes 589832 | tf_op jit(solution)/shard_map/ppermute | solution.py:30
  49.3 3.9 %collective-permute-start.15 = (f32[5,3,32,128]{3,2,1,0:T(8,128)S(1)}, f32[5,3,32,128]{3,2,1,0:T(8,128)S(1)}, u32[]{:S(2)}, u32[]{:S(2)}) collective-permute-start(f32[5,3,32,128]{3,2,1,0:T(8,128)S(1)} %get-tuple-element.100), channel_id=1, source_target_pairs={{0,1},{1,2},{2,3},{3,4},{4,5},{5,6},{6,7},{7,8},{8,9},{9,10},{10,1... | collective-permute-start | bytes 737288 | tf_op jit(solution)/shard_map/ppermute | solution.py:25
  53.8 5.7 %collective-permute-start.17 = (f32[3,32,128]{2,1,0:T(8,128)S(1)}, f32[3,32,128]{2,1,0:T(8,128)S(1)}, u32[]{:S(2)}, u32[]{:S(2)}) collective-permute-start(f32[3,32,128]{2,1,0:T(8,128)S(1)} %get-tuple-element.102.refs_0_), channel_id=1, source_target_pairs={{1,2},{2,1},{3,4},{4,3},{5,6},{6,5},{7,8},{8,7},{9,10},{10,9},{11,... | collective-permute-start | bytes 147464 | tf_op jit(solution)/shard_map/ppermute | solution.py:39
  55.9 15.9 %collective-permute-start.20 = (f32[4,3,32,128]{3,2,1,0:T(8,128)S(1)}, f32[4,3,32,128]{3,2,1,0:T(8,128)S(1)}, u32[]{:S(2)}, u32[]{:S(2)}) collective-permute-start(f32[4,3,32,128]{3,2,1,0:T(8,128)S(1)} %get-tuple-element.113), channel_id=1, source_target_pairs={{0,1},{1,2},{2,3},{3,4},{4,5},{5,6},{6,7},{7,8},{8,9},{9,10},{10,1... | collective-permute-start | bytes 589832 | tf_op jit(solution)/shard_map/ppermute | solution.py:25
  56.1 15.8 %collective-permute-start.21 = (f32[5,3,32,128]{3,2,1,0:T(8,128)S(1)}, f32[5,3,32,128]{3,2,1,0:T(8,128)S(1)}, u32[]{:S(2)}, u32[]{:S(2)}) collective-permute-start(f32[5,3,32,128]{3,2,1,0:T(8,128)S(1)} %get-tuple-element.114), channel_id=1, source_target_pairs={{1,0},{2,1},{3,2},{4,3},{5,4},{6,5},{7,6},{8,7},{9,8},{10,9},{11,1... | collective-permute-start | bytes 737288 | tf_op jit(solution)/shard_map/ppermute | solution.py:30
  60.6 7.1 %collective-permute-start.18 = (f32[2,3,16,128]{3,2,1,0:T(8,128)S(1)}, f32[2,3,16,128]{3,2,1,0:T(8,128)S(1)}, u32[]{:S(2)}, u32[]{:S(2)}) collective-permute-start(f32[2,3,16,128]{3,2,1,0:T(8,128)S(1)} %get-tuple-element.109.mine), channel_id=1, source_target_pairs={{0,4},{1,5},{2,6},{3,7},{4,0},{5,1},{6,2},{7,3},{8,12},{9,13},{10,... | collective-permute-start | bytes 147464 | tf_op jit(solution)/shard_map/ppermute | solution.py:44
  61.1 16.5 %collective-permute-start.22 = (f32[4,3,16,128]{3,2,1,0:T(8,128)S(1)}, f32[4,3,16,128]{3,2,1,0:T(8,128)S(1)}, u32[]{:S(2)}, u32[]{:S(2)}) collective-permute-start(f32[4,3,16,128]{3,2,1,0:T(8,128)S(1)} %get-tuple-element.121), channel_id=1, source_target_pairs={{0,16},{16,32},{32,48},{48,64},{64,80},{80,96},{96,112},{112,0},{1... | collective-permute-start | bytes 294920 | tf_op jit(solution)/shard_map/ppermute | solution.py:25
  61.1 16.5 %collective-permute-start.23 = (f32[5,3,16,128]{3,2,1,0:T(8,128)S(1)}, f32[5,3,16,128]{3,2,1,0:T(8,128)S(1)}, u32[]{:S(2)}, u32[]{:S(2)}) collective-permute-start(f32[5,3,16,128]{3,2,1,0:T(8,128)S(1)} %get-tuple-element.122), channel_id=1, source_target_pairs={{16,0},{32,16},{48,32},{64,48},{80,64},{96,80},{112,96},{0,112},{1... | collective-permute-start | bytes 368648 | tf_op jit(solution)/shard_map/ppermute | solution.py:30
  67.8 6.2 %collective-permute-start.19 = (f32[2,3,16,128]{3,2,1,0:T(8,128)S(1)}, f32[2,3,16,128]{3,2,1,0:T(8,128)S(1)}, u32[]{:S(2)}, u32[]{:S(2)}) collective-permute-start(f32[2,3,16,128]{3,2,1,0:T(8,128)S(1)} %choose.2.mine), channel_id=1, source_target_pairs={{0,2},{1,3},{2,0},{3,1},{4,6},{5,7},{6,4},{7,5},{8,10},{9,11},{10,... | collective-permute-start | bytes 147464 | tf_op jit(solution)/shard_map/ppermute | solution.py:44
  (2 other events, 8.6 us)

commit v5 on v4

--- a/solution.py
+++ b/solution.py
@@ -47,6 +47,7 @@
 VMEM = pl.BlockSpec(memory_space=pltpu.VMEM)
 SMEM = pl.BlockSpec(memory_space=pltpu.SMEM)
 HBM = pl.BlockSpec(memory_space=pltpu.HBM)
+ANY = pl.BlockSpec(memory_space=pl.ANY)
 
 
 def call(body, ins, outs, args, scratch=(), aliases=None, cost=None, name=None):
@@ -485,8 +486,9 @@
     wait(SZZ)
 
 
-def velocity_edges_body(nx, ny, v_in, w, s, xl, xh, yl, yh, v, mine, traction):
+def velocity_edges_body(nx, ny, rows, v_in, w, s, xl, xh, yl, yh, *refs):
     del v_in
+    v, mine, traction = refs[-3:]
     e = Edges(nx, ny)
     fxl, fxh, fyl, fyh = sides()
     a = [xl[k] * fxl for k in range(5)]
@@ -508,7 +510,15 @@
         for i, value in terms:
             add_rows(v, comp, w, e.y(i), 1.0, value)
     odd = lax.rem(lax.axis_index("normal"), 2) == 1
-    mine[...] = jnp.where(odd, v[0, :, e.y(ny - 1), :], v[0, :, e.y(0), :])
+    mine[:, 0:nx, :] = jnp.where(odd, v[0, :, e.y(ny - 1), :], v[0, :, e.y(0), :])
+    if rows:
+        known = refs[0]
+        count = known.shape[0] * rows
+        for k in range(known.shape[0]):
+            for q in range(3):
+                at = slice(nx + q * count + k * rows, nx + q * count + (k + 1) * rows)
+                for z in range(mine.shape[0]):
+                    mine[z, at, :] = known[k, q * rows : (q + 1) * rows, tile(z)]
     traction[...] = jnp.where(odd, s[SXY, :, e.y(ny - 1), :], yl[2])
 
 
@@ -527,15 +537,37 @@
     return jnp.where(values < 0.0, -result, result)
 
 
-def fault_body(nx, ny, last, *refs):
-    mine, other, traction, par, st_in, v_in, v, xu, xd, st, minus_o, plus_o, trac_o = refs[:13]
+def fault_parameters(nx, mine, other, table, state, par):
+    half = nx // 2
+    upper = lax.axis_index("normal") >= lax.axis_size("normal") // 2
+    full = []
+    for q in range(3):
+        at = slice(nx + q * half, nx + (q + 1) * half)
+        a, b = mine[:, at, :], other[:, at, :]
+        full.append(jnp.concatenate((jnp.where(upper, b, a), jnp.where(upper, a, b)), 1))
+    state[...] = full[0]
+    par[0] = full[1]
+    for j in range(4):
+        p = jnp.zeros_like(full[2])
+        for r in range(table.shape[1]):
+            p = jnp.where(full[2] == float(r), table[j, r], p)
+        par[1 + j] = p
+
+
+def fault_body(nx, ny, first, last, *refs):
+    if first:
+        mine, other, traction, table, v_in, v, xu, xd, st, minus_o, plus_o, trac_o, par = refs[:13]
+        fault_parameters(nx, mine, other, table, st, par)
+        st_in = st
+    else:
+        mine, other, traction, par, st_in, v_in, v, xu, xd, st, minus_o, plus_o, trac_o = refs[:13]
     del v_in
     e = Edges(nx, ny)
     position = lax.axis_index("normal")
     members = lax.axis_size("normal")
     odd = lax.rem(position, 2) == 1
     on_minus, on_plus = fault_side()
-    m, o = mine[...], other[...]
+    m, o = mine[:, 0:nx, :], other[:, 0:nx, :]
     minus = jnp.where(odd, m, o)
     plus = jnp.where(odd, o, m)
     mask, a, b, inv_len, sigma = (par[k] for k in range(5))
@@ -655,35 +687,16 @@
     out[n : 2 * n] = jnp.where(upper, a, b)
 
 
-def parameters_body(rows, mine, got, table, st, par, tmp):
-    half = mine.shape[0]
-    upper = lax.axis_index("normal") >= half
-    for k in range(2 * half):
-        at = slice(k * rows, (k + 1) * rows)
-        a, b = (mine, got) if k < half else (got, mine)
-        block = jnp.where(upper, b[k % half], a[k % half])
-        for z in range(st.shape[0]):
-            st[z, at, :] = block[0:rows, tile(z)]
-            par[0, z, at, :] = block[rows : 2 * rows, tile(z)]
-            tmp[z, at, :] = block[2 * rows : 3 * rows, tile(z)]
-    ids = tmp[...]
-    for j in range(4):
-        p = jnp.zeros_like(ids)
-        for r in range(table.shape[1]):
-            p = jnp.where(ids == float(r), table[j, r], p)
-        par[1 + j] = p
-
-
 def local(velocity, stress, modulus, buoyancy, fault_state, fault_mask, region_ids, friction_table):
     members = lax.axis_size("normal")
     _, nx, ny, nz = velocity.shape
     rows = fault_state.shape[0]
     flat, nt = nx * ny, nz // LANES
     pin = lambda x: pltpu.with_memory_space_constraint(x, pltpu.HBM)
-    vel_in = pin(velocity.reshape(3, flat, nz))
+    vel_in = velocity.reshape(3, flat, nz)
     str_in = pin(stress.reshape(6, flat, nz))
-    mod_in = pin(modulus.reshape(flat, nz))
-    buo_in = pin(buoyancy.reshape(flat, nz))
+    mod_in = modulus.reshape(flat, nz)
+    buo_in = buoyancy.reshape(flat, nz)
     fault_in = (pin(fault_state), pin(fault_mask), pin(region_ids))
     dma = lambda n: pltpu.SemaphoreType.DMA((n, nt))
     stage_cost = pl.CostEstimate(flops=4_000_000_000, bytes_accessed=16_000_000, transcendentals=0)
@@ -726,7 +739,7 @@
         yl, yh = shift_up(yu, "normal"), shift_down(yd, "normal")
         if first:
             v, w, m = call(
-                functools.partial(velocity_body, nx, ny, True), [VMEM, HBM, HBM, HBM],
+                functools.partial(velocity_body, nx, ny, True), [VMEM, ANY, ANY, ANY],
                 [block_v, block_1, block_1], (s, vel_in, buo_in, mod_in),
                 scratch=[dma(4 * LOADS + 1)], cost=stage_cost, name="velocity_first",
             )
@@ -734,20 +747,17 @@
                 known = merge(known, swap(known, bit), bit)
                 bit *= 2
             known, v = tie((known, v))
-            state, par = call(
-                functools.partial(parameters_body, rows), [VMEM, VMEM, SMEM],
-                [((nt, nx, LANES), VMEM), ((5, nt, nx, LANES), VMEM)],
-                (known, swap(known, bit), friction_table),
-                scratch=[pltpu.VMEM((nt, nx, LANES), F32)], cost=side_cost, name="parameters",
-            )
         else:
             (v,) = call(
                 functools.partial(velocity_body, nx, ny, False), [VMEM] * 3, [block_v], (s, v, w),
                 aliases={1: 0}, cost=stage_cost, name="velocity",
             )
+        extra = [known] if first else []
+        sent = ((nt, nx + 3 * (nx // 2), LANES), VMEM) if first else row_1
         v, mine, traction = call(
-            functools.partial(velocity_edges_body, nx, ny), [VMEM] * 7, [block_v, row_1, row_1],
-            (v, w, s, xl, xh, yl, yh), aliases={0: 0}, cost=side_cost, name="velocity_edges",
+            functools.partial(velocity_edges_body, nx, ny, rows if first else 0),
+            [VMEM] * (7 + len(extra)), [block_v, sent, row_1], (v, w, s, xl, xh, yl, yh, *extra),
+            aliases={0: 0}, cost=side_cost, name="velocity_edges",
         )
         other = swap_odd(mine, "normal")
         yu, yd = call(
@@ -759,10 +769,17 @@
         outs = [block_v, ((4, nt, ny, LANES), VMEM), ((5, nt, ny, LANES), VMEM)] + [row_1] * 4
         if last:
             outs.append(((2, nt, nx // 2, LANES), VMEM))
+        elif first:
+            outs.append(((5, nt, nx, LANES), VMEM))
+        ins = [VMEM, VMEM, VMEM, SMEM, VMEM] if first else [VMEM] * 6
+        args = (friction_table, v) if first else (par, state, v)
         got = call(
-            functools.partial(fault_body, nx, ny, last), [VMEM] * 6, outs,
-            (mine, other, traction, par, state, v), aliases={5: 0}, cost=side_cost, name="fault",
+            functools.partial(fault_body, nx, ny, first, last), ins, outs,
+            (mine, other, traction, *args), aliases={len(ins) - 1: 0}, cost=side_cost,
+            name="fault",
         )
+        if first:
+            par = got[7]
         v, xu, xd, state, minus, plus, trac_new = got[:7]
         xl, xh = shift_up(xu, "strike"), shift_down(xd, "strike")
         body = functools.partial(stress_body, nx, ny, first)

time: 79.6 us -> 79.2 us (level)
  starting transfers between devices: 47.5 us -> 50.1 us
  waiting for transfers between devices: 4.49 us -> 2.2 us
  Pallas kernels: 26.4 us -> 25.6 us
    ppermute x7 -> x6, waiting for transfers between devices: 3.83 us -> 0.87 us  [swap(): return lax.ppermute(x, 'normal', [(i, i ^ bit) for i in range(count)])]
    ppermute x8, starting transfers between devices: 2.2 us -> 3.71 us  [shift_up(): return lax.ppermute(x, axis, [(i, (i + 1) % count) for i in range(count)])]
    ppermute x2, waiting for transfers between devices: 0.01 us -> 1.29 us  [swap_odd(): return lax.ppermute(x, axis, pairs)]
    ppermute x2, starting transfers between devices: 2.05 us -> 2.9 us  [swap_odd(): return lax.ppermute(x, axis, pairs)]
    pallas_call x22 -> x21, Pallas kernels: 26.4 us -> 25.6 us  [call(): pl.pallas_call(body, out_shape=shapes, in_specs=ins, out_specs=[spec for...]
    ppermute x7 -> x6, starting transfers between devices: 12.9 us -> 12.6 us  [swap(): return lax.ppermute(x, 'normal', [(i, i ^ bit) for i in range(count)])]
  transfers between devices with their start and end apart: 25 -> 24, of which waited for: 3 -> 2; matrix products, arithmetic and copies ran while one was open for 0% -> 0% of each run, Pallas kernels for 28% -> 26%
where the time goes in v5:
time: 79.2 us; the launch traced here: 79.1 us
  starting transfers between devices  50.1 us (63%)
  Pallas kernels  25.6 us (32%)
  waiting for transfers between devices  2.2 us (3%)
  between operations  1.13 us (1%)
    ppermute x8, starting transfers between devices, shift_down(): return lax.ppermute(x, axis, [((i + 1) % count, i) for i in range(count)])  30.9 us
    pallas_call x21, Pallas kernels, call(): pl.pallas_call(body, out_shape=shapes, in_specs=ins, out_specs=[spec for...  25.6 us
    ppermute x6, starting transfers between devices, swap(): return lax.ppermute(x, 'normal', [(i, i ^ bit) for i in range(count)])  12.6 us
    ppermute x8, starting transfers between devices, shift_up(): return lax.ppermute(x, axis, [(i, (i + 1) % count) for i in range(count)])  3.71 us
    ppermute x2, starting transfers between devices, swap_odd(): return lax.ppermute(x, axis, pairs)  2.9 us
  transfers between devices with their start and end apart: 24, of which 2 were waited for; matrix products, arithmetic and copies ran while one was open for 0% of the time, Pallas kernels for 26%

profile of v5, /device:TPU:1, one launch (start us, length us, event | category | flops | bytes accessed | tf_op | source)
XLA Modules:
  0.0 79.1 jit_solution(10134743185424219209)
XLA Ops:
  1.6 1.5 %collective-permute-start = (f32[1,8,384]{2,1,0:T(8,128)S(1)}, f32[1,8,384]{2,1,0:T(8,128)S(1)}, u32[]{:S(2)}, u32[]{:S(2)}) collective-permute-start(f32[1,8,384]{2,1,0:T(8,128)S(1)} %own.1.mine), channel_id=1, source_target_pairs={{0,1},{1,0},{2,3},{3,2},{4,5},{5,4},{6,7},{7,6},{8,9},{9,8},{10,11... | collective-permute-start | bytes 36872 | tf_op jit(solution)/shard_map/ppermute | solution.py:44
  3.1 2.5 %load.1 = (f32[6,3,512,128]{3,2,1,0:T(8,128)S(1)}, f32[5,3,16,128]{3,2,1,0:T(8,128)S(1)}, f32[4,3,16,128]{3,2,1,0:T(8,128)S(1)}, f32[5,3,32,128]{3,2,1,0:T(8,128)S(1)}, f32[4,3,32,128]{3,2,1,0:T(8,128)S(1)}) custom-call(f32[6,512,384]{2,1,0:T(8,128)} %bitcast.10), custom_call_target="tpu_custom_call" | custom-call | flops 1000000 | bytes 1000000 | tf_op jit(solution)/shard_map/load/pallas_call | solution.py:58
  5.6 1.5 %collective-permute-start.1 = (f32[2,8,384]{2,1,0:T(8,128)S(1)}, f32[2,8,384]{2,1,0:T(8,128)S(1)}, u32[]{:S(2)}, u32[]{:S(2)}) collective-permute-start(f32[2,8,384]{2,1,0:T(8,128)S(1)} %merge.3.mine), channel_id=1, source_target_pairs={{0,2},{1,3},{2,0},{3,1},{4,6},{5,7},{6,4},{7,5},{8,10},{9,11},{10,... | collective-permute-start | bytes 73736 | tf_op jit(solution)/shard_map/ppermute | solution.py:44
  7.1 6.2 %collective-permute-start.4 = (f32[4,3,16,128]{3,2,1,0:T(8,128)S(1)}, f32[4,3,16,128]{3,2,1,0:T(8,128)S(1)}, u32[]{:S(2)}, u32[]{:S(2)}) collective-permute-start(f32[4,3,16,128]{3,2,1,0:T(8,128)S(1)} %get-tuple-element.76), channel_id=1, source_target_pairs={{16,0},{32,16},{48,32},{64,48},{80,64},{96,80},{112,96},{0,112},{1... | collective-permute-start | bytes 294920 | tf_op jit(solution)/shard_map/ppermute | solution.py:30
  15.1 2.7 %collective-permute-start.2 = (f32[4,8,384]{2,1,0:T(8,128)S(1)}, f32[4,8,384]{2,1,0:T(8,128)S(1)}, u32[]{:S(2)}, u32[]{:S(2)}) collective-permute-start(f32[4,8,384]{2,1,0:T(8,128)S(1)} %merge.4.mine), channel_id=1, source_target_pairs={{0,4},{1,5},{2,6},{3,7},{4,0},{5,1},{6,2},{7,3},{8,12},{9,13},{10,... | collective-permute-start | bytes 147464 | tf_op jit(solution)/shard_map/ppermute | solution.py:44
  17.8 4.2 %velocity_first.1 = (f32[3,3,512,128]{3,2,1,0:T(8,128)S(1)}, f32[3,512,128]{2,1,0:T(8,128)S(1)}, f32[3,512,128]{2,1,0:T(8,128)S(1)}) custom-call(f32[6,3,512,128]{3,2,1,0:T(8,128)S(1)} %get-tuple-element.71.s.s_in, f32[3,512,384]{2,1,0:T(8,128)S(1)} %bitcast.6, f32[512,384]{1,0:T(8,128)S(1)} %bitcast.7, f32[512,384]{1,0:T(8,128)S(1)} %bitcast.8), custom_call_target="tpu_custom_call" | custom-call | flops 4000000000 | bytes 16000000 | tf_op jit(solution)/shard_map/velocity_first/pallas_call | solution.py:58
  23.8 1.8 %collective-permute-start.10 = (f32[4,3,32,128]{3,2,1,0:T(8,128)S(1)}, f32[4,3,32,128]{3,2,1,0:T(8,128)S(1)}, u32[]{:S(2)}, u32[]{:S(2)}) collective-permute-start(f32[4,3,32,128]{3,2,1,0:T(8,128)S(1)} %get-tuple-element.89), channel_id=1, source_target_pairs={{0,1},{1,2},{2,3},{3,4},{4,5},{5,6},{6,7},{7,8},{8,9},{9,10},{10,1... | collective-permute-start | bytes 589832 | tf_op jit(solution)/shard_map/ppermute | solution.py:25
  26.7 1.3 %collective-permute-done.7.refs_1_ = f32[3,80,128]{2,1,0:T(8,128)S(1)} collective-permute-done((f32[3,80,128]{2,1,0:T(8,128)S(1)}, f32[3,80,128]{2,1,0:T(8,128)S(1)}, u32[]{:S(2)}, u32[]{:S(2)}) %collective-permute-start.7) | collective-permute-done | bytes 122912 | tf_op jit(solution)/shard_map/ppermute | solution.py:39
  28.0 1.1 %fault.2 = (f32[3,3,512,128]{3,2,1,0:T(8,128)S(1)}, f32[4,3,16,128]{3,2,1,0:T(8,128)S(1)}, f32[5,3,16,128]{3,2,1,0:T(8,128)S(1)}, f32[3,32,128]{2,1,0:T(8,128)S(...) custom-call(f32[3,80,128]{2,1,0:T(8,128)S(1)} %get-tuple-element.80., ...), custom_call_target="tpu_custom_call", output_to_operand_aliasing={{0}: (4, {})} | custom-call | flops 1000000 | bytes 1000000 | tf_op jit(solution)/shard_map/fault/pallas_call | solution.py:58
  29.9 4.8 %collective-permute-start.9 = (f32[5,3,16,128]{3,2,1,0:T(8,128)S(1)}, f32[5,3,16,128]{3,2,1,0:T(8,128)S(1)}, u32[]{:S(2)}, u32[]{:S(2)}) collective-permute-start(f32[5,3,16,128]{3,2,1,0:T(8,128)S(1)} %get-tuple-element.88), channel_id=1, source_target_pairs={{16,0},{32,16},{48,32},{64,48},{80,64},{96,80},{112,96},{0,112},{1... | collective-permute-start | bytes 368648 | tf_op jit(solution)/shard_map/ppermute | solution.py:30
  34.7 3.3 %stress_first.1 = (f32[6,3,512,128]{3,2,1,0:T(8,128)S(1)}, f32[3,512,128]{2,1,0:T(8,128)S(1)}) custom-call(f32[3,3,512,128]{3,2,1,0:T(8,128)S(1)} %get-tuple-element.83.v.v_in, f32[6,3,512,128]{3,2,1,0:T(8,128)S(1)} %get-tuple-element.71.s.s_in, f32[3,512,128]{2,1,0:T(8,128)S(1)} %get-tuple-element.84.m_in), custom_call_target="tpu_custom_call", output_to_operand_aliasing={{0}: (1, {}), {1}: (2, {})} | custom-call | flops 4000000000 | bytes 16000000 | tf_op jit(solution)/shard_map/stress_first/pallas_call | solution.py:58
  39.1 4.6 %collective-permute-start.13 = (f32[4,3,16,128]{3,2,1,0:T(8,128)S(1)}, f32[4,3,16,128]{3,2,1,0:T(8,128)S(1)}, u32[]{:S(2)}, u32[]{:S(2)}) collective-permute-start(f32[4,3,16,128]{3,2,1,0:T(8,128)S(1)} %get-tuple-element.96), channel_id=1, source_target_pairs={{16,0},{32,16},{48,32},{64,48},{80,64},{96,80},{112,96},{0,112},{1... | collective-permute-start | bytes 294920 | tf_op jit(solution)/shard_map/ppermute | solution.py:30
  43.7 4.7 %collective-permute-start.15 = (f32[4,3,32,128]{3,2,1,0:T(8,128)S(1)}, f32[4,3,32,128]{3,2,1,0:T(8,128)S(1)}, u32[]{:S(2)}, u32[]{:S(2)}) collective-permute-start(f32[4,3,32,128]{3,2,1,0:T(8,128)S(1)} %get-tuple-element.98), channel_id=1, source_target_pairs={{1,0},{2,1},{3,2},{4,3},{5,4},{6,5},{7,6},{8,7},{9,8},{10,9},{11,1... | collective-permute-start | bytes 589832 | tf_op jit(solution)/shard_map/ppermute | solution.py:30
  48.4 3.3 %velocity.1.v_in = f32[3,3,512,128]{3,2,1,0:T(8,128)S(1)} custom-call(f32[6,3,512,128]{3,2,1,0:T(8,128)S(1)} %get-tuple-element.94.s.s_in, f32[3,3,512,128]{3,2,1,0:T(8,128)S(1)} %get-tuple-element.83.v.v_in, f32[3,512,128]{2,1,0:T(8,128)S(1)} %get-tuple-element.74.w.b_in), custom_call_target="tpu_custom_call", output_to_operand_aliasing={{}: (1, {})} | custom-call | flops 4000000000 | bytes 16000000 | tf_op jit(solution)/shard_map/velocity/pallas_call | solution.py:58
  52.4 2.8 %collective-permute-start.16 = (f32[3,32,128]{2,1,0:T(8,128)S(1)}, f32[3,32,128]{2,1,0:T(8,128)S(1)}, u32[]{:S(2)}, u32[]{:S(2)}) collective-permute-start(f32[3,32,128]{2,1,0:T(8,128)S(1)} %get-tuple-element.99.refs_0_), channel_id=1, source_target_pairs={{1,2},{2,1},{3,4},{4,3},{5,6},{6,5},{7,8},{8,7},{9,10},{10,9},{11,... | collective-permute-start | bytes 147464 | tf_op jit(solution)/shard_map/ppermute | solution.py:39
  55.4 3.8 %collective-permute-start.20 = (f32[5,3,32,128]{3,2,1,0:T(8,128)S(1)}, f32[5,3,32,128]{3,2,1,0:T(8,128)S(1)}, u32[]{:S(2)}, u32[]{:S(2)}) collective-permute-start(f32[5,3,32,128]{3,2,1,0:T(8,128)S(1)} %get-tuple-element.112), channel_id=1, source_target_pairs={{1,0},{2,1},{3,2},{4,3},{5,4},{6,5},{7,6},{8,7},{9,8},{10,9},{11,1... | collective-permute-start | bytes 737288 | tf_op jit(solution)/shard_map/ppermute | solution.py:30
  59.2 1.1 %fault.3 = (f32[3,3,512,128]{3,2,1,0:T(8,128)S(1)}, f32[4,3,16,128]{3,2,1,0:T(8,128)S(1)}, f32[5,3,16,128]{3,2,1,0:T(8,128)S(1)}, f32[3,32,128]{2,1,0:T(8,128)},...) custom-call(f32[3,32,128]{2,1,0:T(8,128)S(1)} %get-tuple-element.99., ...), custom_call_target="tpu_custom_call", output_to_operand_aliasing={{0}: (5, {})} | custom-call | flops 1000000 | bytes 1000000 | tf_op jit(solution)/shard_map/fault/pallas_call | solution.py:58
  60.8 5.1 %collective-permute-start.22 = (f32[5,3,16,128]{3,2,1,0:T(8,128)S(1)}, f32[5,3,16,128]{3,2,1,0:T(8,128)S(1)}, u32[]{:S(2)}, u32[]{:S(2)}) collective-permute-start(f32[5,3,16,128]{3,2,1,0:T(8,128)S(1)} %get-tuple-element.120), channel_id=1, source_target_pairs={{16,0},{32,16},{48,32},{64,48},{80,64},{96,80},{112,96},{0,112},{1... | collective-permute-start | bytes 368648 | tf_op jit(solution)/shard_map/ppermute | solution.py:30
  65.9 1.5 %last_slabs_0.1 = (f32[6,3,512,128]{3,2,1,0:T(8,128)S(1)}, f32[3,512,384]{2,1,0:T(8,128)}) custom-call(f32[3,3,512,128]{3,2,1,0:T(8,128)S(1)} %get-tuple-element.104.v, f32[6,3,512,128]{3,2,1,0:T(8,128)S(1)} %get-tuple-element.94.s.s_in, f32[3,512,128]{2,1,0:T(8,128)S(1)} %get-tuple-element.86.w.m, ...), custom_call_target="tpu_custom_call", output_to_operand_aliasing={{0}: (1, {})} | custom-call | flops 4000000000 | bytes 16000000 | tf_op jit(solution)/shard_map/last_slabs_0/pallas_call | solution.py:58
  67.5 4.7 %collective-permute-start.18 = (f32[2,3,16,128]{3,2,1,0:T(8,128)S(1)}, f32[2,3,16,128]{3,2,1,0:T(8,128)S(1)}, u32[]{:S(2)}, u32[]{:S(2)}) collective-permute-start(f32[2,3,16,128]{3,2,1,0:T(8,128)S(1)} %choose.2.mine), channel_id=1, source_target_pairs={{0,2},{1,3},{2,0},{3,1},{4,6},{5,7},{6,4},{7,5},{8,10},{9,11},{10,... | collective-permute-start | bytes 147464 | tf_op jit(solution)/shard_map/ppermute | solution.py:44
  72.2 2.0 %last_slabs_1.1 = (f32[6,3,512,128]{3,2,1,0:T(8,128)S(1)}, f32[6,512,384]{2,1,0:T(8,128)}) custom-call(f32[3,3,512,128]{3,2,1,0:T(8,128)S(1)} %get-tuple-element.104.v, f32[6,3,512,128]{3,2,1,0:T(8,128)S(1)} %get-tuple-element.110.s_in, f32[3,512,128]{2,1,0:T(8,128)S(1)} %get-tuple-element.86.w.m, ...), custom_call_target="tpu_custom_call", output_to_operand_aliasing={{0}: (1, {})} | custom-call | flops 2000000000 | bytes 8000000 | tf_op jit(solution)/shard_map/last_slabs_1/pallas_call | solution.py:58
  74.3 1.7 %collective-permute-start.23 = (f32[2,3,16,128]{3,2,1,0:T(8,128)S(1)}, f32[2,3,16,128]{3,2,1,0:T(8,128)S(1)}, u32[]{:S(2)}, u32[]{:S(2)}) collective-permute-start(f32[2,3,16,128]{3,2,1,0:T(8,128)S(1)} %choose.3.mine), channel_id=1, source_target_pairs={{0,1},{1,0},{2,3},{3,2},{4,5},{5,4},{6,7},{7,6},{8,9},{9,8},{10,11... | collective-permute-start | bytes 147464 | tf_op jit(solution)/shard_map/ppermute | solution.py:44
  76.0 1.3 %last_slabs_2.1 = (f32[6,3,512,128]{3,2,1,0:T(8,128)S(1)}, f32[6,512,384]{2,1,0:T(8,128)}) custom-call(f32[3,3,512,128]{3,2,1,0:T(8,128)S(1)} %get-tuple-element.104.v, f32[6,3,512,128]{3,2,1,0:T(8,128)S(1)} %get-tuple-element.116.s_in, f32[3,512,128]{2,1,0:T(8,128)S(1)} %get-tuple-element.86.w.m, ...), custom_call_target="tpu_custom_call", output_to_operand_aliasing={{0}: (1, {}), {1}: (4, {})} | custom-call | flops 2000000000 | bytes 8000000 | tf_op jit(solution)/shard_map/last_slabs_2/pallas_call | solution.py:58
  77.3 1.7 %edges_last.1 = (f32[6,512,384]{2,1,0:T(8,128)}, f32[2,384]{1,0:T(2,128)}, f32[2,384]{1,0:T(2,128)}) custom-call(f32[6,3,512,128]{3,2,1,0:T(8,128)S(1)} %get-tuple-element.118.s, f32[3,512,128]{2,1,0:T(8,128)S(1)} %get-tuple-element.86.w.m, f32[4,3,16,128]{3,2,1,0:T(8,128)S(1)} %collective-permute-done.21.xl, ...), custom_call_target="tpu_custom_call", output_to_operand_aliasing={{0}: (7, {})} | custom-call | flops 1000000 | bytes 1000000 | tf_op jit(solution)/shard_map/edges_last/pallas_call | solution.py:58
  (53 shorter events, 8.9 us)
Async XLA Ops:
  1.6 4.0 %collective-permute-start = (f32[1,8,384]{2,1,0:T(8,128)S(1)}, f32[1,8,384]{2,1,0:T(8,128)S(1)}, u32[]{:S(2)}, u32[]{:S(2)}) collective-permute-start(f32[1,8,384]{2,1,0:T(8,128)S(1)} %own.1.mine), channel_id=1, source_target_pairs={{0,1},{1,0},{2,3},{3,2},{4,5},{5,4},{6,7},{7,6},{8,9},{9,8},{10,11... | collective-permute-start | bytes 36872 | tf_op jit(solution)/shard_map/ppermute | solution.py:44
  5.6 9.4 %collective-permute-start.1 = (f32[2,8,384]{2,1,0:T(8,128)S(1)}, f32[2,8,384]{2,1,0:T(8,128)S(1)}, u32[]{:S(2)}, u32[]{:S(2)}) collective-permute-start(f32[2,8,384]{2,1,0:T(8,128)S(1)} %merge.3.mine), channel_id=1, source_target_pairs={{0,2},{1,3},{2,0},{3,1},{4,6},{5,7},{6,4},{7,5},{8,10},{9,11},{10,... | collective-permute-start | bytes 73736 | tf_op jit(solution)/shard_map/ppermute | solution.py:44
  7.1 15.8 %collective-permute-start.4 = (f32[4,3,16,128]{3,2,1,0:T(8,128)S(1)}, f32[4,3,16,128]{3,2,1,0:T(8,128)S(1)}, u32[]{:S(2)}, u32[]{:S(2)}) collective-permute-start(f32[4,3,16,128]{3,2,1,0:T(8,128)S(1)} %get-tuple-element.76), channel_id=1, source_target_pairs={{16,0},{32,16},{48,32},{64,48},{80,64},{96,80},{112,96},{0,112},{1... | collective-permute-start | bytes 294920 | tf_op jit(solution)/shard_map/ppermute | solution.py:30
  13.3 9.6 %collective-permute-start.3 = (f32[5,3,16,128]{3,2,1,0:T(8,128)S(1)}, f32[5,3,16,128]{3,2,1,0:T(8,128)S(1)}, u32[]{:S(2)}, u32[]{:S(2)}) collective-permute-start(f32[5,3,16,128]{3,2,1,0:T(8,128)S(1)} %get-tuple-element.75), channel_id=1, source_target_pairs={{0,16},{16,32},{32,48},{48,64},{64,80},{80,96},{96,112},{112,0},{1... | collective-permute-start | bytes 368648 | tf_op jit(solution)/shard_map/ppermute | solution.py:25
  13.3 9.6 %collective-permute-start.6 = (f32[4,3,32,128]{3,2,1,0:T(8,128)S(1)}, f32[4,3,32,128]{3,2,1,0:T(8,128)S(1)}, u32[]{:S(2)}, u32[]{:S(2)}) collective-permute-start(f32[4,3,32,128]{3,2,1,0:T(8,128)S(1)} %get-tuple-element.78), channel_id=1, source_target_pairs={{1,0},{2,1},{3,2},{4,3},{5,4},{6,5},{7,6},{8,7},{9,8},{10,9},{11,1... | collective-permute-start | bytes 589832 | tf_op jit(solution)/shard_map/ppermute | solution.py:30
  14.1 8.8 %collective-permute-start.5 = (f32[5,3,32,128]{3,2,1,0:T(8,128)S(1)}, f32[5,3,32,128]{3,2,1,0:T(8,128)S(1)}, u32[]{:S(2)}, u32[]{:S(2)}) collective-permute-start(f32[5,3,32,128]{3,2,1,0:T(8,128)S(1)} %get-tuple-element.77), channel_id=1, source_target_pairs={{0,1},{1,2},{2,3},{3,4},{4,5},{5,6},{6,7},{7,8},{8,9},{9,10},{10,1... | collective-permute-start | bytes 737288 | tf_op jit(solution)/shard_map/ppermute | solution.py:25
  15.1 7.8 %collective-permute-start.2 = (f32[4,8,384]{2,1,0:T(8,128)S(1)}, f32[4,8,384]{2,1,0:T(8,128)S(1)}, u32[]{:S(2)}, u32[]{:S(2)}) collective-permute-start(f32[4,8,384]{2,1,0:T(8,128)S(1)} %merge.4.mine), channel_id=1, source_target_pairs={{0,4},{1,5},{2,6},{3,7},{4,0},{5,1},{6,2},{7,3},{8,12},{9,13},{10,... | collective-permute-start | bytes 147464 | tf_op jit(solution)/shard_map/ppermute | solution.py:44
  23.6 4.4 %collective-permute-start.7 = (f32[3,80,128]{2,1,0:T(8,128)S(1)}, f32[3,80,128]{2,1,0:T(8,128)S(1)}, u32[]{:S(2)}, u32[]{:S(2)}) collective-permute-start(f32[3,80,128]{2,1,0:T(8,128)S(1)} %get-tuple-element.80.refs_0_), channel_id=1, source_target_pairs={{1,2},{2,1},{3,4},{4,3},{5,6},{6,5},{7,8},{8,7},{9,10},{10,9},{11,... | collective-permute-start | bytes 368648 | tf_op jit(solution)/shard_map/ppermute | solution.py:39
  23.8 14.2 %collective-permute-start.10 = (f32[4,3,32,128]{3,2,1,0:T(8,128)S(1)}, f32[4,3,32,128]{3,2,1,0:T(8,128)S(1)}, u32[]{:S(2)}, u32[]{:S(2)}) collective-permute-start(f32[4,3,32,128]{3,2,1,0:T(8,128)S(1)} %get-tuple-element.89), channel_id=1, source_target_pairs={{0,1},{1,2},{2,3},{3,4},{4,5},{5,6},{6,7},{7,8},{8,9},{9,10},{10,1... | collective-permute-start | bytes 589832 | tf_op jit(solution)/shard_map/ppermute | solution.py:25
  25.6 12.4 %collective-permute-start.11 = (f32[5,3,32,128]{3,2,1,0:T(8,128)S(1)}, f32[5,3,32,128]{3,2,1,0:T(8,128)S(1)}, u32[]{:S(2)}, u32[]{:S(2)}) collective-permute-start(f32[5,3,32,128]{3,2,1,0:T(8,128)S(1)} %get-tuple-element.90), channel_id=1, source_target_pairs={{1,0},{2,1},{3,2},{4,3},{5,4},{6,5},{7,6},{8,7},{9,8},{10,9},{11,1... | collective-permute-start | bytes 737288 | tf_op jit(solution)/shard_map/ppermute | solution.py:30
  29.1 9.0 %collective-permute-start.8 = (f32[4,3,16,128]{3,2,1,0:T(8,128)S(1)}, f32[4,3,16,128]{3,2,1,0:T(8,128)S(1)}, u32[]{:S(2)}, u32[]{:S(2)}) collective-permute-start(f32[4,3,16,128]{3,2,1,0:T(8,128)S(1)} %get-tuple-element.87), channel_id=1, source_target_pairs={{0,16},{16,32},{32,48},{48,64},{64,80},{80,96},{96,112},{112,0},{1... | collective-permute-start | bytes 294920 | tf_op jit(solution)/shard_map/ppermute | solution.py:25
  29.9 8.1 %collective-permute-start.9 = (f32[5,3,16,128]{3,2,1,0:T(8,128)S(1)}, f32[5,3,16,128]{3,2,1,0:T(8,128)S(1)}, u32[]{:S(2)}, u32[]{:S(2)}) collective-permute-start(f32[5,3,16,128]{3,2,1,0:T(8,128)S(1)} %get-tuple-element.88), channel_id=1, source_target_pairs={{16,0},{32,16},{48,32},{64,48},{80,64},{96,80},{112,96},{0,112},{1... | collective-permute-start | bytes 368648 | tf_op jit(solution)/shard_map/ppermute | solution.py:30
  39.1 12.6 %collective-permute-start.13 = (f32[4,3,16,128]{3,2,1,0:T(8,128)S(1)}, f32[4,3,16,128]{3,2,1,0:T(8,128)S(1)}, u32[]{:S(2)}, u32[]{:S(2)}) collective-permute-start(f32[4,3,16,128]{3,2,1,0:T(8,128)S(1)} %get-tuple-element.96), channel_id=1, source_target_pairs={{16,0},{32,16},{48,32},{64,48},{80,64},{96,80},{112,96},{0,112},{1... | collective-permute-start | bytes 294920 | tf_op jit(solution)/shard_map/ppermute | solution.py:30
  43.7 8.0 %collective-permute-start.12 = (f32[5,3,16,128]{3,2,1,0:T(8,128)S(1)}, f32[5,3,16,128]{3,2,1,0:T(8,128)S(1)}, u32[]{:S(2)}, u32[]{:S(2)}) collective-permute-start(f32[5,3,16,128]{3,2,1,0:T(8,128)S(1)} %get-tuple-element.95), channel_id=1, source_target_pairs={{0,16},{16,32},{32,48},{48,64},{64,80},{80,96},{96,112},{112,0},{1... | collective-permute-start | bytes 368648 | tf_op jit(solution)/shard_map/ppermute | solution.py:25
  43.7 8.0 %collective-permute-start.15 = (f32[4,3,32,128]{3,2,1,0:T(8,128)S(1)}, f32[4,3,32,128]{3,2,1,0:T(8,128)S(1)}, u32[]{:S(2)}, u32[]{:S(2)}) collective-permute-start(f32[4,3,32,128]{3,2,1,0:T(8,128)S(1)} %get-tuple-element.98), channel_id=1, source_target_pairs={{1,0},{2,1},{3,2},{4,3},{5,4},{6,5},{7,6},{8,7},{9,8},{10,9},{11,1... | collective-permute-start | bytes 589832 | tf_op jit(solution)/shard_map/ppermute | solution.py:30
  48.4 3.3 %collective-permute-start.14 = (f32[5,3,32,128]{3,2,1,0:T(8,128)S(1)}, f32[5,3,32,128]{3,2,1,0:T(8,128)S(1)}, u32[]{:S(2)}, u32[]{:S(2)}) collective-permute-start(f32[5,3,32,128]{3,2,1,0:T(8,128)S(1)} %get-tuple-element.97), channel_id=1, source_target_pairs={{0,1},{1,2},{2,3},{3,4},{4,5},{5,6},{6,7},{7,8},{8,9},{9,10},{10,1... | collective-permute-start | bytes 737288 | tf_op jit(solution)/shard_map/ppermute | solution.py:25
  52.4 6.8 %collective-permute-start.16 = (f32[3,32,128]{2,1,0:T(8,128)S(1)}, f32[3,32,128]{2,1,0:T(8,128)S(1)}, u32[]{:S(2)}, u32[]{:S(2)}) collective-permute-start(f32[3,32,128]{2,1,0:T(8,128)S(1)} %get-tuple-element.99.refs_0_), channel_id=1, source_target_pairs={{1,2},{2,1},{3,4},{4,3},{5,6},{6,5},{7,8},{8,7},{9,10},{10,9},{11,... | collective-permute-start | bytes 147464 | tf_op jit(solution)/shard_map/ppermute | solution.py:39
  55.3 16.8 %collective-permute-start.19 = (f32[4,3,32,128]{3,2,1,0:T(8,128)S(1)}, f32[4,3,32,128]{3,2,1,0:T(8,128)S(1)}, u32[]{:S(2)}, u32[]{:S(2)}) collective-permute-start(f32[4,3,32,128]{3,2,1,0:T(8,128)S(1)} %get-tuple-element.111), channel_id=1, source_target_pairs={{0,1},{1,2},{2,3},{3,4},{4,5},{5,6},{6,7},{7,8},{8,9},{9,10},{10,1... | collective-permute-start | bytes 589832 | tf_op jit(solution)/shard_map/ppermute | solution.py:25
  55.4 16.7 %collective-permute-start.20 = (f32[5,3,32,128]{3,2,1,0:T(8,128)S(1)}, f32[5,3,32,128]{3,2,1,0:T(8,128)S(1)}, u32[]{:S(2)}, u32[]{:S(2)}) collective-permute-start(f32[5,3,32,128]{3,2,1,0:T(8,128)S(1)} %get-tuple-element.112), channel_id=1, source_target_pairs={{1,0},{2,1},{3,2},{4,3},{5,4},{6,5},{7,6},{8,7},{9,8},{10,9},{11,1... | collective-permute-start | bytes 737288 | tf_op jit(solution)/shard_map/ppermute | solution.py:30
  60.3 7.2 %collective-permute-start.17 = (f32[2,3,16,128]{3,2,1,0:T(8,128)S(1)}, f32[2,3,16,128]{3,2,1,0:T(8,128)S(1)}, u32[]{:S(2)}, u32[]{:S(2)}) collective-permute-start(f32[2,3,16,128]{3,2,1,0:T(8,128)S(1)} %get-tuple-element.107.mine), channel_id=1, source_target_pairs={{0,4},{1,5},{2,6},{3,7},{4,0},{5,1},{6,2},{7,3},{8,12},{9,13},{10,... | collective-permute-start | bytes 147464 | tf_op jit(solution)/shard_map/ppermute | solution.py:44
  60.8 16.4 %collective-permute-start.21 = (f32[4,3,16,128]{3,2,1,0:T(8,128)S(1)}, f32[4,3,16,128]{3,2,1,0:T(8,128)S(1)}, u32[]{:S(2)}, u32[]{:S(2)}) collective-permute-start(f32[4,3,16,128]{3,2,1,0:T(8,128)S(1)} %get-tuple-element.119), channel_id=1, source_target_pairs={{0,16},{16,32},{32,48},{48,64},{64,80},{80,96},{96,112},{112,0},{1... | collective-permute-start | bytes 294920 | tf_op jit(solution)/shard_map/ppermute | solution.py:25
  60.8 16.4 %collective-permute-start.22 = (f32[5,3,16,128]{3,2,1,0:T(8,128)S(1)}, f32[5,3,16,128]{3,2,1,0:T(8,128)S(1)}, u32[]{:S(2)}, u32[]{:S(2)}) collective-permute-start(f32[5,3,16,128]{3,2,1,0:T(8,128)S(1)} %get-tuple-element.120), channel_id=1, source_target_pairs={{16,0},{32,16},{48,32},{64,48},{80,64},{96,80},{112,96},{0,112},{1... | collective-permute-start | bytes 368648 | tf_op jit(solution)/shard_map/ppermute | solution.py:30
  67.5 6.7 %collective-permute-start.18 = (f32[2,3,16,128]{3,2,1,0:T(8,128)S(1)}, f32[2,3,16,128]{3,2,1,0:T(8,128)S(1)}, u32[]{:S(2)}, u32[]{:S(2)}) collective-permute-start(f32[2,3,16,128]{3,2,1,0:T(8,128)S(1)} %choose.2.mine), channel_id=1, source_target_pairs={{0,2},{1,3},{2,0},{3,1},{4,6},{5,7},{6,4},{7,5},{8,10},{9,11},{10,... | collective-permute-start | bytes 147464 | tf_op jit(solution)/shard_map/ppermute | solution.py:44
  74.3 3.0 %collective-permute-start.23 = (f32[2,3,16,128]{3,2,1,0:T(8,128)S(1)}, f32[2,3,16,128]{3,2,1,0:T(8,128)S(1)}, u32[]{:S(2)}, u32[]{:S(2)}) collective-permute-start(f32[2,3,16,128]{3,2,1,0:T(8,128)S(1)} %choose.3.mine), channel_id=1, source_target_pairs={{0,1},{1,0},{2,3},{3,2},{4,5},{5,4},{6,7},{7,6},{8,9},{9,8},{10,11... | collective-permute-start | bytes 147464 | tf_op jit(solution)/shard_map/ppermute | solution.py:44
  (4 other events, 56.5 us)

commit v6 on v5

--- a/solution.py
+++ b/solution.py
@@ -237,7 +237,7 @@
             body(x, True)
 
 
-LOADS = 4
+LOADS = 2
 
 
 def velocity_body(nx, ny, first, s, v_in, b_in, *refs):

time: 79.2 us -> 79 us (level)
  no operation moved by 1% of the time
where the time goes in v6:
time: 79 us; the launch traced here: 78.9 us
  starting transfers between devices  50 us (63%)
  Pallas kernels  25.3 us (32%)
  waiting for transfers between devices  2.51 us (3%)
  between operations  1.13 us (1%)
    ppermute x8, starting transfers between devices, shift_down(): return lax.ppermute(x, axis, [((i + 1) % count, i) for i in range(count)])  30.8 us
    pallas_call x21, Pallas kernels, call(): pl.pallas_call(body, out_shape=shapes, in_specs=ins, out_specs=[spec for...  25.3 us
    ppermute x6, starting transfers between devices, swap(): return lax.ppermute(x, 'normal', [(i, i ^ bit) for i in range(count)])  12.4 us
    ppermute x8, starting transfers between devices, shift_up(): return lax.ppermute(x, axis, [(i, (i + 1) % count) for i in range(count)])  3.89 us
    ppermute x2, starting transfers between devices, swap_odd(): return lax.ppermute(x, axis, pairs)  2.85 us
  transfers between devices with their start and end apart: 24, of which 2 were waited for; matrix products, arithmetic and copies ran while one was open for 0% of the time, Pallas kernels for 26%

profile of v6, /device:TPU:1, one launch (start us, length us, event | category | flops | bytes accessed | tf_op | source)
XLA Modules:
  0.0 78.9 jit_solution(2857909223094544860)
XLA Ops:
  1.6 1.5 %collective-permute-start = (f32[1,8,384]{2,1,0:T(8,128)S(1)}, f32[1,8,384]{2,1,0:T(8,128)S(1)}, u32[]{:S(2)}, u32[]{:S(2)}) collective-permute-start(f32[1,8,384]{2,1,0:T(8,128)S(1)} %own.1.mine), channel_id=1, source_target_pairs={{0,1},{1,0},{2,3},{3,2},{4,5},{5,4},{6,7},{7,6},{8,9},{9,8},{10,11... | collective-permute-start | bytes 36872 | tf_op jit(solution)/shard_map/ppermute | solution.py:44
  3.1 2.5 %load.1 = (f32[6,3,512,128]{3,2,1,0:T(8,128)S(1)}, f32[5,3,16,128]{3,2,1,0:T(8,128)S(1)}, f32[4,3,16,128]{3,2,1,0:T(8,128)S(1)}, f32[5,3,32,128]{3,2,1,0:T(8,128)S(1)}, f32[4,3,32,128]{3,2,1,0:T(8,128)S(1)}) custom-call(f32[6,512,384]{2,1,0:T(8,128)} %bitcast.10), custom_call_target="tpu_custom_call" | custom-call | flops 1000000 | bytes 1000000 | tf_op jit(solution)/shard_map/load/pallas_call | solution.py:58
  5.6 1.5 %collective-permute-start.1 = (f32[2,8,384]{2,1,0:T(8,128)S(1)}, f32[2,8,384]{2,1,0:T(8,128)S(1)}, u32[]{:S(2)}, u32[]{:S(2)}) collective-permute-start(f32[2,8,384]{2,1,0:T(8,128)S(1)} %merge.3.mine), channel_id=1, source_target_pairs={{0,2},{1,3},{2,0},{3,1},{4,6},{5,7},{6,4},{7,5},{8,10},{9,11},{10,... | collective-permute-start | bytes 73736 | tf_op jit(solution)/shard_map/ppermute | solution.py:44
  7.1 6.2 %collective-permute-start.4 = (f32[4,3,16,128]{3,2,1,0:T(8,128)S(1)}, f32[4,3,16,128]{3,2,1,0:T(8,128)S(1)}, u32[]{:S(2)}, u32[]{:S(2)}) collective-permute-start(f32[4,3,16,128]{3,2,1,0:T(8,128)S(1)} %get-tuple-element.76), channel_id=1, source_target_pairs={{16,0},{32,16},{48,32},{64,48},{80,64},{96,80},{112,96},{0,112},{1... | collective-permute-start | bytes 294920 | tf_op jit(solution)/shard_map/ppermute | solution.py:30
  15.1 2.7 %collective-permute-start.2 = (f32[4,8,384]{2,1,0:T(8,128)S(1)}, f32[4,8,384]{2,1,0:T(8,128)S(1)}, u32[]{:S(2)}, u32[]{:S(2)}) collective-permute-start(f32[4,8,384]{2,1,0:T(8,128)S(1)} %merge.4.mine), channel_id=1, source_target_pairs={{0,4},{1,5},{2,6},{3,7},{4,0},{5,1},{6,2},{7,3},{8,12},{9,13},{10,... | collective-permute-start | bytes 147464 | tf_op jit(solution)/shard_map/ppermute | solution.py:44
  17.8 3.9 %velocity_first.1 = (f32[3,3,512,128]{3,2,1,0:T(8,128)S(1)}, f32[3,512,128]{2,1,0:T(8,128)S(1)}, f32[3,512,128]{2,1,0:T(8,128)S(1)}) custom-call(f32[6,3,512,128]{3,2,1,0:T(8,128)S(1)} %get-tuple-element.71.s.s_in, f32[3,512,384]{2,1,0:T(8,128)S(1)} %bitcast.6, f32[512,384]{1,0:T(8,128)S(1)} %bitcast.7, f32[512,384]{1,0:T(8,128)S(1)} %bitcast.8), custom_call_target="tpu_custom_call" | custom-call | flops 4000000000 | bytes 16000000 | tf_op jit(solution)/shard_map/velocity_first/pallas_call | solution.py:58
  21.7 1.2 %collective-permute-done.2.got = f32[4,8,384]{2,1,0:T(8,128)S(1)} collective-permute-done((f32[4,8,384]{2,1,0:T(8,128)S(1)}, f32[4,8,384]{2,1,0:T(8,128)S(1)}, u32[]{:S(2)}, u32[]{:S(2)}) %collective-permute-start.2) | collective-permute-done | bytes 49184 | tf_op jit(solution)/shard_map/ppermute | solution.py:44
  23.8 1.8 %collective-permute-start.10 = (f32[4,3,32,128]{3,2,1,0:T(8,128)S(1)}, f32[4,3,32,128]{3,2,1,0:T(8,128)S(1)}, u32[]{:S(2)}, u32[]{:S(2)}) collective-permute-start(f32[4,3,32,128]{3,2,1,0:T(8,128)S(1)} %get-tuple-element.89), channel_id=1, source_target_pairs={{0,1},{1,2},{2,3},{3,4},{4,5},{5,6},{6,7},{7,8},{8,9},{9,10},{10,1... | collective-permute-start | bytes 589832 | tf_op jit(solution)/shard_map/ppermute | solution.py:25
  26.7 1.3 %collective-permute-done.7.refs_1_ = f32[3,80,128]{2,1,0:T(8,128)S(1)} collective-permute-done((f32[3,80,128]{2,1,0:T(8,128)S(1)}, f32[3,80,128]{2,1,0:T(8,128)S(1)}, u32[]{:S(2)}, u32[]{:S(2)}) %collective-permute-start.7) | collective-permute-done | bytes 122912 | tf_op jit(solution)/shard_map/ppermute | solution.py:39
  28.0 1.1 %fault.2 = (f32[3,3,512,128]{3,2,1,0:T(8,128)S(1)}, f32[4,3,16,128]{3,2,1,0:T(8,128)S(1)}, f32[5,3,16,128]{3,2,1,0:T(8,128)S(1)}, f32[3,32,128]{2,1,0:T(8,128)S(...) custom-call(f32[3,80,128]{2,1,0:T(8,128)S(1)} %get-tuple-element.80., ...), custom_call_target="tpu_custom_call", output_to_operand_aliasing={{0}: (4, {})} | custom-call | flops 1000000 | bytes 1000000 | tf_op jit(solution)/shard_map/fault/pallas_call | solution.py:58
  29.9 4.8 %collective-permute-start.9 = (f32[5,3,16,128]{3,2,1,0:T(8,128)S(1)}, f32[5,3,16,128]{3,2,1,0:T(8,128)S(1)}, u32[]{:S(2)}, u32[]{:S(2)}) collective-permute-start(f32[5,3,16,128]{3,2,1,0:T(8,128)S(1)} %get-tuple-element.88), channel_id=1, source_target_pairs={{16,0},{32,16},{48,32},{64,48},{80,64},{96,80},{112,96},{0,112},{1... | collective-permute-start | bytes 368648 | tf_op jit(solution)/shard_map/ppermute | solution.py:30
  34.7 3.3 %stress_first.1 = (f32[6,3,512,128]{3,2,1,0:T(8,128)S(1)}, f32[3,512,128]{2,1,0:T(8,128)S(1)}) custom-call(f32[3,3,512,128]{3,2,1,0:T(8,128)S(1)} %get-tuple-element.83.v.v_in, f32[6,3,512,128]{3,2,1,0:T(8,128)S(1)} %get-tuple-element.71.s.s_in, f32[3,512,128]{2,1,0:T(8,128)S(1)} %get-tuple-element.84.m_in), custom_call_target="tpu_custom_call", output_to_operand_aliasing={{0}: (1, {}), {1}: (2, {})} | custom-call | flops 4000000000 | bytes 16000000 | tf_op jit(solution)/shard_map/stress_first/pallas_call | solution.py:58
  39.1 4.6 %collective-permute-start.13 = (f32[4,3,16,128]{3,2,1,0:T(8,128)S(1)}, f32[4,3,16,128]{3,2,1,0:T(8,128)S(1)}, u32[]{:S(2)}, u32[]{:S(2)}) collective-permute-start(f32[4,3,16,128]{3,2,1,0:T(8,128)S(1)} %get-tuple-element.96), channel_id=1, source_target_pairs={{16,0},{32,16},{48,32},{64,48},{80,64},{96,80},{112,96},{0,112},{1... | collective-permute-start | bytes 294920 | tf_op jit(solution)/shard_map/ppermute | solution.py:30
  43.7 4.7 %collective-permute-start.15 = (f32[4,3,32,128]{3,2,1,0:T(8,128)S(1)}, f32[4,3,32,128]{3,2,1,0:T(8,128)S(1)}, u32[]{:S(2)}, u32[]{:S(2)}) collective-permute-start(f32[4,3,32,128]{3,2,1,0:T(8,128)S(1)} %get-tuple-element.98), channel_id=1, source_target_pairs={{1,0},{2,1},{3,2},{4,3},{5,4},{6,5},{7,6},{8,7},{9,8},{10,9},{11,1... | collective-permute-start | bytes 589832 | tf_op jit(solution)/shard_map/ppermute | solution.py:30
  48.4 3.3 %velocity.1.v_in = f32[3,3,512,128]{3,2,1,0:T(8,128)S(1)} custom-call(f32[6,3,512,128]{3,2,1,0:T(8,128)S(1)} %get-tuple-element.94.s.s_in, f32[3,3,512,128]{3,2,1,0:T(8,128)S(1)} %get-tuple-element.83.v.v_in, f32[3,512,128]{2,1,0:T(8,128)S(1)} %get-tuple-element.74.w.b_in), custom_call_target="tpu_custom_call", output_to_operand_aliasing={{}: (1, {})} | custom-call | flops 4000000000 | bytes 16000000 | tf_op jit(solution)/shard_map/velocity/pallas_call | solution.py:58
  52.4 2.8 %collective-permute-start.16 = (f32[3,32,128]{2,1,0:T(8,128)S(1)}, f32[3,32,128]{2,1,0:T(8,128)S(1)}, u32[]{:S(2)}, u32[]{:S(2)}) collective-permute-start(f32[3,32,128]{2,1,0:T(8,128)S(1)} %get-tuple-element.99.refs_0_), channel_id=1, source_target_pairs={{1,2},{2,1},{3,4},{4,3},{5,6},{6,5},{7,8},{8,7},{9,10},{10,9},{11,... | collective-permute-start | bytes 147464 | tf_op jit(solution)/shard_map/ppermute | solution.py:39
  55.6 3.6 %collective-permute-start.20 = (f32[5,3,32,128]{3,2,1,0:T(8,128)S(1)}, f32[5,3,32,128]{3,2,1,0:T(8,128)S(1)}, u32[]{:S(2)}, u32[]{:S(2)}) collective-permute-start(f32[5,3,32,128]{3,2,1,0:T(8,128)S(1)} %get-tuple-element.112), channel_id=1, source_target_pairs={{1,0},{2,1},{3,2},{4,3},{5,4},{6,5},{7,6},{8,7},{9,8},{10,9},{11,1... | collective-permute-start | bytes 737288 | tf_op jit(solution)/shard_map/ppermute | solution.py:30
  60.7 5.1 %collective-permute-start.22 = (f32[5,3,16,128]{3,2,1,0:T(8,128)S(1)}, f32[5,3,16,128]{3,2,1,0:T(8,128)S(1)}, u32[]{:S(2)}, u32[]{:S(2)}) collective-permute-start(f32[5,3,16,128]{3,2,1,0:T(8,128)S(1)} %get-tuple-element.120), channel_id=1, source_target_pairs={{16,0},{32,16},{48,32},{64,48},{80,64},{96,80},{112,96},{0,112},{1... | collective-permute-start | bytes 368648 | tf_op jit(solution)/shard_map/ppermute | solution.py:30
  65.7 1.5 %last_slabs_0.1 = (f32[6,3,512,128]{3,2,1,0:T(8,128)S(1)}, f32[3,512,384]{2,1,0:T(8,128)}) custom-call(f32[3,3,512,128]{3,2,1,0:T(8,128)S(1)} %get-tuple-element.104.v, f32[6,3,512,128]{3,2,1,0:T(8,128)S(1)} %get-tuple-element.94.s.s_in, f32[3,512,128]{2,1,0:T(8,128)S(1)} %get-tuple-element.86.w.m, ...), custom_call_target="tpu_custom_call", output_to_operand_aliasing={{0}: (1, {})} | custom-call | flops 4000000000 | bytes 16000000 | tf_op jit(solution)/shard_map/last_slabs_0/pallas_call | solution.py:58
  67.3 4.7 %collective-permute-start.18 = (f32[2,3,16,128]{3,2,1,0:T(8,128)S(1)}, f32[2,3,16,128]{3,2,1,0:T(8,128)S(1)}, u32[]{:S(2)}, u32[]{:S(2)}) collective-permute-start(f32[2,3,16,128]{3,2,1,0:T(8,128)S(1)} %choose.2.mine), channel_id=1, source_target_pairs={{0,2},{1,3},{2,0},{3,1},{4,6},{5,7},{6,4},{7,5},{8,10},{9,11},{10,... | collective-permute-start | bytes 147464 | tf_op jit(solution)/shard_map/ppermute | solution.py:44
  72.0 2.0 %last_slabs_1.1 = (f32[6,3,512,128]{3,2,1,0:T(8,128)S(1)}, f32[6,512,384]{2,1,0:T(8,128)}) custom-call(f32[3,3,512,128]{3,2,1,0:T(8,128)S(1)} %get-tuple-element.104.v, f32[6,3,512,128]{3,2,1,0:T(8,128)S(1)} %get-tuple-element.110.s_in, f32[3,512,128]{2,1,0:T(8,128)S(1)} %get-tuple-element.86.w.m, ...), custom_call_target="tpu_custom_call", output_to_operand_aliasing={{0}: (1, {})} | custom-call | flops 2000000000 | bytes 8000000 | tf_op jit(solution)/shard_map/last_slabs_1/pallas_call | solution.py:58
  74.1 1.7 %collective-permute-start.23 = (f32[2,3,16,128]{3,2,1,0:T(8,128)S(1)}, f32[2,3,16,128]{3,2,1,0:T(8,128)S(1)}, u32[]{:S(2)}, u32[]{:S(2)}) collective-permute-start(f32[2,3,16,128]{3,2,1,0:T(8,128)S(1)} %choose.3.mine), channel_id=1, source_target_pairs={{0,1},{1,0},{2,3},{3,2},{4,5},{5,4},{6,7},{7,6},{8,9},{9,8},{10,11... | collective-permute-start | bytes 147464 | tf_op jit(solution)/shard_map/ppermute | solution.py:44
  75.8 1.3 %last_slabs_2.1 = (f32[6,3,512,128]{3,2,1,0:T(8,128)S(1)}, f32[6,512,384]{2,1,0:T(8,128)}) custom-call(f32[3,3,512,128]{3,2,1,0:T(8,128)S(1)} %get-tuple-element.104.v, f32[6,3,512,128]{3,2,1,0:T(8,128)S(1)} %get-tuple-element.116.s_in, f32[3,512,128]{2,1,0:T(8,128)S(1)} %get-tuple-element.86.w.m, ...), custom_call_target="tpu_custom_call", output_to_operand_aliasing={{0}: (1, {}), {1}: (4, {})} | custom-call | flops 2000000000 | bytes 8000000 | tf_op jit(solution)/shard_map/last_slabs_2/pallas_call | solution.py:58
  77.1 1.7 %edges_last.1 = (f32[6,512,384]{2,1,0:T(8,128)}, f32[2,384]{1,0:T(2,128)}, f32[2,384]{1,0:T(2,128)}) custom-call(f32[6,3,512,128]{3,2,1,0:T(8,128)S(1)} %get-tuple-element.118.s, f32[3,512,128]{2,1,0:T(8,128)S(1)} %get-tuple-element.86.w.m, f32[4,3,16,128]{3,2,1,0:T(8,128)S(1)} %collective-permute-done.21.xl, ...), custom_call_target="tpu_custom_call", output_to_operand_aliasing={{0}: (7, {})} | custom-call | flops 1000000 | bytes 1000000 | tf_op jit(solution)/shard_map/edges_last/pallas_call | solution.py:58
  (53 shorter events, 9.1 us)
Async XLA Ops:
  1.6 4.0 %collective-permute-start = (f32[1,8,384]{2,1,0:T(8,128)S(1)}, f32[1,8,384]{2,1,0:T(8,128)S(1)}, u32[]{:S(2)}, u32[]{:S(2)}) collective-permute-start(f32[1,8,384]{2,1,0:T(8,128)S(1)} %own.1.mine), channel_id=1, source_target_pairs={{0,1},{1,0},{2,3},{3,2},{4,5},{5,4},{6,7},{7,6},{8,9},{9,8},{10,11... | collective-permute-start | bytes 36872 | tf_op jit(solution)/shard_map/ppermute | solution.py:44
  5.6 9.4 %collective-permute-start.1 = (f32[2,8,384]{2,1,0:T(8,128)S(1)}, f32[2,8,384]{2,1,0:T(8,128)S(1)}, u32[]{:S(2)}, u32[]{:S(2)}) collective-permute-start(f32[2,8,384]{2,1,0:T(8,128)S(1)} %merge.3.mine), channel_id=1, source_target_pairs={{0,2},{1,3},{2,0},{3,1},{4,6},{5,7},{6,4},{7,5},{8,10},{9,11},{10,... | collective-permute-start | bytes 73736 | tf_op jit(solution)/shard_map/ppermute | solution.py:44
  7.1 15.8 %collective-permute-start.4 = (f32[4,3,16,128]{3,2,1,0:T(8,128)S(1)}, f32[4,3,16,128]{3,2,1,0:T(8,128)S(1)}, u32[]{:S(2)}, u32[]{:S(2)}) collective-permute-start(f32[4,3,16,128]{3,2,1,0:T(8,128)S(1)} %get-tuple-element.76), channel_id=1, source_target_pairs={{16,0},{32,16},{48,32},{64,48},{80,64},{96,80},{112,96},{0,112},{1... | collective-permute-start | bytes 294920 | tf_op jit(solution)/shard_map/ppermute | solution.py:30
  13.3 9.6 %collective-permute-start.3 = (f32[5,3,16,128]{3,2,1,0:T(8,128)S(1)}, f32[5,3,16,128]{3,2,1,0:T(8,128)S(1)}, u32[]{:S(2)}, u32[]{:S(2)}) collective-permute-start(f32[5,3,16,128]{3,2,1,0:T(8,128)S(1)} %get-tuple-element.75), channel_id=1, source_target_pairs={{0,16},{16,32},{32,48},{48,64},{64,80},{80,96},{96,112},{112,0},{1... | collective-permute-start | bytes 368648 | tf_op jit(solution)/shard_map/ppermute | solution.py:25
  13.3 9.6 %collective-permute-start.6 = (f32[4,3,32,128]{3,2,1,0:T(8,128)S(1)}, f32[4,3,32,128]{3,2,1,0:T(8,128)S(1)}, u32[]{:S(2)}, u32[]{:S(2)}) collective-permute-start(f32[4,3,32,128]{3,2,1,0:T(8,128)S(1)} %get-tuple-element.78), channel_id=1, source_target_pairs={{1,0},{2,1},{3,2},{4,3},{5,4},{6,5},{7,6},{8,7},{9,8},{10,9},{11,1... | collective-permute-start | bytes 589832 | tf_op jit(solution)/shard_map/ppermute | solution.py:30
  14.1 8.8 %collective-permute-start.5 = (f32[5,3,32,128]{3,2,1,0:T(8,128)S(1)}, f32[5,3,32,128]{3,2,1,0:T(8,128)S(1)}, u32[]{:S(2)}, u32[]{:S(2)}) collective-permute-start(f32[5,3,32,128]{3,2,1,0:T(8,128)S(1)} %get-tuple-element.77), channel_id=1, source_target_pairs={{0,1},{1,2},{2,3},{3,4},{4,5},{5,6},{6,7},{7,8},{8,9},{9,10},{10,1... | collective-permute-start | bytes 737288 | tf_op jit(solution)/shard_map/ppermute | solution.py:25
  15.1 7.8 %collective-permute-start.2 = (f32[4,8,384]{2,1,0:T(8,128)S(1)}, f32[4,8,384]{2,1,0:T(8,128)S(1)}, u32[]{:S(2)}, u32[]{:S(2)}) collective-permute-start(f32[4,8,384]{2,1,0:T(8,128)S(1)} %merge.4.mine), channel_id=1, source_target_pairs={{0,4},{1,5},{2,6},{3,7},{4,0},{5,1},{6,2},{7,3},{8,12},{9,13},{10,... | collective-permute-start | bytes 147464 | tf_op jit(solution)/shard_map/ppermute | solution.py:44
  23.6 4.4 %collective-permute-start.7 = (f32[3,80,128]{2,1,0:T(8,128)S(1)}, f32[3,80,128]{2,1,0:T(8,128)S(1)}, u32[]{:S(2)}, u32[]{:S(2)}) collective-permute-start(f32[3,80,128]{2,1,0:T(8,128)S(1)} %get-tuple-element.80.refs_0_), channel_id=1, source_target_pairs={{1,2},{2,1},{3,4},{4,3},{5,6},{6,5},{7,8},{8,7},{9,10},{10,9},{11,... | collective-permute-start | bytes 368648 | tf_op jit(solution)/shard_map/ppermute | solution.py:39
  23.8 14.2 %collective-permute-start.10 = (f32[4,3,32,128]{3,2,1,0:T(8,128)S(1)}, f32[4,3,32,128]{3,2,1,0:T(8,128)S(1)}, u32[]{:S(2)}, u32[]{:S(2)}) collective-permute-start(f32[4,3,32,128]{3,2,1,0:T(8,128)S(1)} %get-tuple-element.89), channel_id=1, source_target_pairs={{0,1},{1,2},{2,3},{3,4},{4,5},{5,6},{6,7},{7,8},{8,9},{9,10},{10,1... | collective-permute-start | bytes 589832 | tf_op jit(solution)/shard_map/ppermute | solution.py:25
  25.6 12.4 %collective-permute-start.11 = (f32[5,3,32,128]{3,2,1,0:T(8,128)S(1)}, f32[5,3,32,128]{3,2,1,0:T(8,128)S(1)}, u32[]{:S(2)}, u32[]{:S(2)}) collective-permute-start(f32[5,3,32,128]{3,2,1,0:T(8,128)S(1)} %get-tuple-element.90), channel_id=1, source_target_pairs={{1,0},{2,1},{3,2},{4,3},{5,4},{6,5},{7,6},{8,7},{9,8},{10,9},{11,1... | collective-permute-start | bytes 737288 | tf_op jit(solution)/shard_map/ppermute | solution.py:30
  29.1 9.0 %collective-permute-start.8 = (f32[4,3,16,128]{3,2,1,0:T(8,128)S(1)}, f32[4,3,16,128]{3,2,1,0:T(8,128)S(1)}, u32[]{:S(2)}, u32[]{:S(2)}) collective-permute-start(f32[4,3,16,128]{3,2,1,0:T(8,128)S(1)} %get-tuple-element.87), channel_id=1, source_target_pairs={{0,16},{16,32},{32,48},{48,64},{64,80},{80,96},{96,112},{112,0},{1... | collective-permute-start | bytes 294920 | tf_op jit(solution)/shard_map/ppermute | solution.py:25
  29.9 8.1 %collective-permute-start.9 = (f32[5,3,16,128]{3,2,1,0:T(8,128)S(1)}, f32[5,3,16,128]{3,2,1,0:T(8,128)S(1)}, u32[]{:S(2)}, u32[]{:S(2)}) collective-permute-start(f32[5,3,16,128]{3,2,1,0:T(8,128)S(1)} %get-tuple-element.88), channel_id=1, source_target_pairs={{16,0},{32,16},{48,32},{64,48},{80,64},{96,80},{112,96},{0,112},{1... | collective-permute-start | bytes 368648 | tf_op jit(solution)/shard_map/ppermute | solution.py:30
  39.1 12.6 %collective-permute-start.13 = (f32[4,3,16,128]{3,2,1,0:T(8,128)S(1)}, f32[4,3,16,128]{3,2,1,0:T(8,128)S(1)}, u32[]{:S(2)}, u32[]{:S(2)}) collective-permute-start(f32[4,3,16,128]{3,2,1,0:T(8,128)S(1)} %get-tuple-element.96), channel_id=1, source_target_pairs={{16,0},{32,16},{48,32},{64,48},{80,64},{96,80},{112,96},{0,112},{1... | collective-permute-start | bytes 294920 | tf_op jit(solution)/shard_map/ppermute | solution.py:30
  43.7 8.0 %collective-permute-start.12 = (f32[5,3,16,128]{3,2,1,0:T(8,128)S(1)}, f32[5,3,16,128]{3,2,1,0:T(8,128)S(1)}, u32[]{:S(2)}, u32[]{:S(2)}) collective-permute-start(f32[5,3,16,128]{3,2,1,0:T(8,128)S(1)} %get-tuple-element.95), channel_id=1, source_target_pairs={{0,16},{16,32},{32,48},{48,64},{64,80},{80,96},{96,112},{112,0},{1... | collective-permute-start | bytes 368648 | tf_op jit(solution)/shard_map/ppermute | solution.py:25
  43.7 8.0 %collective-permute-start.15 = (f32[4,3,32,128]{3,2,1,0:T(8,128)S(1)}, f32[4,3,32,128]{3,2,1,0:T(8,128)S(1)}, u32[]{:S(2)}, u32[]{:S(2)}) collective-permute-start(f32[4,3,32,128]{3,2,1,0:T(8,128)S(1)} %get-tuple-element.98), channel_id=1, source_target_pairs={{1,0},{2,1},{3,2},{4,3},{5,4},{6,5},{7,6},{8,7},{9,8},{10,9},{11,1... | collective-permute-start | bytes 589832 | tf_op jit(solution)/shard_map/ppermute | solution.py:30
  48.4 3.3 %collective-permute-start.14 = (f32[5,3,32,128]{3,2,1,0:T(8,128)S(1)}, f32[5,3,32,128]{3,2,1,0:T(8,128)S(1)}, u32[]{:S(2)}, u32[]{:S(2)}) collective-permute-start(f32[5,3,32,128]{3,2,1,0:T(8,128)S(1)} %get-tuple-element.97), channel_id=1, source_target_pairs={{0,1},{1,2},{2,3},{3,4},{4,5},{5,6},{6,7},{7,8},{8,9},{9,10},{10,1... | collective-permute-start | bytes 737288 | tf_op jit(solution)/shard_map/ppermute | solution.py:25
  52.4 6.8 %collective-permute-start.16 = (f32[3,32,128]{2,1,0:T(8,128)S(1)}, f32[3,32,128]{2,1,0:T(8,128)S(1)}, u32[]{:S(2)}, u32[]{:S(2)}) collective-permute-start(f32[3,32,128]{2,1,0:T(8,128)S(1)} %get-tuple-element.99.refs_0_), channel_id=1, source_target_pairs={{1,2},{2,1},{3,4},{4,3},{5,6},{6,5},{7,8},{8,7},{9,10},{10,9},{11,... | collective-permute-start | bytes 147464 | tf_op jit(solution)/shard_map/ppermute | solution.py:39
  55.3 16.7 %collective-permute-start.19 = (f32[4,3,32,128]{3,2,1,0:T(8,128)S(1)}, f32[4,3,32,128]{3,2,1,0:T(8,128)S(1)}, u32[]{:S(2)}, u32[]{:S(2)}) collective-permute-start(f32[4,3,32,128]{3,2,1,0:T(8,128)S(1)} %get-tuple-element.111), channel_id=1, source_target_pairs={{0,1},{1,2},{2,3},{3,4},{4,5},{5,6},{6,7},{7,8},{8,9},{9,10},{10,1... | collective-permute-start | bytes 589832 | tf_op jit(solution)/shard_map/ppermute | solution.py:25
  55.6 16.4 %collective-permute-start.20 = (f32[5,3,32,128]{3,2,1,0:T(8,128)S(1)}, f32[5,3,32,128]{3,2,1,0:T(8,128)S(1)}, u32[]{:S(2)}, u32[]{:S(2)}) collective-permute-start(f32[5,3,32,128]{3,2,1,0:T(8,128)S(1)} %get-tuple-element.112), channel_id=1, source_target_pairs={{1,0},{2,1},{3,2},{4,3},{5,4},{6,5},{7,6},{8,7},{9,8},{10,9},{11,1... | collective-permute-start | bytes 737288 | tf_op jit(solution)/shard_map/ppermute | solution.py:30
  60.3 7.0 %collective-permute-start.17 = (f32[2,3,16,128]{3,2,1,0:T(8,128)S(1)}, f32[2,3,16,128]{3,2,1,0:T(8,128)S(1)}, u32[]{:S(2)}, u32[]{:S(2)}) collective-permute-start(f32[2,3,16,128]{3,2,1,0:T(8,128)S(1)} %get-tuple-element.107.mine), channel_id=1, source_target_pairs={{0,4},{1,5},{2,6},{3,7},{4,0},{5,1},{6,2},{7,3},{8,12},{9,13},{10,... | collective-permute-start | bytes 147464 | tf_op jit(solution)/shard_map/ppermute | solution.py:44
  60.7 16.4 %collective-permute-start.21 = (f32[4,3,16,128]{3,2,1,0:T(8,128)S(1)}, f32[4,3,16,128]{3,2,1,0:T(8,128)S(1)}, u32[]{:S(2)}, u32[]{:S(2)}) collective-permute-start(f32[4,3,16,128]{3,2,1,0:T(8,128)S(1)} %get-tuple-element.119), channel_id=1, source_target_pairs={{0,16},{16,32},{32,48},{48,64},{64,80},{80,96},{96,112},{112,0},{1... | collective-permute-start | bytes 294920 | tf_op jit(solution)/shard_map/ppermute | solution.py:25
  60.7 16.4 %collective-permute-start.22 = (f32[5,3,16,128]{3,2,1,0:T(8,128)S(1)}, f32[5,3,16,128]{3,2,1,0:T(8,128)S(1)}, u32[]{:S(2)}, u32[]{:S(2)}) collective-permute-start(f32[5,3,16,128]{3,2,1,0:T(8,128)S(1)} %get-tuple-element.120), channel_id=1, source_target_pairs={{16,0},{32,16},{48,32},{64,48},{80,64},{96,80},{112,96},{0,112},{1... | collective-permute-start | bytes 368648 | tf_op jit(solution)/shard_map/ppermute | solution.py:30
  67.3 6.7 %collective-permute-start.18 = (f32[2,3,16,128]{3,2,1,0:T(8,128)S(1)}, f32[2,3,16,128]{3,2,1,0:T(8,128)S(1)}, u32[]{:S(2)}, u32[]{:S(2)}) collective-permute-start(f32[2,3,16,128]{3,2,1,0:T(8,128)S(1)} %choose.2.mine), channel_id=1, source_target_pairs={{0,2},{1,3},{2,0},{3,1},{4,6},{5,7},{6,4},{7,5},{8,10},{9,11},{10,... | collective-permute-start | bytes 147464 | tf_op jit(solution)/shard_map/ppermute | solution.py:44
  74.1 3.0 %collective-permute-start.23 = (f32[2,3,16,128]{3,2,1,0:T(8,128)S(1)}, f32[2,3,16,128]{3,2,1,0:T(8,128)S(1)}, u32[]{:S(2)}, u32[]{:S(2)}) collective-permute-start(f32[2,3,16,128]{3,2,1,0:T(8,128)S(1)} %choose.3.mine), channel_id=1, source_target_pairs={{0,1},{1,0},{2,3},{3,2},{4,5},{5,4},{6,7},{7,6},{8,9},{9,8},{10,11... | collective-permute-start | bytes 147464 | tf_op jit(solution)/shard_map/ppermute | solution.py:44
  (4 other events, 56.5 us)
